TPU v7x, 32 devices: a whole 2x2x4 slice. The times are simulated.
32 devices in a mesh: omega: 8 (over y, x, core), row: 4 (over z).
Axes of the slice: x: 2, y: 2, z: 4, core: 2. Of those that a mesh axis runs over, the one named last changes fastest.
Arguments:
- frames: float32 [128, 256, 1024], P('omega', 'row'), may hold values from -6 to 6
- thresholds: int32 [256], P('row'), may hold values from 0 to 31
- spot_boxes: int32 [3, 1024], P(None, ('omega', 'row')), may hold values from -1 to 1023, as said below
Outputs:
- peak_weight: float32 [128, 256, 1024], P('omega', 'row')
- moments: float32 [4, 1024], P(None, ('omega', 'row'))
Inputs may be any that keep to these rules, and one draw needn't show every extreme that they name: `spot_boxes`: slot block d of 32 slots (d = omega index * the number of row indices + row index) lists boxes that lie wholly inside the frames and rows of that device; its live boxes fill the leading slots, each block has 1 to 32 of them, and one block has 32; empty slots hold -1 in all three entries.
All inputs are finite; a program needn't handle non-finite values.
Results may differ from a plain program's by a relative error of at most 0.0003.
Values sent between devices are 32-bit elements; how exact they have to be, the bound alone decides.
No kernel may reach another device: no remote copies, remote signals or barrier semaphores. Data moves between devices by JAX's collectives and lax.ppermute only.
A program may use at most 64 MiB of HBM per device.

v0:
```python
import jax
import jax.numpy as jnp
from jax import lax
from jax.sharding import PartitionSpec as P

BW = 4
BOX_F = 8
BOX_R = 16
BOX_C = 16


SHARP = 8.0


def extended_2(x, sides, width, wrap):
    for axis, dim in sides:
        peers, length = (lax.axis_size(axis), x.shape[dim])
        up = [(i, (i + 1) % peers) for i in range(peers if wrap else peers - 1)]
        down = [(j, i) for i, j in up]
        last = lax.slice_in_dim(x, length - width, length, axis=dim)
        leading = lax.slice_in_dim(x, 0, width, axis=dim)
        before = lax.ppermute(last, axis, up)
        after = lax.ppermute(leading, axis, down)
        x = jnp.concatenate([before, x, after], axis=dim)
    return x


def selectors(start, length, extent, live):
    places = jnp.arange(extent)
    distance = places[None, :] - start[:, None]
    inside = (distance >= 0) & (distance < length) & live[:, None]
    middle = (length - 1) / 2.0
    offset = (distance.astype(jnp.float32) - middle) / middle
    member = jnp.where(inside, 1.0, 0.0).astype(jnp.float32)
    return (member, member * offset)


def frame_filter(padded):
    return (padded[:-2] + 2.0 * padded[1:-1] + padded[2:]) * 0.25


def row_filter(padded):
    return (padded[:, :-2] + 2.0 * padded[:, 1:-1] + padded[:, 2:]) * 0.25


def column_filter(values):
    padded = jnp.pad(values, ((0, 0), (0, 0), (1, 1)))
    return (padded[:, :, :-2] + 2.0 * padded[:, :, 1:-1] + padded[:, :, 2:]) * 0.25


def frame_maxima(padded):
    return jnp.maximum(jnp.maximum(padded[:-2], padded[1:-1]), padded[2:])


def row_maxima(padded):
    position = lax.axis_index("row")
    final = lax.axis_size("row") - 1
    upper = jnp.where(position == 0, padded[:, 1:2], padded[:, 0:1])
    lower = jnp.where(position == final, padded[:, -2:-1], padded[:, -1:])
    fixed = jnp.concatenate([upper, padded[:, 1:-1], lower], axis=1)
    return jnp.maximum(jnp.maximum(fixed[:, :-2], fixed[:, 1:-1]), fixed[:, 2:])


def column_maxima(values):
    padded = jnp.pad(values, ((0, 0), (0, 0), (1, 1)), mode="edge")
    return jnp.maximum(jnp.maximum(padded[:, :, :-2], padded[:, :, 1:-1]), padded[:, :, 2:])


def on_device(frames, thresholds, spot_boxes):
    frame_count = frames.shape[0]
    row_count = frames.shape[1]
    column_count = frames.shape[2]
    span = 2 * BW + 1
    extended = extended_2(frames, (("omega", 0),), BW, True)
    total = extended[0:frame_count]
    for offset in range(1, span):
        total = total + extended[offset : offset + frame_count]
    corrected = frames - total / span
    padded = extended_2(corrected, (("omega", 0),), 1, True)
    smooth = frame_filter(padded)
    padded = extended_2(smooth, (("row", 1),), 1, False)
    smooth = column_filter(row_filter(padded))
    padded = extended_2(smooth, (("omega", 0),), 1, True)
    highest = frame_maxima(padded)
    padded = extended_2(highest, (("row", 1),), 1, False)
    highest = column_maxima(row_maxima(padded))
    level = thresholds.astype(jnp.float32) / 64.0
    weight = jnp.exp(SHARP * (smooth - highest)) * jnp.maximum(smooth - level[None, :, None], 0.0)
    frame_base = lax.axis_index("omega") * frame_count
    row_base = lax.axis_index("row") * row_count
    live = spot_boxes[0] >= 0
    slots = spot_boxes.shape[1]
    frame_pick, frame_moment = selectors(spot_boxes[0] - frame_base, BOX_F, frame_count, live)
    row_pick, row_moment = selectors(spot_boxes[1] - row_base, BOX_R, row_count, live)
    column_pick, column_moment = selectors(spot_boxes[2], BOX_C, column_count, live)
    stacked = jnp.concatenate([column_pick, column_moment], axis=0)
    folded = jnp.einsum("frc,kc->kfr", weight, stacked, precision=lax.Precision.HIGHEST)
    plain = folded[:slots]
    by_column = folded[slots:]
    plain_rows = jnp.sum(plain * row_pick[:, None, :], axis=2)
    moment_rows = jnp.sum(plain * row_moment[:, None, :], axis=2)
    column_rows = jnp.sum(by_column * row_pick[:, None, :], axis=2)
    stats = jnp.stack(
        [
            jnp.sum(plain_rows * frame_pick, axis=1),
            jnp.sum(plain_rows * frame_moment, axis=1),
            jnp.sum(moment_rows * frame_pick, axis=1),
            jnp.sum(column_rows * frame_pick, axis=1),
        ]
    )
    return (weight, stats / float(BOX_F * BOX_R * BOX_C))


def solution(mesh):
    return jax.shard_map(
        on_device,
        mesh=mesh,
        in_specs=(P("omega", "row", None), P("row"), P(None, ("omega", "row"))),
        out_specs=(P("omega", "row", None), P(None, ("omega", "row"))),
        check_vma=False,
    )
```

profile of v0, /device:TPU:0, one launch (start us, length us, event | category | flops | bytes accessed | tf_op | source)
XLA Modules:
  0.0 114.5 jit_solution(9032921533755204258)
XLA Ops:
  0.6 0.0 copy-start.5
  0.6 1.8 %fusion.49 = (f32[4,64,1024]{2,1,0:T(8,128)S(1)}, f32[4,64,1024]{2,1,0:T(8,128)S(1)}) fusion(f32[16,64,1024]{2,1,0:T(8,128)} %param.3), kind=kLoop, calls=%fused_computation.95 | loop fusion | bytes 4194304 | tf_op jit(solution)/shard_map/slice | solution.py:20
  2.5 0.5 collective-permute-start
  3.0 2.9 %collective-permute-start.1 = (f32[4,64,1024]{2,1,0:T(8,128)S(1)}, f32[4,64,1024]{2,1,0:T(8,128)S(1)}, u32[]{:S(2)}, u32[]{:S(2)}) collective-permute-start(f32[4,64,1024]{2,1,0:T(8,128)S(1)} %get-tuple-element.24), channel_id=1, source_target_pairs={{4,0},{8,4},{12,8},{16,12},{20,16},{24,20},{28,24},{0,28},{5,1},{9... | collective-permute-start | bytes 3145736 | tf_op jit(solution)/shard_map/ppermute | solution.py:23
  6.0 21.1 %collective-permute-done = f32[4,64,1024]{2,1,0:T(8,128)S(1)} collective-permute-done((f32[4,64,1024]{2,1,0:T(8,128)S(1)}, f32[4,64,1024]{2,1,0:T(8,128)S(1)}, u32[]{:S(2)}, u32[]{:S(2)}) %collective-permute-start) | collective-permute-done | bytes 1048608 | tf_op jit(solution)/shard_map/ppermute | solution.py:22
  27.0 0.1 constant_dynamic-update-slice_fusion.1
  27.1 0.0 copy-done.5
  27.1 0.9 constant_dynamic-update-slice_fusion
  28.0 0.0 copy-start.2
  28.0 0.5 collective-permute-done.1
  28.5 0.1 constant_dynamic-update-slice_fusion.2
  28.5 1.7 %copy-done.2 = f32[20,64,1024]{2,1,0:T(8,128)} copy-done((f32[20,64,1024]{2,1,0:T(8,128)}, f32[20,64,1024]{2,1,0:T(8,128)S(1)}, u32[]{:S(2)}) %copy-start.2) | copy-done | bytes 5242904
  30.3 0.0 copy-start.8
  30.3 8.7 %fusion.18 = f32[16,64,1024]{2,1,0:T(8,128)S(1)} fusion(f32[16,64,1024]{2,1,0:T(8,128)S(1)} %copy-done.5, f32[20,64,1024]{2,1,0:T(8,128)S(1)} %constant_dynamic-update-slice_fusion.2, f32[20,64,1024]{2,1,0:T(8,128)} %copy-done.2), kind=kLoop, calls=%fused_computation.31 | loop fusion | flops 10485760 | bytes 41943040 | tf_op jit(solution)/shard_map/sub | solution.py:78
  39.0 0.0 copy-start
  39.0 2.0 %copy-done = f32[16,64,1024]{2,1,0:T(8,128)} copy-done((f32[16,64,1024]{2,1,0:T(8,128)}, f32[16,64,1024]{2,1,0:T(8,128)S(1)}, u32[]{:S(2)}) %copy-start) | copy-done | bytes 4194328
  41.0 0.6 collective-permute-start.2
  41.6 2.1 %collective-permute-start.3 = (f32[1,64,1024]{2,1,0:T(8,128)S(1)}, f32[1,64,1024]{2,1,0:T(8,128)S(1)}, u32[]{:S(2)}, u32[]{:S(2)}) collective-permute-start(f32[1,64,1024]{2,1,0:T(8,128)S(1)} %get-tuple-element.20), channel_id=1, source_target_pairs={{4,0},{8,4},{12,8},{16,12},{20,16},{24,20},{28,24},{0,28},{5,1},{9... | collective-permute-start | bytes 786440 | tf_op jit(solution)/shard_map/ppermute | solution.py:23
  43.7 0.0 copy-done.8
  43.7 0.0 copy-start.1
  43.8 4.3 %collective-permute-done.2 = f32[1,64,1024]{2,1,0:T(8,128)S(1)} collective-permute-done((f32[1,64,1024]{2,1,0:T(8,128)S(1)}, f32[1,64,1024]{2,1,0:T(8,128)S(1)}, u32[]{:S(2)}, u32[]{:S(2)}) %collective-permute-start.2) | collective-permute-done | bytes 262176 | tf_op jit(solution)/shard_map/ppermute | solution.py:22
  48.0 2.1 %collective-permute-done.3 = f32[1,64,1024]{2,1,0:T(8,128)S(1)} collective-permute-done((f32[1,64,1024]{2,1,0:T(8,128)S(1)}, f32[1,64,1024]{2,1,0:T(8,128)S(1)}, u32[]{:S(2)}, u32[]{:S(2)}) %collective-permute-start.3) | collective-permute-done | bytes 262176 | tf_op jit(solution)/shard_map/ppermute | solution.py:23
  50.1 5.6 %broadcast_multiply_fusion.1 = f32[16,64,1024]{2,1,0:T(8,128)S(1)} fusion(f32[1,64,1024]{2,1,0:T(8,128)S(1)} %collective-permute-done.3, f32[16,64,1024]{2,1,0:T(8,128)} %copy-done, f32[1,64,1024]{2,1,0:T(8,128)S(1)} %collective-permute-done.2), kind=kLoop, calls=%fused_computation.40 | loop fusion | flops 6291456 | bytes 8912896 | tf_op jit(solution)/shard_map/mul | solution.py:39
  55.8 0.1 fusion.47
  55.9 4.4 %collective-permute-start.4 = (f32[16,1,1024]{2,1,0:T(1,128)S(1)}, f32[16,1,1024]{2,1,0:T(1,128)S(1)}, u32[]{:S(2)}, u32[]{:S(2)}) collective-permute-start(f32[16,1,1024]{2,1,0:T(1,128)S(1)} %get-tuple-element.17), channel_id=1, source_target_pairs={{0,1},{1,2},{2,3},{4,5},{5,6},{6,7},{8,9},{9,10},{10,11},{12,13},{... | collective-permute-start | bytes 196616 | tf_op jit(solution)/shard_map/ppermute | solution.py:22
  60.3 1.3 %collective-permute-start.5 = (f32[16,1,1024]{2,1,0:T(1,128)S(1)}, f32[16,1,1024]{2,1,0:T(1,128)S(1)}, u32[]{:S(2)}, u32[]{:S(2)}) collective-permute-start(f32[16,1,1024]{2,1,0:T(1,128)S(1)} %get-tuple-element.18), channel_id=1, source_target_pairs={{1,0},{2,1},{3,2},{5,4},{6,5},{7,6},{9,8},{10,9},{11,10},{13,12},{... | collective-permute-start | bytes 196616 | tf_op jit(solution)/shard_map/ppermute | solution.py:23
  61.6 0.6 collective-permute-done.4
  62.2 4.3 %collective-permute-done.5 = f32[16,1,1024]{2,1,0:T(1,128)S(1)} collective-permute-done((f32[16,1,1024]{2,1,0:T(1,128)S(1)}, f32[16,1,1024]{2,1,0:T(1,128)S(1)}, u32[]{:S(2)}, u32[]{:S(2)}) %collective-permute-start.5) | collective-permute-done | bytes 65568 | tf_op jit(solution)/shard_map/ppermute | solution.py:23
  66.5 0.0 copy-done.1
  66.5 3.1 %broadcast_multiply_fusion = f32[16,64,1024]{2,1,0:T(8,128)S(1)} fusion(f32[16,1,1024]{2,1,0:T(1,128)S(1)} %collective-permute-done.5, f32[16,64,1024]{2,1,0:T(8,128)S(1)} %broadcast_multiply_fusion.1, f32[1,64,1024]{2,1,0:T(8,128)S(1)} %collective-permute-done.3, f32[16,64,1024]{2,1,0:T(8,128)S(1)} %copy-done.1, ...), kind=kLoop, calls=%fused_computation.39 | loop fusion | flops 11534336 | bytes 13238272 | tf_op jit(solution)/shard_map/mul | solution.py:43
  69.6 4.6 %fusion.2 = f32[16,64,1024]{2,1,0:T(8,128)S(1)} fusion(f32[16,64,1024]{2,1,0:T(8,128)S(1)} %broadcast_multiply_fusion, f32[16,1,1024]{2,1,0:T(1,128)S(1)} %collective-permute-done.5, f32[16,64,1024]{2,1,0:T(8,128)S(1)} %broadcast_multiply_fusion.1, f32[1,64,1024]{2,1,0:T(8,128)S(1)} %collective-permute-done.3, f32[16,64,1024]{2,1,0:T(8,128)S(1)} %copy-done.1, ...), kind=kLoop, calls=%fused_computation.4 | loop fusion | flops 14680064 | bytes 17432576 | tf_op jit(solution)/shard_map/mul | solution.py:48
  74.2 0.0 copy-start.3
  74.3 0.1 collective-permute-start.6
  74.4 2.6 %collective-permute-start.7 = (f32[1,64,1024]{2,1,0:T(8,128)S(1)}, f32[1,64,1024]{2,1,0:T(8,128)S(1)}, u32[]{:S(2)}, u32[]{:S(2)}) collective-permute-start(f32[1,64,1024]{2,1,0:T(8,128)S(1)} %get-tuple-element.16), channel_id=1, source_target_pairs={{4,0},{8,4},{12,8},{16,12},{20,16},{24,20},{28,24},{0,28},{5,1},{9... | collective-permute-start | bytes 786440 | tf_op jit(solution)/shard_map/ppermute | solution.py:23
  77.0 0.1 multiply_multiply_fusion.1
  77.1 0.1 fusion.28
  77.2 0.0 copy-start.9
  77.2 6.2 %collective-permute-done.6 = f32[1,64,1024]{2,1,0:T(8,128)S(1)} collective-permute-done((f32[1,64,1024]{2,1,0:T(8,128)S(1)}, f32[1,64,1024]{2,1,0:T(8,128)S(1)}, u32[]{:S(2)}, u32[]{:S(2)}) %collective-permute-start.6) | collective-permute-done | bytes 262176 | tf_op jit(solution)/shard_map/ppermute | solution.py:22
  83.4 0.0 collective-permute-done.7
  83.4 0.9 fusion.11
  84.4 0.0 copy-done.3
  84.4 0.0 copy-start.6
  84.4 0.1 fusion.45
  84.5 1.8 %copy-done.6 = f32[16,64,1024]{2,1,0:T(8,128)} copy-done((f32[16,64,1024]{2,1,0:T(8,128)}, f32[16,64,1024]{2,1,0:T(8,128)S(1)}, u32[]{:S(2)}) %copy-start.6) | copy-done | bytes 4194328
  86.3 3.5 %collective-permute-start.8 = (f32[16,1,1024]{2,1,0:T(1,128)S(1)}, f32[16,1,1024]{2,1,0:T(1,128)S(1)}, u32[]{:S(2)}, u32[]{:S(2)}) collective-permute-start(f32[16,1,1024]{2,1,0:T(1,128)S(1)} %get-tuple-element.13), channel_id=1, source_target_pairs={{0,1},{1,2},{2,3},{4,5},{5,6},{6,7},{8,9},{9,10},{10,11},{12,13},{... | collective-permute-start | bytes 196616 | tf_op jit(solution)/shard_map/ppermute | solution.py:22
  89.8 1.5 %collective-permute-start.9 = (f32[16,1,1024]{2,1,0:T(1,128)S(1)}, f32[16,1,1024]{2,1,0:T(1,128)S(1)}, u32[]{:S(2)}, u32[]{:S(2)}) collective-permute-start(f32[16,1,1024]{2,1,0:T(1,128)S(1)} %get-tuple-element.14), channel_id=1, source_target_pairs={{1,0},{2,1},{3,2},{5,4},{6,5},{7,6},{9,8},{10,9},{11,10},{13,12},{... | collective-permute-start | bytes 196616 | tf_op jit(solution)/shard_map/ppermute | solution.py:23
  91.3 0.0 copy-done.9
  91.3 0.4 collective-permute-done.8
  91.7 4.3 %collective-permute-done.9 = f32[16,1,1024]{2,1,0:T(1,128)S(1)} collective-permute-done((f32[16,1,1024]{2,1,0:T(1,128)S(1)}, f32[16,1,1024]{2,1,0:T(1,128)S(1)}, u32[]{:S(2)}, u32[]{:S(2)}) %collective-permute-start.9) | collective-permute-done | bytes 65568 | tf_op jit(solution)/shard_map/ppermute | solution.py:23
  96.0 1.3 %broadcast_select_fusion.1 = (f32[16,1,1024]{2,1,0:T(1,128)S(1)}, f32[16,1,1024]{2,1,0:T(1,128)S(1)}) fusion(f32[16,1,1024]{2,1,0:T(1,128)S(1)} %collective-permute-done.8, pred[]{:T(512)S(6)} %eq.6, f32[16,64,1024]{2,1,0:T(8,128)} %copy-done.6, f32[16,1,1024]{2,1,0:T(1,128)S(1)} %collective-permute-done.9, pred[]{:T(512)S(6)} %eq.7), kind=kLoop, calls=%fused_computation.57 | loop fusion | flops 32768 | bytes 393218 | tf_op jit(solution)/shard_map/jit(_where)/select_n | solution.py:58
  97.3 0.0 copy-start.4
  97.3 6.5 %fusion.9 = f32[16,64,1024]{2,1,0:T(8,128)S(1)} fusion(f32[16,1,1024]{2,1,0:T(1,128)S(1)} %get-tuple-element.12, f32[16,64,1024]{2,1,0:T(8,128)} %copy-done.6, f32[16,1,1024]{2,1,0:T(1,128)S(1)} %get-tuple-element.11), kind=kLoop, calls=%fused_computation.14 | loop fusion | flops 4194304 | bytes 8519680 | tf_op jit(solution)/shard_map/max | solution.py:61
  103.8 0.2 fusion.44
  104.0 0.0 copy-done.4
  104.0 3.4 %fusion.7 = f32[16,64,1024]{2,1,0:T(8,128)S(1)} fusion(f32[16,64,1024]{2,1,0:T(8,128)S(1)} %copy-done.4, f32[16,64,1]{2,1,0:T(8,128)S(1)} %get-tuple-element.10, f32[16,64,1024]{2,1,0:T(8,128)S(1)} %fusion.9, f32[16,64,1]{2,1,0:T(8,128)S(1)} %get-tuple-element.9, f32[64]{0:T(128)S(1)} %convert_multiply_fusion), kind=kLoop, calls=%fused_computation.10 | loop fusion | flops 9437184 | bytes 12591360 | tf_op jit(solution)/shard_map/mul | solution.py:88
  107.4 0.0 copy-start.7
  107.4 6.2 %fusion.21 = f32[64,16,64]{2,0,1:T(8,128)S(1)} fusion(f32[16,64,1024]{2,1,0:T(8,128)S(1)} %fusion.7, f32[32,1024]{1,0:T(8,128)S(1)} %get-tuple-element.31, f32[32,1024]{1,0:T(8,128)S(1)} %get-tuple-element.30), kind=kOutput, calls=%fused_computation.44 | convolution fusion | flops 805371904 | bytes 4718592 | tf_op jit(solution)/shard_map/frc,kc->kfr/dot_general | solution.py:97
  113.6 0.3 multiply_reduce_fusion.1
  113.9 0.6 maximum_multiply_fusion
  114.5 0.0 copy-done.7
  (6 shorter events, 0.1 us)
Async XLA Ops:
  0.6 26.5 %copy-start.5 = (f32[16,64,1024]{2,1,0:T(8,128)S(1)}, f32[16,64,1024]{2,1,0:T(8,128)}, u32[]{:S(2)}) copy-start(f32[16,64,1024]{2,1,0:T(8,128)} %param.3) | copy-start | bytes 12582916
  2.5 24.5 %collective-permute-start = (f32[4,64,1024]{2,1,0:T(8,128)S(1)}, f32[4,64,1024]{2,1,0:T(8,128)S(1)}, u32[]{:S(2)}, u32[]{:S(2)}) collective-permute-start(f32[4,64,1024]{2,1,0:T(8,128)S(1)} %get-tuple-element.23), channel_id=1, source_target_pairs={{0,4},{4,8},{8,12},{12,16},{16,20},{20,24},{24,28},{28,0},{1,5},{5... | collective-permute-start | bytes 3145736 | tf_op jit(solution)/shard_map/ppermute | solution.py:22
  3.0 25.5 %collective-permute-start.1 = (f32[4,64,1024]{2,1,0:T(8,128)S(1)}, f32[4,64,1024]{2,1,0:T(8,128)S(1)}, u32[]{:S(2)}, u32[]{:S(2)}) collective-permute-start(f32[4,64,1024]{2,1,0:T(8,128)S(1)} %get-tuple-element.24), channel_id=1, source_target_pairs={{4,0},{8,4},{12,8},{16,12},{20,16},{24,20},{28,24},{0,28},{5,1},{9... | collective-permute-start | bytes 3145736 | tf_op jit(solution)/shard_map/ppermute | solution.py:23
  28.0 2.3 %copy-start.2 = (f32[20,64,1024]{2,1,0:T(8,128)}, f32[20,64,1024]{2,1,0:T(8,128)S(1)}, u32[]{:S(2)}) copy-start(f32[20,64,1024]{2,1,0:T(8,128)S(1)} %get-tuple-element.21) | copy-start | bytes 15728644
  30.3 13.5 %copy-start.8 = (s32[3,32]{1,0:T(4,128)S(1)}, s32[3,32]{1,0:T(4,128)}, u32[]{:S(2)}) copy-start(s32[3,32]{1,0:T(4,128)} %param.5) | copy-start | bytes 1156
  39.0 2.0 %copy-start = (f32[16,64,1024]{2,1,0:T(8,128)}, f32[16,64,1024]{2,1,0:T(8,128)S(1)}, u32[]{:S(2)}) copy-start(f32[16,64,1024]{2,1,0:T(8,128)S(1)} %fusion.18) | copy-start | bytes 12582916
  41.0 7.0 %collective-permute-start.2 = (f32[1,64,1024]{2,1,0:T(8,128)S(1)}, f32[1,64,1024]{2,1,0:T(8,128)S(1)}, u32[]{:S(2)}, u32[]{:S(2)}) collective-permute-start(f32[1,64,1024]{2,1,0:T(8,128)S(1)} %get-tuple-element.19), channel_id=1, source_target_pairs={{0,4},{4,8},{8,12},{12,16},{16,20},{20,24},{24,28},{28,0},{1,5},{5... | collective-permute-start | bytes 786440 | tf_op jit(solution)/shard_map/ppermute | solution.py:22
  41.6 8.5 %collective-permute-start.3 = (f32[1,64,1024]{2,1,0:T(8,128)S(1)}, f32[1,64,1024]{2,1,0:T(8,128)S(1)}, u32[]{:S(2)}, u32[]{:S(2)}) collective-permute-start(f32[1,64,1024]{2,1,0:T(8,128)S(1)} %get-tuple-element.20), channel_id=1, source_target_pairs={{4,0},{8,4},{12,8},{16,12},{20,16},{24,20},{28,24},{0,28},{5,1},{9... | collective-permute-start | bytes 786440 | tf_op jit(solution)/shard_map/ppermute | solution.py:23
  43.7 22.7 %copy-start.1 = (f32[16,64,1024]{2,1,0:T(8,128)S(1)}, f32[16,64,1024]{2,1,0:T(8,128)}, u32[]{:S(2)}) copy-start(f32[16,64,1024]{2,1,0:T(8,128)} %copy-done) | copy-start | bytes 12582916
  55.9 6.3 %collective-permute-start.4 = (f32[16,1,1024]{2,1,0:T(1,128)S(1)}, f32[16,1,1024]{2,1,0:T(1,128)S(1)}, u32[]{:S(2)}, u32[]{:S(2)}) collective-permute-start(f32[16,1,1024]{2,1,0:T(1,128)S(1)} %get-tuple-element.17), channel_id=1, source_target_pairs={{0,1},{1,2},{2,3},{4,5},{5,6},{6,7},{8,9},{9,10},{10,11},{12,13},{... | collective-permute-start | bytes 196616 | tf_op jit(solution)/shard_map/ppermute | solution.py:22
  60.3 6.2 %collective-permute-start.5 = (f32[16,1,1024]{2,1,0:T(1,128)S(1)}, f32[16,1,1024]{2,1,0:T(1,128)S(1)}, u32[]{:S(2)}, u32[]{:S(2)}) collective-permute-start(f32[16,1,1024]{2,1,0:T(1,128)S(1)} %get-tuple-element.18), channel_id=1, source_target_pairs={{1,0},{2,1},{3,2},{5,4},{6,5},{7,6},{9,8},{10,9},{11,10},{13,12},{... | collective-permute-start | bytes 196616 | tf_op jit(solution)/shard_map/ppermute | solution.py:23
  74.2 10.1 %copy-start.3 = (f32[16,64,1024]{2,1,0:T(8,128)}, f32[16,64,1024]{2,1,0:T(8,128)S(1)}, u32[]{:S(2)}) copy-start(f32[16,64,1024]{2,1,0:T(8,128)S(1)} %fusion.2) | copy-start | bytes 12582916
  74.3 9.1 %collective-permute-start.6 = (f32[1,64,1024]{2,1,0:T(8,128)S(1)}, f32[1,64,1024]{2,1,0:T(8,128)S(1)}, u32[]{:S(2)}, u32[]{:S(2)}) collective-permute-start(f32[1,64,1024]{2,1,0:T(8,128)S(1)} %get-tuple-element.15), channel_id=1, source_target_pairs={{0,4},{4,8},{8,12},{12,16},{16,20},{20,24},{24,28},{28,0},{1,5},{5... | collective-permute-start | bytes 786440 | tf_op jit(solution)/shard_map/ppermute | solution.py:22
  74.4 9.1 %collective-permute-start.7 = (f32[1,64,1024]{2,1,0:T(8,128)S(1)}, f32[1,64,1024]{2,1,0:T(8,128)S(1)}, u32[]{:S(2)}, u32[]{:S(2)}) collective-permute-start(f32[1,64,1024]{2,1,0:T(8,128)S(1)} %get-tuple-element.16), channel_id=1, source_target_pairs={{4,0},{8,4},{12,8},{16,12},{20,16},{24,20},{28,24},{0,28},{5,1},{9... | collective-permute-start | bytes 786440 | tf_op jit(solution)/shard_map/ppermute | solution.py:23
  77.2 14.1 %copy-start.9 = (s32[64]{0:T(128)S(1)}, s32[64]{0:T(128)}, u32[]{:S(2)}) copy-start(s32[64]{0:T(128)} %param.4) | copy-start | bytes 772
  84.4 2.0 %copy-start.6 = (f32[16,64,1024]{2,1,0:T(8,128)}, f32[16,64,1024]{2,1,0:T(8,128)S(1)}, u32[]{:S(2)}) copy-start(f32[16,64,1024]{2,1,0:T(8,128)S(1)} %fusion.11) | copy-start | bytes 12582916
  86.3 5.4 %collective-permute-start.8 = (f32[16,1,1024]{2,1,0:T(1,128)S(1)}, f32[16,1,1024]{2,1,0:T(1,128)S(1)}, u32[]{:S(2)}, u32[]{:S(2)}) collective-permute-start(f32[16,1,1024]{2,1,0:T(1,128)S(1)} %get-tuple-element.13), channel_id=1, source_target_pairs={{0,1},{1,2},{2,3},{4,5},{5,6},{6,7},{8,9},{9,10},{10,11},{12,13},{... | collective-permute-start | bytes 196616 | tf_op jit(solution)/shard_map/ppermute | solution.py:22
  89.8 6.2 %collective-permute-start.9 = (f32[16,1,1024]{2,1,0:T(1,128)S(1)}, f32[16,1,1024]{2,1,0:T(1,128)S(1)}, u32[]{:S(2)}, u32[]{:S(2)}) collective-permute-start(f32[16,1,1024]{2,1,0:T(1,128)S(1)} %get-tuple-element.14), channel_id=1, source_target_pairs={{1,0},{2,1},{3,2},{5,4},{6,5},{7,6},{9,8},{10,9},{11,10},{13,12},{... | collective-permute-start | bytes 196616 | tf_op jit(solution)/shard_map/ppermute | solution.py:23
  97.3 6.7 %copy-start.4 = (f32[16,64,1024]{2,1,0:T(8,128)S(1)}, f32[16,64,1024]{2,1,0:T(8,128)}, u32[]{:S(2)}) copy-start(f32[16,64,1024]{2,1,0:T(8,128)} %copy-done.3) | copy-start | bytes 12582916
  107.4 7.1 %copy-start.7 = (f32[16,64,1024]{2,1,0:T(8,128)}, f32[16,64,1024]{2,1,0:T(8,128)S(1)}, u32[]{:S(2)}) copy-start(f32[16,64,1024]{2,1,0:T(8,128)S(1)} %fusion.7) | copy-start | bytes 12582916
where the time goes:
time: 115 us; the launch traced here: 114 us
  waiting for transfers between devices  43.6 us (38%)
  other arithmetic  35.3 us (31%)
  starting transfers between devices  19.5 us (17%)
  local copies, waits for them, and re-layouts  8.96 us (8%)
  matrix products  6.18 us (5%)
    ppermute x5, waiting for transfers between devices, extended_2(): before = lax.ppermute(last, axis, up)  32.5 us
    ppermute x5, waiting for transfers between devices, extended_2(): after = lax.ppermute(leading, axis, down)  11.1 us
    ppermute x5, starting transfers between devices, extended_2(): after = lax.ppermute(leading, axis, down)  10.4 us
    ppermute x5, starting transfers between devices, extended_2(): before = lax.ppermute(last, axis, up)  9.08 us
    sub x1, other arithmetic, on_device(): corrected = frames - total / span  8.68 us
    max x1, other arithmetic, row_maxima(): return jnp.maximum(jnp.maximum(fixed[:, :-2], fixed[:, 1:-1]), fixed[:, 2:])  6.46 us
    dot_general x1, matrix products, on_device(): jnp.einsum('frc,kc->kfr', weight, stacked, precision=lax.Precision.HIGHEST)  6.18 us
    unnamed x21, local copies, waits for them, and re-layouts  5.73 us
  transfers between devices with their start and end apart: 10, of which 9 were waited for; matrix products, arithmetic and copies ran while one was open for 1% of the time, Pallas kernels for 0%

commit v1 on v0

v1 whole, which is shorter than its diff:
```python
import functools

import jax
import jax.numpy as jnp
from jax import lax
from jax.experimental import pallas as pl
from jax.experimental.pallas import tpu as pltpu
from jax.sharding import PartitionSpec as P

BW = 4
BOX_F = 8
BOX_R = 16
BOX_C = 16
SHARP = 8.0

SUB = 8
LANES = 128
REACH = BW + 2
SPAN = 2 * BW + 1
NEG = -1e30
SCALE = 1.0 / (SPAN * 64.0)


def next_row(tiles, sub):
    rolled = [pltpu.roll(v, SUB - 1, 0) for v in tiles]
    n = len(tiles)
    return [jnp.where(sub == SUB - 1, rolled[(t + 1) % n], rolled[t]) for t in range(n)]


def previous_row(tiles, sub):
    rolled = [pltpu.roll(v, 1, 0) for v in tiles]
    return [jnp.where(sub == 0, rolled[t - 1], rolled[t]) for t in range(len(tiles))]


def row_sums(tiles, sub):
    pairs = [a + b for a, b in zip(tiles, next_row(tiles, sub))]
    return [a + b for a, b in zip(pairs, previous_row(pairs, sub))]


def row_tops(tiles, sub):
    pairs = [jnp.maximum(a, b) for a, b in zip(tiles, next_row(tiles, sub))]
    return [jnp.maximum(a, b) for a, b in zip(pairs, previous_row(pairs, sub))]


def next_column(strips, lane, edge):
    rolled = [pltpu.roll(v, LANES - 1, 1) for v in strips] + [edge]
    return [jnp.where(lane == LANES - 1, rolled[j + 1], rolled[j]) for j in range(len(strips))]


def previous_column(strips, lane, edge):
    rolled = [edge] + [pltpu.roll(v, 1, 1) for v in strips]
    return [jnp.where(lane == 0, rolled[j], rolled[j + 1]) for j in range(len(strips))]


def column_stage(strips, lane):
    zero = jnp.zeros_like(strips[0])
    pairs = [a + b for a, b in zip(strips, next_column(strips, lane, zero))]
    sums = [(a + b) * SCALE for a, b in zip(pairs, previous_column(pairs, lane, strips[0]))]
    tops = [jnp.maximum(a, b) for a, b in zip(sums, next_column(sums, lane, sums[-1]))]
    tops = [jnp.maximum(a, b) for a, b in zip(tops, previous_column(tops, lane, tops[0]))]
    return sums, tops


def iotas():
    sub = lax.broadcasted_iota(jnp.int32, (SUB, LANES), 0)
    lane = lax.broadcasted_iota(jnp.int32, (SUB, LANES), 1)
    return sub, lane


def rows_of(t):
    return pl.ds(t * SUB, SUB)


def smooth_and_column_tops(flags, sec, smooth, tops, frames, tiles, halo, columns):
    sub, lane = iotas()
    off = ((sub == SUB - 1) & (flags[1] == 1)) | ((sub == 0) & (flags[2] == 1))

    def body(i, carry):
        for k in range(tiles):
            strips = [sec[i, rows_of(k), pl.ds(j * LANES, LANES)] for j in range(columns // LANES)]
            sums, highs = column_stage(strips, lane)
            for j in range(columns // LANES):
                at = pl.ds(j * LANES, LANES)
                if k == halo:
                    tops[i, rows_of(k), at] = jnp.where(off, NEG, highs[j])
                else:
                    smooth[i, rows_of(k), at] = sums[j]
                    tops[i, rows_of(k), at] = highs[j]
        return carry

    lax.fori_loop(0, frames, body, 0)


def weigh(smooth, tops, level, weight, place, count, tiles, outs, columns):
    sub, _ = iotas()

    def body(j, carry):
        at = pl.ds(pl.multiple_of(j * LANES, LANES), LANES)
        load = lambda i: [tops[i, rows_of(k), at] for k in range(tiles)]
        here = load(1)
        before = [jnp.maximum(a, b) for a, b in zip(load(0), here)]
        for i in range(1, count + 1):
            after = load(i + 1)
            pairs = [jnp.maximum(a, b) for a, b in zip(here, after)]
            highs = row_tops([jnp.maximum(a, b) for a, b in zip(before, pairs)], sub)
            here, before = after, pairs
            for k, o, v in outs:
                s = smooth[i, rows_of(k), at]
                w = jnp.exp(SHARP * (s - highs[k])) * jnp.maximum(s - level[rows_of(v), :], 0.0)
                weight[place(i), rows_of(o), at] = w
        return carry

    lax.fori_loop(0, columns // LANES, body, 0)


def box_sums(weight, sel, boxes, frame_of, count, row_of, rows, start):
    slots2 = sel.shape[1]
    f0, r0 = boxes[0:1, :], boxes[1:2, :]
    row = row_of(lax.broadcasted_iota(jnp.int32, (rows, slots2), 0)) - r0
    row_pick = jnp.where((row >= 0) & (row < BOX_R), 1.0, 0.0)
    row_odd = row_pick * (2 * row - (BOX_R - 1)).astype(jnp.float32)

    def body(i, carry):
        w = weight[i]
        high = w.astype(jnp.bfloat16)
        low = (w - high.astype(jnp.float32)).astype(jnp.bfloat16)
        table = sel[...]
        folded = jnp.dot(high, table, preferred_element_type=jnp.float32)
        folded = folded + jnp.dot(low, table, preferred_element_type=jnp.float32)
        frame = frame_of(i) - f0
        pick = jnp.where((frame >= 0) & (frame < BOX_F), 1.0, 0.0)
        odd = pick * (2 * frame - (BOX_F - 1)).astype(jnp.float32)
        plain = jnp.sum(folded * row_pick, axis=0, keepdims=True)
        by_row = jnp.sum(folded * row_odd, axis=0, keepdims=True)
        return (carry[0] + plain * pick, carry[1] + plain * odd, carry[2] + by_row * pick)

    return lax.fori_loop(0, count, body, start)


def early_kernel(
    flags, x, a, h, level, sel, boxes, out, own, sums, sec, smooth, tops, weight, sem, *, early, halo_first
):
    count, rows, columns = x.shape
    tiles = rows // SUB
    sub, _ = iotas()
    even = flags[0] == 1

    def body(j, carry):
        at = pl.ds(pl.multiple_of(j * LANES, LANES), LANES)

        def load(p):
            if p >= count:
                return None
            if p < 0:
                index = jnp.where(even, -1 - p, REACH + p)
                return [a[index, rows_of(t), at] for t in range(tiles)] + [h[index, :, at]]
            index = jnp.where(even, count - 1 - p, p)
            return [x[index, rows_of(t), at] for t in range(tiles)] + [h[halo_first + index, :, at]]

        window = load(-REACH)
        for p in range(1 - REACH, SPAN - REACH):
            window = [u + v for u, v in zip(window, load(p))]
        last_c = last_d = None
        for p in range(-2, count + 2):
            if p > -2:
                if p + BW < count:
                    window = [u + v for u, v in zip(window, load(p + BW))]
                window = [u - v for u, v in zip(window, load(p - BW - 1))]
            f = load(p)
            c = [-v for v in window] if f is None else [float(SPAN) * u - v for u, v in zip(f, window)]
            if last_c is not None:
                d = [u + v for u, v in zip(last_c, c)]
                if last_d is not None:
                    second = row_sums([u + v for u, v in zip(last_d, d)], sub)
                    q = p - 1
                    for t in range(tiles + 1):
                        if q <= early:
                            sec[q + 1, rows_of(t), at] = second[t]
                        if q >= early - 1:
                            own[q - early + 1, rows_of(t), at] = second[t]
                last_d = d
            last_c = c
        return carry

    lax.fori_loop(0, columns // LANES, body, 0)
    smooth_and_column_tops(flags, sec, smooth, tops, early + 2, tiles + 1, tiles, columns)
    weigh(
        smooth,
        tops,
        level,
        weight,
        lambda i: jnp.where(even, early - i, i - 1),
        early,
        tiles + 1,
        [(t, t, t) for t in range(tiles)],
        columns,
    )
    first = jnp.where(even, count - early, 0)
    copy = pltpu.make_async_copy(weight, out.at[pl.ds(first, early)], sem)
    copy.start()
    zero = jnp.zeros((1, sel.shape[1]), jnp.float32)
    result = box_sums(weight, sel, boxes, lambda i: first + i, early, lambda r: r, rows, (zero,) * 3)
    for i in range(3):
        sums[i : i + 1, :] = result[i]
    copy.wait()


def late_kernel(
    flags, own, b0, b1, h, level, sel, boxes, sums, _, out, stats, sec, smooth, tops, weight, sem, *, count, early
):
    late = count - early
    rows, columns = out.shape[1], out.shape[2]
    tiles = rows // SUB
    sub, _ = iotas()
    even = flags[0] == 1

    def body(j, carry):
        at = pl.ds(pl.multiple_of(j * LANES, LANES), LANES)

        def load(q):
            index = jnp.where(even, REACH - 1 - q, q)
            return (
                [b0[index, rows_of(0), at]]
                + [b1[index, rows_of(t), at] for t in range(tiles - 2)]
                + [b0[index, rows_of(1), at], h[index, :, at]]
            )

        for t in range(tiles + 1):
            for i in range(2):
                sec[i, rows_of(t), at] = own[i, rows_of(t), at]
        total = None
        c = []
        fresh = []
        for q in range(REACH):
            fresh.append(load(q))
            total = fresh[0] if q == 0 else [u + v for u, v in zip(total, fresh[q])]
            c.append([-v for v in total] if q < BW else [float(SPAN) * u - v for u, v in zip(fresh[q - BW], total)])
            d = c[0] if q == 0 else [u + v for u, v in zip(c[q - 1], c[q])]
            first = d if q == 0 else [u + v for u, v in zip(last_d, d)]
            last_d = d
            added = row_sums(first, sub)
            for t in range(tiles + 1):
                sec[q + 2, rows_of(t), at] = own[q + 2, rows_of(t), at] + added[t]
        return carry

    lax.fori_loop(0, columns // LANES, body, 0)
    smooth_and_column_tops(flags, sec, smooth, tops, late + 2, tiles + 1, tiles, columns)
    weigh(
        smooth,
        tops,
        level,
        weight,
        lambda i: jnp.where(even, late - i, i - 1),
        late,
        tiles + 1,
        [(t, t, t) for t in range(tiles)],
        columns,
    )
    first = jnp.where(even, 0, early)
    copy = pltpu.make_async_copy(weight, out.at[pl.ds(first, late)], sem)
    copy.start()
    start = tuple(sums[i : i + 1, :] for i in range(3))
    total, by_frame, by_row = box_sums(weight, sel, boxes, lambda i: first + i, late, lambda r: r, rows, start)
    slots = stats.shape[1]
    cells = float(BOX_F * BOX_R * BOX_C)
    stats[0:1, :] = total[:, :slots] / cells
    stats[1:2, :] = by_frame[:, :slots] / (cells * (BOX_F - 1))
    stats[2:3, :] = by_row[:, :slots] / (cells * (BOX_R - 1))
    stats[3:4, :] = total[:, slots:] / (cells * (BOX_C - 1))
    copy.wait()


def vmem():
    return pl.BlockSpec(memory_space=pltpu.VMEM)


def on_device(frames, thresholds, spot_boxes):
    count, rows, columns = frames.shape
    slots = spot_boxes.shape[1]
    early = count - REACH
    tiles = rows // SUB
    ring = lax.axis_size("omega")
    column = lax.axis_size("row")
    place = lax.axis_index("omega")
    even = place % 2 == 0
    partner = [(i, i ^ 1) for i in range(ring)]
    other = [(i, (i - 1) % ring if i % 2 == 0 else (i + 1) % ring) for i in range(ring)]
    up = [(i + 1, i) for i in range(column - 1)]
    down = [(i, i + 1) for i in range(column - 1)]

    far = lax.dynamic_slice_in_dim(frames, jnp.where(even, 0, count - REACH), REACH, axis=0)
    near = lax.dynamic_slice_in_dim(frames, jnp.where(even, count - REACH, 0), REACH, axis=0)
    edges = jnp.concatenate([far[:, :SUB], far[:, rows - SUB :]], axis=1)
    b0 = lax.ppermute(edges, "omega", other)
    b1 = lax.ppermute(far[:, SUB : rows - SUB], "omega", other)
    a = lax.ppermute(near, "omega", partner)

    lower = jnp.concatenate([a[:, rows - 2 :], frames[:, rows - 2 :], b0[:, 2 * SUB - 2 :]], axis=0)
    upper = jnp.concatenate([a[:, :2], frames[:, :2], b0[:, :2]], axis=0)
    above = lax.ppermute(lower, "row", down)
    below = lax.ppermute(upper, "row", up)
    h = jnp.concatenate([below, jnp.zeros((below.shape[0], SUB - 4, columns), jnp.float32), above], axis=1)

    row_place = lax.axis_index("row")
    flags = jnp.stack([even, row_place == 0, row_place == column - 1]).astype(jnp.int32)
    level = jnp.broadcast_to((thresholds.astype(jnp.float32) / 64.0)[:, None], (rows, LANES))
    live = spot_boxes[0] >= 0
    f0 = jnp.where(live, spot_boxes[0] - place * count, -BOX_F - count)
    r0 = spot_boxes[1] - row_place * rows
    boxes = jnp.stack([jnp.concatenate([f0, f0]), jnp.concatenate([r0, r0])])
    step = jnp.arange(columns)[:, None] - spot_boxes[2][None, :]
    inside = (step >= 0) & (step < BOX_C) & live[None, :]
    sel = jnp.where(
        jnp.concatenate([inside, inside], axis=1),
        jnp.concatenate([jnp.ones_like(step), 2 * step - (BOX_C - 1)], axis=1),
        0,
    ).astype(jnp.bfloat16)

    smem = pl.BlockSpec(memory_space=pltpu.SMEM)
    anywhere = pl.BlockSpec(memory_space=pl.ANY)
    padded = rows + SUB
    weight, own, sums = pl.pallas_call(
        functools.partial(early_kernel, early=early, halo_first=REACH),
        out_shape=(
            jax.ShapeDtypeStruct(frames.shape, jnp.float32),
            jax.ShapeDtypeStruct((REACH + 2, padded, columns), jnp.float32),
            jax.ShapeDtypeStruct((3, 2 * slots), jnp.float32),
        ),
        in_specs=[smem] + [vmem()] * 6,
        out_specs=(anywhere, vmem(), vmem()),
        scratch_shapes=[
            pltpu.VMEM((early + 2, padded, columns), jnp.float32),
            pltpu.VMEM((early + 2, padded, columns), jnp.float32),
            pltpu.VMEM((early + 2, padded, columns), jnp.float32),
            pltpu.VMEM((early, rows, columns), jnp.float32),
            pltpu.SemaphoreType.DMA,
        ],
        compiler_params=pltpu.CompilerParams(vmem_limit_bytes=56 << 20),
        cost_estimate=pl.CostEstimate(flops=40 * frames.size, bytes_accessed=16 << 20, transcendentals=0),
        name="early",
    )(flags, frames, a, h[: REACH + count], level, sel, boxes)
    weight, stats = pl.pallas_call(
        functools.partial(late_kernel, count=count, early=early),
        out_shape=(
            jax.ShapeDtypeStruct(frames.shape, jnp.float32),
            jax.ShapeDtypeStruct((4, slots), jnp.float32),
        ),
        in_specs=[smem] + [vmem()] * 8 + [anywhere],
        out_specs=(anywhere, vmem()),
        input_output_aliases={9: 0},
        scratch_shapes=[
            pltpu.VMEM((REACH + 2, padded, columns), jnp.float32),
            pltpu.VMEM((REACH + 2, padded, columns), jnp.float32),
            pltpu.VMEM((REACH + 2, padded, columns), jnp.float32),
            pltpu.VMEM((REACH, rows, columns), jnp.float32),
            pltpu.SemaphoreType.DMA,
        ],
        compiler_params=pltpu.CompilerParams(vmem_limit_bytes=56 << 20),
        cost_estimate=pl.CostEstimate(flops=20 * frames.size, bytes_accessed=8 << 20, transcendentals=0),
        name="late",
    )(flags, own, b0, b1, h[REACH + count :], level, sel, boxes, sums, weight)
    return weight, stats


def solution(mesh):
    return jax.shard_map(
        on_device,
        mesh=mesh,
        in_specs=(P("omega", "row", None), P("row"), P(None, ("omega", "row"))),
        out_specs=(P("omega", "row", None), P(None, ("omega", "row"))),
        check_vma=False,
    )
```

time: 115 us -> 61.5 us (0.53)
  waiting for transfers between devices: 43.6 us -> 8.23 us
  other arithmetic: 35.3 us -> 3.84 us
  Pallas kernels: 0 us -> 29.3 us
  starting transfers between devices: 19.5 us -> 9.04 us
  matrix products: 6.18 us -> 0 us
    ppermute x10 -> x5, waiting for transfers between devices: 43.6 us -> 8.23 us  [the longest x1 4.52 us: on_device(): below = lax.ppermute(upper, 'row', up)]
    pallas_call x0 -> x2, Pallas kernels: none -> 29.3 us  [the longest x1 18.3 us: on_device(): pl.pallas_call(functools.partial(early_kernel, early=early, halo_first=RE...]
    mul x5 -> x0, other arithmetic: 16.9 us -> none  [the longest x1 5.63 us: frame_filter(): return (padded[:-2] + 2.0 * padded[1:-1] + padded[2:]) * 0.25]
    ppermute x10 -> x5, starting transfers between devices: 19.5 us -> 9.04 us  [the longest x1 4.31 us: on_device(): above = lax.ppermute(lower, 'row', down)]
    sub x2 -> x1, other arithmetic: 8.68 us -> 0.07 us  [on_device(): 2 * step - (BOX_C - 1)]
    max x2 -> x0, other arithmetic: 7.38 us -> none  [the longest x1 6.46 us: row_maxima(): return jnp.maximum(jnp.maximum(fixed[:, :-2], fixed[:, 1:-1]), fixed[:, 2:])]
    dot_general x1 -> x0, matrix products: 6.18 us -> none  [on_device(): jnp.einsum('frc,kc->kfr', weight, stacked, precision=lax.Precision.HIGHEST)]
    unnamed x21 -> x6, local copies, waits for them, and re-layouts: 5.73 us -> 0.01 us
  transfers between devices with their start and end apart: 10 -> 5, of which waited for: 9 -> 3; matrix products, arithmetic and copies ran while one was open for 1% -> 20% of each run, Pallas kernels for 0% -> 30%
where the time goes in v1:
time: 61.5 us; the launch traced here: 61.2 us
  Pallas kernels  29.3 us (48%)
  local copies, waits for them, and re-layouts  9.96 us (16%)
  starting transfers between devices  9.04 us (15%)
  waiting for transfers between devices  8.23 us (13%)
  other arithmetic  3.84 us (6%)
  between operations  0.79 us (1%)
    pallas_call x1, Pallas kernels, on_device(): pl.pallas_call(functools.partial(early_kernel, early=early, halo_first=RE...  18.3 us
    pallas_call x1, Pallas kernels, on_device(): pl.pallas_call(functools.partial(late_kernel, count=count, early=early),...  11 us
    ppermute x1, waiting for transfers between devices, on_device(): below = lax.ppermute(upper, 'row', up)  4.52 us
    ppermute x1, starting transfers between devices, on_device(): above = lax.ppermute(lower, 'row', down)  4.31 us
    ppermute x1, starting transfers between devices, on_device(): b0 = lax.ppermute(edges, 'omega', other)  3.36 us
    dynamic_slice x1, local copies, waits for them, and re-layouts, on_device(): lax.dynamic_slice_in_dim(frames, jnp.where(even, count - REACH, 0), REACH...  2.73 us
    slice x3, local copies, waits for them, and re-layouts, on_device(): upper = jnp.concatenate([a[:, :2], frames[:, :2], b0[:, :2]], axis=0)  2.39 us
    ppermute x1, waiting for transfers between devices, on_device(): b0 = lax.ppermute(edges, 'omega', other)  2.35 us
  transfers between devices with their start and end apart: 5, of which 3 were waited for; matrix products, arithmetic and copies ran while one was open for 20% of the time, Pallas kernels for 30%

profile of v1, /device:TPU:0, one launch (start us, length us, event | category | flops | bytes accessed | tf_op | source)
XLA Modules:
  0.0 61.2 jit_solution(14173715141182973820)
XLA Ops:
  0.6 1.1 %constant_dynamic-slice_fusion.1 = (f32[6,8,1024]{2,1,0:T(8,128)S(1)}, f32[6,8,1024]{2,1,0:T(8,128)S(1)}) fusion(f32[16,64,1024]{2,1,0:T(8,128)} %x.3, s32[]{:T(128)S(6)} %select_n.29, s32[]{:T(128)S(6)} %add.16), kind=kLoop, calls=%fused_computation.16 | loop fusion | bytes 786440 | tf_op jit(solution)/shard_map/slice | solution.py:293
  1.7 0.8 %pad_maximum_fusion.1 = f32[6,16,1024]{2,1,0:T(8,128)} fusion(f32[6,8,1024]{2,1,0:T(8,128)S(1)} %get-tuple-element.11, f32[6,8,1024]{2,1,0:T(8,128)S(1)} %get-tuple-element.10), kind=kLoop, calls=%fused_computation.8 | loop fusion | flops 98304 | bytes 786432 | tf_op jit(solution)/shard_map/concatenate | solution.py:293
  2.5 3.4 %collective-permute-start.1 = (f32[6,16,1024]{2,1,0:T(8,128)}, f32[6,16,1024]{2,1,0:T(8,128)}, u32[]{:S(2)}, u32[]{:S(2)}) collective-permute-start(f32[6,16,1024]{2,1,0:T(8,128)} %pad_maximum_fusion.1), channel_id=1, source_target_pairs={{0,28},{4,8},{8,4},{12,16},{16,12},{20,24},{24,20},{28,0},{1,29},{... | collective-permute-start | bytes 1179656 | tf_op jit(solution)/shard_map/ppermute | solution.py:294
  5.9 0.0 copy-start.1
  5.9 1.4 %constant_dynamic-slice_fusion.2 = f32[6,48,1024]{2,1,0:T(8,128)S(1)} fusion(f32[16,64,1024]{2,1,0:T(8,128)} %x.3, s32[]{:T(128)S(6)} %select_n.29, s32[]{:T(128)S(6)} %add.17), kind=kLoop, calls=%fused_computation.17 | loop fusion | bytes 2359304 | tf_op jit(solution)/shard_map/slice | solution.py:295
  7.2 0.1 collective-permute-start.4
  7.3 2.7 %constant_dynamic-slice_fusion.3 = f32[6,64,1024]{2,1,0:T(8,128)} fusion(f32[16,64,1024]{2,1,0:T(8,128)} %x.3, s32[]{:T(128)S(6)} %select_n.28), kind=kLoop, calls=%fused_computation.18 | loop fusion | bytes 3145732 | tf_op jit(solution)/shard_map/dynamic_slice | solution.py:292
  10.0 0.0 copy-start.2
  10.0 0.0 collective-permute-start
  10.1 0.0 copy-done.1
  10.1 0.1 add_bitcast_fusion
  10.2 0.2 fusion.3
  10.3 0.1 multiply_add_fusion
  10.4 0.6 pad_add_fusion.boxes
  11.0 1.0 %select_convert_fusion.sel = bf16[1024,64]{1,0:T(8,128)(2,1)} fusion(s32[1024,32]{1,0:T(8,128)S(1)} %multiply_add_fusion, pred[1024,32]{1,0:T(8,128)(4,1)S(1)} %fusion.3), kind=kLoop, calls=%fused_computation.1 | loop fusion | flops 196608 | bytes 294912 | tf_op jit(solution)/shard_map/convert_element_type | solution.py:317
  12.0 1.3 %fusion.5 = (f32[16,2,1024]{2,1,0:T(2,128)S(1)}, f32[16,2,1024]{2,1,0:T(2,128)S(1)}) fusion(f32[16,64,1024]{2,1,0:T(8,128)} %x.3), kind=kLoop, calls=%fused_computation.25 | loop fusion | bytes 524288 | tf_op jit(solution)/shard_map/slice | solution.py:299
  13.3 2.3 %collective-permute-done.1.b0 = f32[6,16,1024]{2,1,0:T(8,128)} collective-permute-done((f32[6,16,1024]{2,1,0:T(8,128)}, f32[6,16,1024]{2,1,0:T(8,128)}, u32[]{:S(2)}, u32[]{:S(2)}) %collective-permute-start.1) | collective-permute-done | bytes 393248 | tf_op jit(solution)/shard_map/ppermute | solution.py:294
  15.7 1.1 %fusion.7 = (f32[6,2,1024]{2,1,0:T(2,128)S(1)}, f32[6,2,1024]{2,1,0:T(2,128)S(1)}) fusion(f32[6,16,1024]{2,1,0:T(8,128)} %collective-permute-done.1.b0), kind=kLoop, calls=%fused_computation.27 | loop fusion | bytes 196608 | tf_op jit(solution)/shard_map/slice | solution.py:299
  16.7 0.0 collective-permute-done.a
  16.8 0.0 copy-start
  16.8 0.1 pad_maximum_fusion.3
  16.9 4.3 %collective-permute-start.3 = (f32[28,2,1024]{2,1,0:T(2,128)S(1)}, f32[28,2,1024]{2,1,0:T(2,128)S(1)}, u32[]{:S(2)}, u32[]{:S(2)}) collective-permute-start(f32[28,2,1024]{2,1,0:T(2,128)S(1)} %pad_maximum_fusion.3), channel_id=1, source_target_pairs={{0,1},{1,2},{2,3},{4,5},{5,6},{6,7},{8,9},{9,10},{10,11},{12,13},{... | collective-permute-start | bytes 688136 | tf_op jit(solution)/shard_map/ppermute | solution.py:300
  21.2 0.1 pad_maximum_fusion.2
  21.3 1.3 %collective-permute-start.2 = (f32[28,2,1024]{2,1,0:T(2,128)S(1)}, f32[28,2,1024]{2,1,0:T(2,128)S(1)}, u32[]{:S(2)}, u32[]{:S(2)}) collective-permute-start(f32[28,2,1024]{2,1,0:T(2,128)S(1)} %pad_maximum_fusion.2), channel_id=1, source_target_pairs={{1,0},{2,1},{3,2},{5,4},{6,5},{7,6},{9,8},{10,9},{11,10},{13,12},{... | collective-permute-start | bytes 688136 | tf_op jit(solution)/shard_map/ppermute | solution.py:301
  22.6 0.7 %add_convert_fusion.flags = s32[3]{0:T(128)} fusion(pred[1]{0:T(512)(128)(4,1)} %bitcast.2, pred[1]{0:T(512)(128)(4,1)} %bitcast.1, pred[1]{0:T(512)(128)(4,1)} %bitcast), kind=kLoop, calls=%fused_computation.11 | loop fusion | flops 9 | bytes 15 | tf_op jit(solution)/shard_map/convert_element_type | solution.py:305
  23.3 0.1 pad.10.clone
  23.4 0.0 copy-done.2
  23.4 1.4 %collective-permute-done.3 = f32[28,2,1024]{2,1,0:T(2,128)S(1)} collective-permute-done((f32[28,2,1024]{2,1,0:T(2,128)S(1)}, f32[28,2,1024]{2,1,0:T(2,128)S(1)}, u32[]{:S(2)}, u32[]{:S(2)}) %collective-permute-start.3) | collective-permute-done | bytes 229408 | tf_op jit(solution)/shard_map/ppermute | solution.py:300
  24.7 4.5 %collective-permute-done.2 = f32[28,2,1024]{2,1,0:T(2,128)S(1)} collective-permute-done((f32[28,2,1024]{2,1,0:T(2,128)S(1)}, f32[28,2,1024]{2,1,0:T(2,128)S(1)}, u32[]{:S(2)}, u32[]{:S(2)}) %collective-permute-start.2) | collective-permute-done | bytes 229408 | tf_op jit(solution)/shard_map/ppermute | solution.py:301
  29.3 0.2 pad_maximum_fusion
  29.5 0.7 %slice.62.h = f32[6,8,1024]{2,1,0:T(8,128)} slice(f32[28,8,1024]{2,1,0:T(8,128)S(1)} %pad_maximum_fusion), slice={[22:28], [0:8], [0:1024]} | slice | bytes 393216 | tf_op jit(solution)/shard_map/slice | solution.py:361
  30.2 0.9 %slice.61.h = f32[22,8,1024]{2,1,0:T(8,128)} slice(f32[28,8,1024]{2,1,0:T(8,128)S(1)} %pad_maximum_fusion), slice={[0:22], [0:8], [0:1024]} | slice | bytes 1441792 | tf_op jit(solution)/shard_map/slice | solution.py:341
  31.2 0.7 %broadcast_in_dim.21.level = f32[64,128]{1,0:T(8,128)} broadcast(f32[64]{0:T(128)S(1)} %convert_multiply_fusion), dimensions={0} | broadcast | bytes 33024 | tf_op jit(solution)/shard_map/broadcast_in_dim | solution.py:306
  31.8 0.0 copy-done
  31.8 18.3 %early.1 = (f32[16,64,1024]{2,1,0:T(8,128)}, f32[8,72,1024]{2,1,0:T(8,128)}, f32[3,64]{1,0:T(4,128)}) custom-call(s32[3]{0:T(128)} %add_convert_fusion.flags, f32[16,64,1024]{2,1,0:T(8,128)} %x.3, f32[6,64,1024]{2,1,0:T(8,128)} %copy-done, f32[22,8,1024]{2,1,0:T(8,128)} %slice.61.h, f32[64,128]{1,0:T(8,128)} %broadcast_in_dim.21.level, ...), custom_call_target="tpu_custom_call" | custom-call | flops 41943040 | bytes 16777216 | tf_op jit(solution)/shard_map/early/pallas_call | solution.py:322
  50.2 0.0 collective-permute-done.4.b1
  50.2 11.0 %late.1 = (f32[16,64,1024]{2,1,0:T(8,128)}, f32[4,32]{1,0:T(4,128)}) custom-call(s32[3]{0:T(128)} %add_convert_fusion.flags, f32[8,72,1024]{2,1,0:T(8,128)} %get-tuple-element.5.own, f32[6,16,1024]{2,1,0:T(8,128)} %collective-permute-done.1.b0, f32[6,48,1024]{2,1,0:T(8,128)} %collective-permute-done.4.b1, ...), custom_call_target="tpu_custom_call", output_to_operand_aliasing={{0}: (9, {})} | custom-call | flops 20971520 | bytes 8388608 | tf_op jit(solution)/shard_map/late/pallas_call | solution.py:342
  (5 shorter events, 0.1 us)
Async XLA Ops:
  2.5 13.2 %collective-permute-start.1 = (f32[6,16,1024]{2,1,0:T(8,128)}, f32[6,16,1024]{2,1,0:T(8,128)}, u32[]{:S(2)}, u32[]{:S(2)}) collective-permute-start(f32[6,16,1024]{2,1,0:T(8,128)} %pad_maximum_fusion.1), channel_id=1, source_target_pairs={{0,28},{4,8},{8,4},{12,16},{16,12},{20,24},{24,20},{28,0},{1,29},{... | collective-permute-start | bytes 1179656 | tf_op jit(solution)/shard_map/ppermute | solution.py:294
  5.9 4.2 %copy-start.1 = (s32[3,32]{1,0:T(4,128)S(1)}, s32[3,32]{1,0:T(4,128)}, u32[]{:S(2)}) copy-start(s32[3,32]{1,0:T(4,128)} %param.5) | copy-start | bytes 1156
  7.2 42.9 %collective-permute-start.4 = (f32[6,48,1024]{2,1,0:T(8,128)S(1)}, f32[6,48,1024]{2,1,0:T(8,128)}, u32[]{:S(2)}, u32[]{:S(2)}) collective-permute-start(f32[6,48,1024]{2,1,0:T(8,128)S(1)} %constant_dynamic-slice_fusion.2), channel_id=1, source_target_pairs={{0,28},{4,8},{8,4},{12,16},{16,12},{20,24},{24,20},{28,0},{1,29},{... | collective-permute-start | bytes 3538952 | tf_op jit(solution)/shard_map/ppermute | solution.py:295
  10.0 13.3 %copy-start.2 = (s32[64]{0:T(128)S(1)}, s32[64]{0:T(128)}, u32[]{:S(2)}) copy-start(s32[64]{0:T(128)} %param.4) | copy-start | bytes 772
  10.0 6.7 %collective-permute-start = (f32[6,64,1024]{2,1,0:T(8,128)}, f32[6,64,1024]{2,1,0:T(8,128)S(1)}, u32[]{:S(2)}, u32[]{:S(2)}) collective-permute-start(f32[6,64,1024]{2,1,0:T(8,128)} %constant_dynamic-slice_fusion.3), channel_id=1, source_target_pairs={{0,4},{4,0},{8,12},{12,8},{16,20},{20,16},{24,28},{28,24},{1,5},{5... | collective-permute-start | bytes 4718600 | tf_op jit(solution)/shard_map/ppermute | solution.py:296
  16.8 15.1 %copy-start = (f32[6,64,1024]{2,1,0:T(8,128)}, f32[6,64,1024]{2,1,0:T(8,128)S(1)}, u32[]{:S(2)}) copy-start(f32[6,64,1024]{2,1,0:T(8,128)S(1)} %collective-permute-done.a) | copy-start | bytes 4718596
  16.9 7.8 %collective-permute-start.3 = (f32[28,2,1024]{2,1,0:T(2,128)S(1)}, f32[28,2,1024]{2,1,0:T(2,128)S(1)}, u32[]{:S(2)}, u32[]{:S(2)}) collective-permute-start(f32[28,2,1024]{2,1,0:T(2,128)S(1)} %pad_maximum_fusion.3), channel_id=1, source_target_pairs={{0,1},{1,2},{2,3},{4,5},{5,6},{6,7},{8,9},{9,10},{10,11},{12,13},{... | collective-permute-start | bytes 688136 | tf_op jit(solution)/shard_map/ppermute | solution.py:300
  21.3 7.9 %collective-permute-start.2 = (f32[28,2,1024]{2,1,0:T(2,128)S(1)}, f32[28,2,1024]{2,1,0:T(2,128)S(1)}, u32[]{:S(2)}, u32[]{:S(2)}) collective-permute-start(f32[28,2,1024]{2,1,0:T(2,128)S(1)} %pad_maximum_fusion.2), channel_id=1, source_target_pairs={{1,0},{2,1},{3,2},{5,4},{6,5},{7,6},{9,8},{10,9},{11,10},{13,12},{... | collective-permute-start | bytes 688136 | tf_op jit(solution)/shard_map/ppermute | solution.py:301

commit v2 on v1

v2 whole, which is shorter than its diff:
```python
import functools

import jax
import jax.numpy as jnp
from jax import lax
from jax.experimental import pallas as pl
from jax.experimental.pallas import tpu as pltpu
from jax.sharding import PartitionSpec as P

BW = 4
BOX_F = 8
BOX_R = 16
BOX_C = 16
SHARP = 8.0

SUB = 8
LANES = 128
REACH = BW + 2
SPAN = 2 * BW + 1
NEG = -1e30
TOP = 8
PIECES = ((0, 3), (3, 5), (5, 6))
SCALE = 1.0 / (SPAN * 64.0)


def frame_taps():
    three = {-1: 1, 0: 2, 1: 1}
    return [
        SPAN * three.get(d, 0) - sum(w for e, w in three.items() if abs(d - e) <= BW) for d in range(BW + 2)
    ]


def next_column(strips, lane, edge):
    rolled = [pltpu.roll(v, LANES - 1, 1) for v in strips] + [edge]
    return [jnp.where(lane == LANES - 1, rolled[j + 1], rolled[j]) for j in range(len(strips))]


def previous_column(strips, lane, edge):
    rolled = [edge] + [pltpu.roll(v, 1, 1) for v in strips]
    return [jnp.where(lane == 0, rolled[j], rolled[j + 1]) for j in range(len(strips))]


def iotas():
    sub = lax.broadcasted_iota(jnp.int32, (SUB, LANES), 0)
    lane = lax.broadcasted_iota(jnp.int32, (SUB, LANES), 1)
    return sub, lane


def rows_of(t):
    return pl.ds(t * SUB, SUB)


def store_rows(ref, i, j, tiles):
    for t, v in enumerate(tiles[:-1]):
        ref[i, j, pl.ds(TOP + t * SUB, SUB), :] = v
    ref[i, j, pl.ds(0, SUB), :] = tiles[-1]
    ref[i, j, pl.ds(TOP + (len(tiles) - 1) * SUB, SUB), :] = tiles[-1]


def smooth_stage(flags, first, smooth, count, shift, rows, strips):
    sub, lane = iotas()
    starts = [-1 + SUB * k for k in range(rows // SUB)] + [rows + 1 - SUB]
    above = (sub == 0) & (flags[1] == 1)
    below = (sub == SUB - 1) & (flags[2] == 1)
    zero = jnp.zeros((SUB, LANES), jnp.float32)

    def body(i, carry):
        for k, start in enumerate(starts):
            seconds = []
            for j in range(strips):
                a, b, c = (first[i, j, pl.ds(TOP + start + e, SUB), :] for e in (-1, 0, 1))
                seconds.append((a + b) + (b + c))
            pairs = [a + b for a, b in zip(seconds, next_column(seconds, lane, zero))]
            sums = [a + b for a, b in zip(pairs, previous_column(pairs, lane, seconds[0]))]
            for j in range(strips):
                v = sums[j]
                if k == 0:
                    v = jnp.where(above, NEG, v)
                if k == len(starts) - 1:
                    v = jnp.where(below, NEG, v)
                smooth[i + shift, j, pl.ds(TOP + start, SUB), :] = v
        return carry

    lax.fori_loop(0, count, body, 0)


def weigh(smooth_of, level, weight, place, count, rows, strips):
    _, lane = iotas()

    def body(t, carry):
        base = t * SUB + TOP
        at = pl.ds(pl.multiple_of(t * SUB, SUB), SUB)

        def row_tops(i):
            ref, index = smooth_of(i)
            loads = ([ref[index, j, pl.ds(base + e, SUB), :] for e in (-1, 0, 1)] for j in range(strips))
            return [jnp.maximum(jnp.maximum(a, b), c) for a, b, c in loads]

        here = row_tops(1)
        before = [jnp.maximum(a, b) for a, b in zip(row_tops(0), here)]
        floor = level[at, :]
        for i in range(1, count + 1):
            after = row_tops(i + 1)
            pairs = [jnp.maximum(a, b) for a, b in zip(here, after)]
            highs = [jnp.maximum(a, b) for a, b in zip(before, pairs)]
            here, before = after, pairs
            tops = [jnp.maximum(a, b) for a, b in zip(highs, next_column(highs, lane, highs[-1]))]
            tops = [jnp.maximum(a, b) for a, b in zip(tops, previous_column(tops, lane, tops[0]))]
            ref, index = smooth_of(i)
            for j in range(strips):
                s = ref[index, j, pl.ds(base, SUB), :]
                w = jnp.exp((SHARP * SCALE) * (s - tops[j])) * jnp.maximum(s * SCALE - floor, 0.0)
                weight[place(i), at, pl.ds(j * LANES, LANES)] = w
        return carry

    lax.fori_loop(0, rows // SUB, body, 0)


def box_sums(weight, sel, boxes, first, start):
    count, rows, columns = weight.shape
    group = 2 if count % 2 == 0 else 1
    slots2 = sel.shape[1]
    f0, r0 = boxes[0:1, :], boxes[1:2, :]
    row = lax.broadcasted_iota(jnp.int32, (rows, slots2), 0) - r0
    row_pick = jnp.where((row >= 0) & (row < BOX_R), 1.0, 0.0)
    row_odd = row_pick * (2 * row - (BOX_R - 1)).astype(jnp.float32)

    def body(i, carry):
        w = weight[pl.ds(i * group, group)].reshape(group * rows, columns)
        high = w.astype(jnp.bfloat16)
        low = (w - high.astype(jnp.float32)).astype(jnp.bfloat16)
        table = sel[...]
        folded = jnp.dot(high, table, preferred_element_type=jnp.float32)
        folded = folded + jnp.dot(low, table, preferred_element_type=jnp.float32)
        for k in range(group):
            part = folded[k * rows : (k + 1) * rows]
            frame = first + i * group + k - f0
            pick = jnp.where((frame >= 0) & (frame < BOX_F), 1.0, 0.0)
            odd = pick * (2 * frame - (BOX_F - 1)).astype(jnp.float32)
            plain = jnp.sum(part * row_pick, axis=0, keepdims=True)
            by_row = jnp.sum(part * row_odd, axis=0, keepdims=True)
            carry = (carry[0] + plain * pick, carry[1] + plain * odd, carry[2] + by_row * pick)
        return carry

    return lax.fori_loop(0, count // group, body, start)


def early_kernel(
    flags, x, a, h, level, sel, boxes, out, part, edge, sums, first, smooth, weight, sems, *, early
):
    count, rows, columns = x.shape
    tiles, strips = rows // SUB, columns // LANES
    even = flags[0] == 1

    def body(j, carry):
        at = pl.ds(pl.multiple_of(j * LANES, LANES), LANES)

        def load(p):
            if p >= count:
                return None
            if p < 0:
                index = jnp.where(even, -1 - p, REACH + p)
                where = count + index
                return [a[index, rows_of(t), at] for t in range(tiles)] + [h[where, :, at]]
            index = jnp.where(even, count - 1 - p, p)
            return [x[index, rows_of(t), at] for t in range(tiles)] + [h[index, :, at]]

        window = load(-REACH)
        for p in range(1 - REACH, SPAN - REACH):
            window = [u + v for u, v in zip(window, load(p))]
        last_c = last_d = None
        for p in range(-2, count + 2):
            if p > -2:
                if p + BW < count:
                    window = [u + v for u, v in zip(window, load(p + BW))]
                window = [u - v for u, v in zip(window, load(p - BW - 1))]
            f = load(p)
            c = [-v for v in window] if f is None else [float(SPAN) * u - v for u, v in zip(f, window)]
            if last_c is not None:
                d = [u + v for u, v in zip(last_c, c)]
                if last_d is not None:
                    result = [u + v for u, v in zip(last_d, d)]
                    q = p - 1
                    if q <= early:
                        store_rows(first, q + 1, j, result)
                    else:
                        for t, v in enumerate(result):
                            part[q - early - 1, j, rows_of(t), :] = v
                last_d = d
            last_c = c
        return carry

    lax.fori_loop(0, strips, body, 0)
    smooth_stage(flags, first, smooth, early + 2, 0, rows, strips)
    copy_edge = pltpu.make_async_copy(smooth.at[pl.ds(early, 2)], edge, sems.at[0])
    copy_edge.start()
    weigh(lambda i: (smooth, i), level, weight, lambda i: jnp.where(even, early - i, i - 1), early, rows, strips)
    start = jnp.where(even, count - early, 0)
    copy = pltpu.make_async_copy(weight, out.at[pl.ds(start, early)], sems.at[1])
    copy.start()
    zero = jnp.zeros((1, sel.shape[1]), jnp.float32)
    result = box_sums(weight, sel, boxes, start, (zero,) * 3)
    for i in range(3):
        sums[i : i + 1, :] = result[i]
    copy_edge.wait()
    copy.wait()


def late_kernel(flags, part, edge, b, b0, h, level, sel, boxes, sums, _, out, *rest, count, piece):
    begin, end = piece
    late = end - begin
    final = end == REACH
    if final:
        stats, first, smooth, weight, sems = rest
    else:
        new_part, new_edge, new_sums, first, smooth, weight, sems = rest
    rows, columns = out.shape[1], out.shape[2]
    tiles, strips = rows // SUB, columns // LANES
    even = flags[0] == 1
    taps = frame_taps()
    early = count - REACH

    def body(j, carry):
        at = pl.ds(pl.multiple_of(j * LANES, LANES), LANES)

        def load(q):
            index = jnp.where(even, end - 1 - q, q - begin)
            where = jnp.where(even, REACH - 1 - q, q)
            return (
                [b0[where, rows_of(0), at]]
                + [b[index, rows_of(t), at] for t in range(tiles - 2)]
                + [b0[where, rows_of(1), at], h[where, :, at]]
            )

        fresh = {q: load(q) for q in range(begin, end)}
        for i in range(REACH - begin):
            total = [part[i, j, rows_of(t), :] for t in range(tiles + 1)]
            for q in range(begin, end):
                distance = REACH - 1 + q - begin - i
                if abs(distance) < REACH:
                    tap = float(taps[abs(distance)])
                    if tap == -1.0:
                        total = [u - v for u, v in zip(total, fresh[q])]
                    else:
                        total = [u + tap * v for u, v in zip(total, fresh[q])]
            if i < late:
                store_rows(first, i, j, total)
            else:
                for t, v in enumerate(total):
                    new_part[i - late, j, rows_of(t), :] = v
        return carry

    lax.fori_loop(0, strips, body, 0)
    smooth_stage(flags, first, smooth, late, 0, rows, strips)
    copies = []
    if not final:
        copies.append(pltpu.make_async_copy(smooth.at[pl.ds(late - 2, 2)], new_edge, sems.at[0]))
        copies[0].start()
    weigh(
        lambda i: (edge, i) if i < 2 else (smooth, i - 2),
        level,
        weight,
        lambda i: jnp.where(even, late - i, i - 1),
        late,
        rows,
        strips,
    )
    place = jnp.where(even, REACH - end, early + begin)
    copies.append(pltpu.make_async_copy(weight, out.at[pl.ds(place, late)], sems.at[1]))
    copies[-1].start()
    start = tuple(sums[i : i + 1, :] for i in range(3))
    total, by_frame, by_row = box_sums(weight, sel, boxes, place, start)
    if final:
        slots = stats.shape[1]
        cells = float(BOX_F * BOX_R * BOX_C)
        stats[0:1, :] = total[:, :slots] / cells
        stats[1:2, :] = by_frame[:, :slots] / (cells * (BOX_F - 1))
        stats[2:3, :] = by_row[:, :slots] / (cells * (BOX_R - 1))
        stats[3:4, :] = total[:, slots:] / (cells * (BOX_C - 1))
    else:
        for i, v in enumerate((total, by_frame, by_row)):
            new_sums[i : i + 1, :] = v
    for copy in copies:
        copy.wait()


def shape(*sizes):
    return jax.ShapeDtypeStruct(sizes, jnp.float32)


def vmem():
    return pl.BlockSpec(memory_space=pltpu.VMEM)


def halo_rows(lower, upper):
    column = lax.axis_size("row")
    above = lax.ppermute(lower, "row", [(i, i + 1) for i in range(column - 1)])
    below = lax.ppermute(upper, "row", [(i + 1, i) for i in range(column - 1)])
    middle = jnp.zeros((below.shape[0], SUB - 4, below.shape[2]), jnp.float32)
    return jnp.concatenate([below, middle, above], axis=1)


def on_device(frames, thresholds, spot_boxes):
    count, rows, columns = frames.shape
    slots = spot_boxes.shape[1]
    early = count - REACH
    tiles, strips = rows // SUB, columns // LANES
    ring = lax.axis_size("omega")
    place = lax.axis_index("omega")
    even = place % 2 == 0
    partner = [(i, i ^ 1) for i in range(ring)]
    other = [(i, (i - 1) % ring if i % 2 == 0 else (i + 1) % ring) for i in range(ring)]

    tiled = frames.reshape(count, tiles, SUB, columns)
    far = lax.dynamic_slice_in_dim(tiled, jnp.where(even, 0, count - REACH), REACH, axis=0)
    b0 = lax.ppermute(far[:, :: tiles - 1], "omega", other).reshape(REACH, 2 * SUB, columns)
    near = lax.dynamic_slice_in_dim(frames, jnp.where(even, count - REACH, 0), REACH, axis=0)
    a = lax.ppermute(near, "omega", partner)
    pieces = []
    for begin, end in PIECES:
        piece = lax.dynamic_slice_in_dim(frames, jnp.where(even, begin, count - end), end - begin, axis=0)
        pieces.append(lax.ppermute(piece[:, SUB : rows - SUB], "omega", other))

    own_lower, own_upper = frames[:, rows - 2 :], frames[:, :2]
    a_lower, a_upper = a[:, rows - 2 :], a[:, :2]
    h1 = halo_rows(jnp.concatenate([own_lower, a_lower]), jnp.concatenate([own_upper, a_upper]))
    h2 = halo_rows(b0[:, 2 * SUB - 2 :], b0[:, :2])

    row_place = lax.axis_index("row")
    flags = jnp.stack([even, row_place == 0, row_place == lax.axis_size("row") - 1]).astype(jnp.int32)
    level = jnp.broadcast_to((thresholds.astype(jnp.float32) / 64.0)[:, None], (rows, LANES))
    live = spot_boxes[0] >= 0
    f0 = jnp.where(live, spot_boxes[0] - place * count, -BOX_F - count)
    r0 = spot_boxes[1] - row_place * rows
    boxes = jnp.stack([jnp.concatenate([f0, f0]), jnp.concatenate([r0, r0])])
    step = jnp.arange(columns)[:, None] - spot_boxes[2][None, :]
    inside = (step >= 0) & (step < BOX_C) & live[None, :]
    sel = jnp.where(
        jnp.concatenate([inside, inside], axis=1),
        jnp.concatenate([jnp.ones_like(step), 2 * step - (BOX_C - 1)], axis=1),
        0,
    ).astype(jnp.bfloat16)

    smem = pl.BlockSpec(memory_space=pltpu.SMEM)
    anywhere = pl.BlockSpec(memory_space=pl.ANY)
    padded = rows + 2 * TOP
    params = pltpu.CompilerParams(vmem_limit_bytes=56 << 20)
    weight, part, edge, sums = pl.pallas_call(
        functools.partial(early_kernel, early=early),
        out_shape=(
            shape(count, rows, columns),
            shape(REACH, strips, rows + SUB, LANES),
            shape(2, strips, padded, LANES),
            shape(3, 2 * slots),
        ),
        in_specs=[smem] + [vmem()] * 6,
        out_specs=(anywhere, vmem(), anywhere, vmem()),
        scratch_shapes=[
            pltpu.VMEM((early + 2, strips, padded, LANES), jnp.float32),
            pltpu.VMEM((early + 2, strips, padded, LANES), jnp.float32),
            pltpu.VMEM((early, rows, columns), jnp.float32),
            pltpu.SemaphoreType.DMA((2,)),
        ],
        compiler_params=params,
        cost_estimate=pl.CostEstimate(flops=40 * frames.size, bytes_accessed=16 << 20, transcendentals=0),
        name="early",
    )(flags, frames, a, h1, level, sel, boxes)
    for (begin, end), piece in zip(PIECES, pieces):
        final = end == REACH
        late = end - begin
        results = pl.pallas_call(
            functools.partial(late_kernel, count=count, piece=(begin, end)),
            out_shape=(shape(count, rows, columns),)
            + (
                (shape(4, slots),)
                if final
                else (
                    shape(REACH - end, strips, rows + SUB, LANES),
                    shape(2, strips, padded, LANES),
                    shape(3, 2 * slots),
                )
            ),
            in_specs=[smem] + [vmem()] * 9 + [anywhere],
            out_specs=(anywhere,) + ((vmem(),) if final else (vmem(), anywhere, vmem())),
            input_output_aliases={10: 0},
            scratch_shapes=[
                pltpu.VMEM((late, strips, padded, LANES), jnp.float32),
                pltpu.VMEM((late, strips, padded, LANES), jnp.float32),
                pltpu.VMEM((late, rows, columns), jnp.float32),
                pltpu.SemaphoreType.DMA((2,)),
            ],
            compiler_params=params,
            cost_estimate=pl.CostEstimate(flops=8 * late * rows * columns, bytes_accessed=4 << 20, transcendentals=0),
            name=f"late_{begin}",
        )(flags, part, edge, piece, b0, h2, level, sel, boxes, sums, weight)
        if final:
            weight, stats = results
        else:
            weight, part, edge, sums = results
    return weight, stats


def solution(mesh):
    return jax.shard_map(
        on_device,
        mesh=mesh,
        in_specs=(P("omega", "row", None), P("row"), P(None, ("omega", "row"))),
        out_specs=(P("omega", "row", None), P(None, ("omega", "row"))),
        check_vma=False,
    )
```

time: 61.5 us -> 68 us (1.11)
  starting transfers between devices: 9.04 us -> 18.2 us
  waiting for transfers between devices: 8.23 us -> 2.44 us
  local copies, waits for them, and re-layouts: 9.96 us -> 11.3 us
  Pallas kernels: 29.3 us -> 30.1 us
    ppermute x4 -> x8, starting transfers between devices: 9.04 us -> 17.7 us  [the longest x2 8.92 us: halo_rows(): above = lax.ppermute(lower, 'row', [(i, i + 1) for i in range(column - 1)])]
    ppermute x4 -> x8, waiting for transfers between devices: 8.22 us -> 2.44 us  [the longest x2 1.67 us: halo_rows(): above = lax.ppermute(lower, 'row', [(i, i + 1) for i in range(column - 1)])]
    dynamic_slice x0 -> x1, local copies, waits for them, and re-layouts: none -> 1.51 us  [on_device(): lax.dynamic_slice_in_dim(tiled, jnp.where(even, 0, count - REACH), REACH,...]
    dynamic_slice x1, local copies, waits for them, and re-layouts: 2.73 us -> 1.52 us  [on_device(): lax.dynamic_slice_in_dim(frames, jnp.where(even, count - REACH, 0), REACH...]
    slice x7, local copies, waits for them, and re-layouts: 6.46 us -> 7.49 us  [the longest x3 5.34 us: on_device(): pieces.append(lax.ppermute(piece[:, SUB:rows - SUB], 'omega', other))]
    pallas_call x2 -> x4, Pallas kernels: 29.3 us -> 30.1 us  [the longest x3 16.7 us: on_device(): pl.pallas_call(functools.partial(late_kernel, count=count, piece=(begin,...]
    concatenate x4, other arithmetic: 1.23 us -> 1.97 us  [the longest x2 1.81 us: halo_rows(): return jnp.concatenate([below, middle, above], axis=1)]
  transfers between devices with their start and end apart: 5 -> 9, of which waited for: 3 -> 3; matrix products, arithmetic and copies ran while one was open for 20% -> 21% of each run, Pallas kernels for 30% -> 38%
where the time goes in v2:
time: 68 us; the launch traced here: 67.5 us
  Pallas kernels  30.1 us (44%)
  starting transfers between devices  18.2 us (27%)
  local copies, waits for them, and re-layouts  11.3 us (17%)
  other arithmetic  4.49 us (7%)
  waiting for transfers between devices  2.44 us (4%)
  between operations  0.86 us (1%)
    pallas_call x3, Pallas kernels, on_device(): pl.pallas_call(functools.partial(late_kernel, count=count, piece=(begin,...  16.7 us
    pallas_call x1, Pallas kernels, on_device(): pl.pallas_call(functools.partial(early_kernel, early=early), out_shape=(s...  13.4 us
    ppermute x2, starting transfers between devices, halo_rows(): above = lax.ppermute(lower, 'row', [(i, i + 1) for i in range(column - 1)])  8.92 us
    slice x3, local copies, waits for them, and re-layouts, on_device(): pieces.append(lax.ppermute(piece[:, SUB:rows - SUB], 'omega', other))  5.34 us
    ppermute x1, starting transfers between devices, on_device(): lax.ppermute(far[:, ::tiles - 1], 'omega', other)  3.54 us
    ppermute x3, starting transfers between devices, on_device(): pieces.append(lax.ppermute(piece[:, SUB:rows - SUB], 'omega', other))  2.65 us
    ppermute x2, starting transfers between devices, halo_rows(): below = lax.ppermute(upper, 'row', [(i + 1, i) for i in range(column - 1)])  2.58 us
    concatenate x2, other arithmetic, halo_rows(): return jnp.concatenate([below, middle, above], axis=1)  1.81 us
  transfers between devices with their start and end apart: 9, of which 3 were waited for; matrix products, arithmetic and copies ran while one was open for 21% of the time, Pallas kernels for 38%

profile of v2, /device:TPU:0, one launch (start us, length us, event | category | flops | bytes accessed | tf_op | source)
XLA Modules:
  0.0 67.5 jit_solution(17984826696314883059)
XLA Ops:
  0.6 0.0 copy-start.2
  0.7 0.0 copy-start.3
  0.7 1.5 %constant_dynamic-slice_fusion.4 = f32[6,64,1024]{2,1,0:T(8,128)S(1)} fusion(f32[16,64,1024]{2,1,0:T(8,128)} %x.3, s32[]{:T(128)S(6)} %select_n.40), kind=kLoop, calls=%fused_computation.16 | loop fusion | bytes 3145732 | tf_op jit(solution)/shard_map/dynamic_slice | solution.py:317
  2.2 0.6 collective-permute-start
  2.7 1.5 %constant_dynamic-slice_fusion.2 = f32[6,8,8,1024]{3,2,1,0:T(8,128)S(1)} fusion(f32[16,8,8,1024]{3,2,1,0:T(8,128)} %bitcast.17, s32[]{:T(128)S(6)} %select_n.45), kind=kLoop, calls=%fused_computation.14 | loop fusion | bytes 3145732 | tf_op jit(solution)/shard_map/dynamic_slice | solution.py:315
  4.3 0.8 %slice.48 = f32[6,2,8,1024]{3,2,1,0:T(8,128)} slice(f32[6,8,8,1024]{3,2,1,0:T(8,128)S(1)} %constant_dynamic-slice_fusion.2), slice={[0:6:1], [0:8:7], [0:8:1], [0:1024:1]} | slice | bytes 786432 | tf_op jit(solution)/shard_map/slice | solution.py:316
  5.0 3.5 %collective-permute-start.4 = (f32[6,2,8,1024]{3,2,1,0:T(8,128)}, f32[6,2,8,1024]{3,2,1,0:T(8,128)S(1)}, u32[]{:S(2)}, u32[]{:S(2)}) collective-permute-start(f32[6,2,8,1024]{3,2,1,0:T(8,128)} %slice.48), channel_id=1, source_target_pairs={{0,28},{4,8},{8,4},{12,16},{16,12},{20,24},{24,20},{28,0},{1,29},{... | collective-permute-start | bytes 1179656 | tf_op jit(solution)/shard_map/ppermute | solution.py:316
  8.6 2.0 %constant_dynamic-slice_fusion.3 = f32[3,48,1024]{2,1,0:T(8,128)} fusion(f32[16,64,1024]{2,1,0:T(8,128)} %x.3, s32[]{:T(128)S(6)} %select_n.44, s32[]{:T(128)S(6)} %add.19), kind=kLoop, calls=%fused_computation.15 | loop fusion | bytes 1179656 | tf_op jit(solution)/shard_map/slice | solution.py:322
  10.5 0.0 collective-permute-start.3
  10.5 1.8 %constant_dynamic-slice_fusion.1 = f32[2,48,1024]{2,1,0:T(8,128)} fusion(f32[16,64,1024]{2,1,0:T(8,128)} %x.3, s32[]{:T(128)S(6)} %select_n.46, s32[]{:T(128)S(6)} %add.19), kind=kLoop, calls=%fused_computation.13 | loop fusion | bytes 786440 | tf_op jit(solution)/shard_map/slice | solution.py:322
  12.3 2.6 %collective-permute-start.7 = (f32[2,48,1024]{2,1,0:T(8,128)}, f32[2,48,1024]{2,1,0:T(8,128)}, u32[]{:S(2)}, u32[]{:S(2)}) collective-permute-start(f32[2,48,1024]{2,1,0:T(8,128)} %constant_dynamic-slice_fusion.1), channel_id=1, source_target_pairs={{0,28},{4,8},{8,4},{12,16},{16,12},{20,24},{24,20},{28,0},{1,29},{... | collective-permute-start | bytes 1179656 | tf_op jit(solution)/shard_map/ppermute | solution.py:322
  15.0 1.6 %constant_dynamic-slice_fusion = f32[1,48,1024]{2,1,0:T(8,128)} fusion(f32[16,64,1024]{2,1,0:T(8,128)} %x.3, s32[]{:T(128)S(6)} %select_n.47, s32[]{:T(128)S(6)} %add.19), kind=kLoop, calls=%fused_computation.12 | loop fusion | bytes 393224 | tf_op jit(solution)/shard_map/slice | solution.py:322
  16.6 0.0 collective-permute-start.8
  16.6 0.0 copy-done.2
  16.6 0.1 add_bitcast_fusion
  16.7 0.6 pad_add_fusion.boxes
  17.2 0.0 copy-done.3
  17.2 0.2 fusion.3
  17.4 0.1 multiply_add_fusion
  17.5 0.6 add_convert_fusion.flags
  18.1 0.1 pad.13.clone
  18.1 1.1 %select_convert_fusion.sel = bf16[1024,64]{1,0:T(8,128)(2,1)} fusion(s32[1024,32]{1,0:T(8,128)S(1)} %multiply_add_fusion, pred[1024,32]{1,0:T(8,128)(4,1)S(1)} %fusion.3), kind=kLoop, calls=%fused_computation.1 | loop fusion | flops 196608 | bytes 294912 | tf_op jit(solution)/shard_map/convert_element_type | solution.py:342
  19.2 1.3 %fusion.5 = (f32[16,2,1024]{2,1,0:T(2,128)S(1)}, f32[16,2,1024]{2,1,0:T(2,128)S(1)}) fusion(f32[16,64,1024]{2,1,0:T(8,128)} %x.3), kind=kLoop, calls=%fused_computation.26 | loop fusion | bytes 524288 | tf_op jit(solution)/shard_map/slice | solution.py:324
  20.5 0.0 collective-permute-done.4
  20.5 0.0 copy-start
  20.6 1.3 %collective-permute-start.5 = (f32[6,2,1024]{2,1,0:T(2,128)S(1)}, f32[6,2,1024]{2,1,0:T(2,128)S(1)}, u32[]{:S(2)}, u32[]{:S(2)}) collective-permute-start(f32[6,2,1024]{2,1,0:T(2,128)S(1)} %get-tuple-element.30), channel_id=1, source_target_pairs={{1,0},{2,1},{3,2},{5,4},{6,5},{7,6},{9,8},{10,9},{11,10},{13,12},{... | collective-permute-start | bytes 147464 | tf_op jit(solution)/shard_map/ppermute | solution.py:298
  21.9 0.0 collective-permute-done.a
  21.9 0.0 copy-start.1
  21.9 4.5 %collective-permute-start.6 = (f32[6,2,1024]{2,1,0:T(2,128)S(1)}, f32[6,2,1024]{2,1,0:T(2,128)S(1)}, u32[]{:S(2)}, u32[]{:S(2)}) collective-permute-start(f32[6,2,1024]{2,1,0:T(2,128)S(1)} %get-tuple-element.31), channel_id=1, source_target_pairs={{0,1},{1,2},{2,3},{4,5},{5,6},{6,7},{8,9},{9,10},{10,11},{12,13},{... | collective-permute-start | bytes 147464 | tf_op jit(solution)/shard_map/ppermute | solution.py:297
  26.5 0.1 pad_maximum_fusion.2
  26.6 0.1 pad_maximum_fusion.3
  26.7 0.0 collective-permute-done.5
  26.7 1.3 %collective-permute-start.1 = (f32[22,2,1024]{2,1,0:T(2,128)S(1)}, f32[22,2,1024]{2,1,0:T(2,128)S(1)}, u32[]{:S(2)}, u32[]{:S(2)}) collective-permute-start(f32[22,2,1024]{2,1,0:T(2,128)S(1)} %pad_maximum_fusion.2), channel_id=1, source_target_pairs={{1,0},{2,1},{3,2},{5,4},{6,5},{7,6},{9,8},{10,9},{11,10},{13,12},{... | collective-permute-start | bytes 540680 | tf_op jit(solution)/shard_map/ppermute | solution.py:298
  28.0 0.2 collective-permute-done.6
  28.2 4.4 %collective-permute-start.2 = (f32[22,2,1024]{2,1,0:T(2,128)S(1)}, f32[22,2,1024]{2,1,0:T(2,128)S(1)}, u32[]{:S(2)}, u32[]{:S(2)}) collective-permute-start(f32[22,2,1024]{2,1,0:T(2,128)S(1)} %pad_maximum_fusion.3), channel_id=1, source_target_pairs={{0,1},{1,2},{2,3},{4,5},{5,6},{6,7},{8,9},{9,10},{10,11},{12,13},{... | collective-permute-start | bytes 540680 | tf_op jit(solution)/shard_map/ppermute | solution.py:297
  32.5 0.8 %pad_maximum_fusion.1.h = f32[6,8,1024]{2,1,0:T(8,128)} fusion(f32[6,2,1024]{2,1,0:T(2,128)S(1)} %collective-permute-done.6, f32[6,2,1024]{2,1,0:T(2,128)S(1)} %collective-permute-done.5, f32[8]{0:T(128)S(1)} %pad.13.clone), kind=kLoop, calls=%fused_computation.8 | loop fusion | flops 98304 | bytes 294944 | tf_op jit(solution)/shard_map/concatenate | solution.py:300
  33.3 0.8 %collective-permute-done.1 = f32[22,2,1024]{2,1,0:T(2,128)S(1)} collective-permute-done((f32[22,2,1024]{2,1,0:T(2,128)S(1)}, f32[22,2,1024]{2,1,0:T(2,128)S(1)}, u32[]{:S(2)}, u32[]{:S(2)}) %collective-permute-start.1) | collective-permute-done | bytes 180256 | tf_op jit(solution)/shard_map/ppermute | solution.py:298
  34.1 1.5 %collective-permute-done.2 = f32[22,2,1024]{2,1,0:T(2,128)S(1)} collective-permute-done((f32[22,2,1024]{2,1,0:T(2,128)S(1)}, f32[22,2,1024]{2,1,0:T(2,128)S(1)}, u32[]{:S(2)}, u32[]{:S(2)}) %collective-permute-start.2) | collective-permute-done | bytes 180256 | tf_op jit(solution)/shard_map/ppermute | solution.py:297
  35.5 1.1 %pad_maximum_fusion.h = f32[22,8,1024]{2,1,0:T(8,128)} fusion(f32[22,2,1024]{2,1,0:T(2,128)S(1)} %collective-permute-done.2, f32[22,2,1024]{2,1,0:T(2,128)S(1)} %collective-permute-done.1, f32[8]{0:T(128)S(1)} %pad.13.clone), kind=kLoop, calls=%fused_computation | loop fusion | flops 360448 | bytes 1081376 | tf_op jit(solution)/shard_map/concatenate | solution.py:300
  36.6 0.7 %broadcast_in_dim.24.level = f32[64,128]{1,0:T(8,128)} broadcast(f32[64]{0:T(128)S(1)} %convert_multiply_fusion), dimensions={0} | broadcast | bytes 33024 | tf_op jit(solution)/shard_map/broadcast_in_dim | solution.py:331
  37.3 0.0 copy-done.1
  37.3 13.4 %early.1 = (f32[16,64,1024]{2,1,0:T(8,128)}, f32[6,8,72,128]{3,2,1,0:T(8,128)}, f32[2,8,80,128]{3,2,1,0:T(8,128)}, f32[3,64]{1,0:T(4,128)}) custom-call(s32[3]{0:T(128)} %add_convert_fusion.flags, f32[16,64,1024]{2,1,0:T(8,128)} %x.3, f32[6,64,1024]{2,1,0:T(8,128)} %copy-done.1, f32[22,8,1024]{2,1,0:T(8,128)} %pad_maximum_fusion.h, ...), custom_call_target="tpu_custom_call" | custom-call | flops 41943040 | bytes 16777216 | tf_op jit(solution)/shard_map/early/pallas_call | solution.py:348
  50.7 0.0 copy-done
  50.7 0.0 collective-permute-done.3.b
  50.7 6.6 %late_0.1 = (f32[16,64,1024]{2,1,0:T(8,128)}, f32[3,8,72,128]{3,2,1,0:T(8,128)}, f32[2,8,80,128]{3,2,1,0:T(8,128)}, f32[3,64]{1,0:T(4,128)}) custom-call(s32[3]{0:T(128)} %add_convert_fusion.flags, f32[6,8,72,128]{3,2,1,0:T(8,128)} %get-tuple-element.14.part, f32[2,8,80,128]{3,2,1,0:T(8,128)} %get-tuple-element.15.edge, ...), custom_call_target="tpu_custom_call", output_to_operand_aliasing={{0}: (10, {})} | custom-call | flops 1572864 | bytes 4194304 | tf_op jit(solution)/shard_map/late_0/pallas_call | solution.py:371
  57.4 0.0 collective-permute-done.7.b
  57.4 5.5 %late_3.1 = (f32[16,64,1024]{2,1,0:T(8,128)}, f32[1,8,72,128]{3,2,1,0:T(8,128)}, f32[2,8,80,128]{3,2,1,0:T(8,128)}, f32[3,64]{1,0:T(4,128)}) custom-call(s32[3]{0:T(128)} %add_convert_fusion.flags, f32[3,8,72,128]{3,2,1,0:T(8,128)} %get-tuple-element.18.part, f32[2,8,80,128]{3,2,1,0:T(8,128)} %get-tuple-element.19.edge, ...), custom_call_target="tpu_custom_call", output_to_operand_aliasing={{0}: (10, {})} | custom-call | flops 1048576 | bytes 4194304 | tf_op jit(solution)/shard_map/late_3/pallas_call | solution.py:371
  62.9 0.0 collective-permute-done.8.b
  62.9 4.6 %late_5.1 = (f32[16,64,1024]{2,1,0:T(8,128)}, f32[4,32]{1,0:T(4,128)}) custom-call(s32[3]{0:T(128)} %add_convert_fusion.flags, f32[1,8,72,128]{3,2,1,0:T(8,128)} %get-tuple-element.22.part, f32[2,8,80,128]{3,2,1,0:T(8,128)} %get-tuple-element.23.edge, f32[1,48,1024]{2,1,0:T(8,128)} %collective-permute-done.8.b, ...), custom_call_target="tpu_custom_call", output_to_operand_aliasing={{0}: (10, {})} | custom-call | flops 524288 | bytes 4194304 | tf_op jit(solution)/shard_map/late_5/pallas_call | solution.py:371
  (6 shorter events, 0.1 us)
Async XLA Ops:
  0.6 15.9 %copy-start.2 = (s32[3,32]{1,0:T(4,128)S(1)}, s32[3,32]{1,0:T(4,128)}, u32[]{:S(2)}) copy-start(s32[3,32]{1,0:T(4,128)} %param.5) | copy-start | bytes 1156
  0.7 16.6 %copy-start.3 = (s32[64]{0:T(128)S(1)}, s32[64]{0:T(128)}, u32[]{:S(2)}) copy-start(s32[64]{0:T(128)} %param.4) | copy-start | bytes 772
  2.2 19.7 %collective-permute-start = (f32[6,64,1024]{2,1,0:T(8,128)S(1)}, f32[6,64,1024]{2,1,0:T(8,128)S(1)}, u32[]{:S(2)}, u32[]{:S(2)}) collective-permute-start(f32[6,64,1024]{2,1,0:T(8,128)S(1)} %constant_dynamic-slice_fusion.4), channel_id=1, source_target_pairs={{0,4},{4,0},{8,12},{12,8},{16,20},{20,16},{24,28},{28,24},{1,5},{5... | collective-permute-start | bytes 4718600 | tf_op jit(solution)/shard_map/ppermute | solution.py:318
  5.0 15.5 %collective-permute-start.4 = (f32[6,2,8,1024]{3,2,1,0:T(8,128)}, f32[6,2,8,1024]{3,2,1,0:T(8,128)S(1)}, u32[]{:S(2)}, u32[]{:S(2)}) collective-permute-start(f32[6,2,8,1024]{3,2,1,0:T(8,128)} %slice.48), channel_id=1, source_target_pairs={{0,28},{4,8},{8,4},{12,16},{16,12},{20,24},{24,20},{28,0},{1,29},{... | collective-permute-start | bytes 1179656 | tf_op jit(solution)/shard_map/ppermute | solution.py:316
  10.5 40.2 %collective-permute-start.3 = (f32[3,48,1024]{2,1,0:T(8,128)}, f32[3,48,1024]{2,1,0:T(8,128)}, u32[]{:S(2)}, u32[]{:S(2)}) collective-permute-start(f32[3,48,1024]{2,1,0:T(8,128)} %constant_dynamic-slice_fusion.3), channel_id=1, source_target_pairs={{0,28},{4,8},{8,4},{12,16},{16,12},{20,24},{24,20},{28,0},{1,29},{... | collective-permute-start | bytes 1769480 | tf_op jit(solution)/shard_map/ppermute | solution.py:322
  12.3 45.0 %collective-permute-start.7 = (f32[2,48,1024]{2,1,0:T(8,128)}, f32[2,48,1024]{2,1,0:T(8,128)}, u32[]{:S(2)}, u32[]{:S(2)}) collective-permute-start(f32[2,48,1024]{2,1,0:T(8,128)} %constant_dynamic-slice_fusion.1), channel_id=1, source_target_pairs={{0,28},{4,8},{8,4},{12,16},{16,12},{20,24},{24,20},{28,0},{1,29},{... | collective-permute-start | bytes 1179656 | tf_op jit(solution)/shard_map/ppermute | solution.py:322
  16.6 46.3 %collective-permute-start.8 = (f32[1,48,1024]{2,1,0:T(8,128)}, f32[1,48,1024]{2,1,0:T(8,128)}, u32[]{:S(2)}, u32[]{:S(2)}) collective-permute-start(f32[1,48,1024]{2,1,0:T(8,128)} %constant_dynamic-slice_fusion), channel_id=1, source_target_pairs={{0,28},{4,8},{8,4},{12,16},{16,12},{20,24},{24,20},{28,0},{1,29},{... | collective-permute-start | bytes 589832 | tf_op jit(solution)/shard_map/ppermute | solution.py:322
  20.5 30.2 %copy-start = (f32[6,2,8,1024]{3,2,1,0:T(8,128)}, f32[6,2,8,1024]{3,2,1,0:T(8,128)S(1)}, u32[]{:S(2)}) copy-start(f32[6,2,8,1024]{3,2,1,0:T(8,128)S(1)} %collective-permute-done.4) | copy-start | bytes 1179652
  20.6 6.1 %collective-permute-start.5 = (f32[6,2,1024]{2,1,0:T(2,128)S(1)}, f32[6,2,1024]{2,1,0:T(2,128)S(1)}, u32[]{:S(2)}, u32[]{:S(2)}) collective-permute-start(f32[6,2,1024]{2,1,0:T(2,128)S(1)} %get-tuple-element.30), channel_id=1, source_target_pairs={{1,0},{2,1},{3,2},{5,4},{6,5},{7,6},{9,8},{10,9},{11,10},{13,12},{... | collective-permute-start | bytes 147464 | tf_op jit(solution)/shard_map/ppermute | solution.py:298
  21.9 15.4 %copy-start.1 = (f32[6,64,1024]{2,1,0:T(8,128)}, f32[6,64,1024]{2,1,0:T(8,128)S(1)}, u32[]{:S(2)}) copy-start(f32[6,64,1024]{2,1,0:T(8,128)S(1)} %collective-permute-done.a) | copy-start | bytes 4718596
  21.9 6.3 %collective-permute-start.6 = (f32[6,2,1024]{2,1,0:T(2,128)S(1)}, f32[6,2,1024]{2,1,0:T(2,128)S(1)}, u32[]{:S(2)}, u32[]{:S(2)}) collective-permute-start(f32[6,2,1024]{2,1,0:T(2,128)S(1)} %get-tuple-element.31), channel_id=1, source_target_pairs={{0,1},{1,2},{2,3},{4,5},{5,6},{6,7},{8,9},{9,10},{10,11},{12,13},{... | collective-permute-start | bytes 147464 | tf_op jit(solution)/shard_map/ppermute | solution.py:297
  26.7 7.4 %collective-permute-start.1 = (f32[22,2,1024]{2,1,0:T(2,128)S(1)}, f32[22,2,1024]{2,1,0:T(2,128)S(1)}, u32[]{:S(2)}, u32[]{:S(2)}) collective-permute-start(f32[22,2,1024]{2,1,0:T(2,128)S(1)} %pad_maximum_fusion.2), channel_id=1, source_target_pairs={{1,0},{2,1},{3,2},{5,4},{6,5},{7,6},{9,8},{10,9},{11,10},{13,12},{... | collective-permute-start | bytes 540680 | tf_op jit(solution)/shard_map/ppermute | solution.py:298
  28.2 7.4 %collective-permute-start.2 = (f32[22,2,1024]{2,1,0:T(2,128)S(1)}, f32[22,2,1024]{2,1,0:T(2,128)S(1)}, u32[]{:S(2)}, u32[]{:S(2)}) collective-permute-start(f32[22,2,1024]{2,1,0:T(2,128)S(1)} %pad_maximum_fusion.3), channel_id=1, source_target_pairs={{0,1},{1,2},{2,3},{4,5},{5,6},{6,7},{8,9},{9,10},{10,11},{12,13},{... | collective-permute-start | bytes 540680 | tf_op jit(solution)/shard_map/ppermute | solution.py:297

commit v3 on v2

--- a/solution.py
+++ b/solution.py
@@ -7,6 +7,7 @@
 from jax.experimental.pallas import tpu as pltpu
 from jax.sharding import PartitionSpec as P
 
+
 BW = 4
 BOX_F = 8
 BOX_R = 16
@@ -18,8 +19,9 @@
 REACH = BW + 2
 SPAN = 2 * BW + 1
 NEG = -1e30
+ZPAD = 6
 TOP = 8
-PIECES = ((0, 3), (3, 5), (5, 6))
+PIECES = ((0, 5), (5, 6))
 SCALE = 1.0 / (SPAN * 64.0)
 
 
@@ -46,6 +48,14 @@
     return sub, lane
 
 
+def is_even():
+    return lax.rem(lax.axis_index("omega"), 2) == 0
+
+
+def row_is_even():
+    return lax.rem(lax.axis_index("row"), 2) == 0
+
+
 def rows_of(t):
     return pl.ds(t * SUB, SUB)
 
@@ -57,11 +67,12 @@
     ref[i, j, pl.ds(TOP + (len(tiles) - 1) * SUB, SUB), :] = tiles[-1]
 
 
-def smooth_stage(flags, first, smooth, count, shift, rows, strips):
+def smooth_stage(first, smooth, count, shift, rows, strips):
     sub, lane = iotas()
     starts = [-1 + SUB * k for k in range(rows // SUB)] + [rows + 1 - SUB]
-    above = (sub == 0) & (flags[1] == 1)
-    below = (sub == SUB - 1) & (flags[2] == 1)
+    place = lax.axis_index("row")
+    above = (sub == 0) & (place == 0)
+    below = (sub == SUB - 1) & (place == lax.axis_size("row") - 1)
     zero = jnp.zeros((SUB, LANES), jnp.float32)
 
     def body(i, carry):
@@ -116,11 +127,14 @@
     lax.fori_loop(0, rows // SUB, body, 0)
 
 
-def box_sums(weight, sel, boxes, first, start):
+def box_sums(weight, sel, boxes, first, frames, start):
     count, rows, columns = weight.shape
     group = 2 if count % 2 == 0 else 1
     slots2 = sel.shape[1]
-    f0, r0 = boxes[0:1, :], boxes[1:2, :]
+    frame_base = lax.axis_index("omega") * frames
+    live = boxes[0:1, :] >= 0
+    f0 = jnp.where(live, boxes[0:1, :] - frame_base, -BOX_F - frames)
+    r0 = boxes[1:2, :] - lax.axis_index("row") * rows
     row = lax.broadcasted_iota(jnp.int32, (rows, slots2), 0) - r0
     row_pick = jnp.where((row >= 0) & (row < BOX_R), 1.0, 0.0)
     row_odd = row_pick * (2 * row - (BOX_R - 1)).astype(jnp.float32)
@@ -145,12 +159,76 @@
     return lax.fori_loop(0, count // group, body, start)
 
 
+def halo_tile(z1, z2, index, j):
+    sub, _ = iotas()
+    even = row_is_even()
+    shift1 = jnp.where(even, ZPAD, 0)
+    head = (sub < SUB // 2) == even
+    one = z1[j, pl.ds(2 * index + shift1, SUB), :]
+    two = z2[j, pl.ds(2 * index + ZPAD - shift1, SUB), :]
+    return jnp.where(head, one, two)
+
+
+def edge_kernel(x, b0, sems):
+    count, rows, _ = x.shape
+    start = jnp.where(is_even(), 0, count - REACH)
+    copies = [
+        pltpu.make_async_copy(x.at[pl.ds(start, REACH), pl.ds(row, SUB)], b0.at[:, pl.ds(to, SUB)], sems.at[k])
+        for k, (row, to) in enumerate(((0, 0), (rows - SUB, SUB)))
+    ]
+    for copy in copies:
+        copy.start()
+    for copy in copies:
+        copy.wait()
+
+
+def pack_kernel(x, near, *rest):
+    count, rows, _ = x.shape
+    *pieces, sems = rest
+    even = is_even()
+    copies = [pltpu.make_async_copy(x.at[pl.ds(jnp.where(even, count - REACH, 0), REACH)], near, sems.at[0])]
+    for k, (begin, end) in enumerate(PIECES):
+        start = jnp.where(even, begin, count - end)
+        source = x.at[pl.ds(start, end - begin), pl.ds(SUB, rows - 2 * SUB)]
+        copies.append(pltpu.make_async_copy(source, pieces[k], sems.at[k + 1]))
+    for copy in copies:
+        copy.start()
+    for copy in copies:
+        copy.wait()
+
+
+def rows_kernel(*refs):
+    *sources, z1, z2 = refs
+    _, _ = iotas()
+    even = row_is_even()
+    strips = z1.shape[0]
+    for j in range(strips):
+        at = pl.ds(j * LANES, LANES)
+        k = ZPAD
+        for z in (z1, z2):
+            z[j, 0:SUB, :] = jnp.zeros((SUB, LANES), jnp.float32)
+            z[j, pl.ds(z.shape[1] - SUB, SUB), :] = jnp.zeros((SUB, LANES), jnp.float32)
+        for source in sources:
+            rows = source.shape[1]
+            for i in range(source.shape[0]):
+                upper, lower = source[i, 0:2, at], source[i, rows - 2 : rows, at]
+                z1[j, k : k + 2, :] = jnp.where(even, lower, upper)
+                z2[j, k : k + 2, :] = jnp.where(even, upper, lower)
+                k += 2
+
+
 def early_kernel(
-    flags, x, a, h, level, sel, boxes, out, part, edge, sums, first, smooth, weight, sems, *, early
+    x, a, z1, z2, level, boxes, out, part, edge, sums, sel, first, smooth, weight, sems, *, early
 ):
     count, rows, columns = x.shape
     tiles, strips = rows // SUB, columns // LANES
-    even = flags[0] == 1
+    even = is_even()
+    slots = boxes.shape[1] // 2
+    step = lax.broadcasted_iota(jnp.int32, sel.shape, 0) - boxes[2:3, :]
+    odd = lax.broadcasted_iota(jnp.int32, sel.shape, 1) >= slots
+    value = jnp.where(odd, 2 * step - (BOX_C - 1), 1).astype(jnp.float32)
+    inside = (step >= 0) & (step < BOX_C) & (boxes[0:1, :] >= 0)
+    sel[...] = jnp.where(inside, value, 0.0).astype(jnp.bfloat16)
 
     def body(j, carry):
         at = pl.ds(pl.multiple_of(j * LANES, LANES), LANES)
@@ -160,10 +238,9 @@
                 return None
             if p < 0:
                 index = jnp.where(even, -1 - p, REACH + p)
-                where = count + index
-                return [a[index, rows_of(t), at] for t in range(tiles)] + [h[where, :, at]]
+                return [a[index, rows_of(t), at] for t in range(tiles)] + [halo_tile(z1, z2, count + index, j)]
             index = jnp.where(even, count - 1 - p, p)
-            return [x[index, rows_of(t), at] for t in range(tiles)] + [h[index, :, at]]
+            return [x[index, rows_of(t), at] for t in range(tiles)] + [halo_tile(z1, z2, index, j)]
 
         window = load(-REACH)
         for p in range(1 - REACH, SPAN - REACH):
@@ -191,7 +268,7 @@
         return carry
 
     lax.fori_loop(0, strips, body, 0)
-    smooth_stage(flags, first, smooth, early + 2, 0, rows, strips)
+    smooth_stage(first, smooth, early + 2, 0, rows, strips)
     copy_edge = pltpu.make_async_copy(smooth.at[pl.ds(early, 2)], edge, sems.at[0])
     copy_edge.start()
     weigh(lambda i: (smooth, i), level, weight, lambda i: jnp.where(even, early - i, i - 1), early, rows, strips)
@@ -199,14 +276,14 @@
     copy = pltpu.make_async_copy(weight, out.at[pl.ds(start, early)], sems.at[1])
     copy.start()
     zero = jnp.zeros((1, sel.shape[1]), jnp.float32)
-    result = box_sums(weight, sel, boxes, start, (zero,) * 3)
+    result = box_sums(weight, sel, boxes, start, count, (zero,) * 3)
     for i in range(3):
         sums[i : i + 1, :] = result[i]
     copy_edge.wait()
     copy.wait()
 
 
-def late_kernel(flags, part, edge, b, b0, h, level, sel, boxes, sums, _, out, *rest, count, piece):
+def late_kernel(part, edge, b, b0, z1, z2, level, sel, boxes, sums, _, out, *rest, count, piece):
     begin, end = piece
     late = end - begin
     final = end == REACH
@@ -216,7 +293,7 @@
         new_part, new_edge, new_sums, first, smooth, weight, sems = rest
     rows, columns = out.shape[1], out.shape[2]
     tiles, strips = rows // SUB, columns // LANES
-    even = flags[0] == 1
+    even = is_even()
     taps = frame_taps()
     early = count - REACH
 
@@ -229,7 +306,7 @@
             return (
                 [b0[where, rows_of(0), at]]
                 + [b[index, rows_of(t), at] for t in range(tiles - 2)]
-                + [b0[where, rows_of(1), at], h[where, :, at]]
+                + [b0[where, rows_of(1), at], halo_tile(z1, z2, where, j)]
             )
 
         fresh = {q: load(q) for q in range(begin, end)}
@@ -251,7 +328,7 @@
         return carry
 
     lax.fori_loop(0, strips, body, 0)
-    smooth_stage(flags, first, smooth, late, 0, rows, strips)
+    smooth_stage(first, smooth, late, 0, rows, strips)
     copies = []
     if not final:
         copies.append(pltpu.make_async_copy(smooth.at[pl.ds(late - 2, 2)], new_edge, sems.at[0]))
@@ -269,7 +346,7 @@
     copies.append(pltpu.make_async_copy(weight, out.at[pl.ds(place, late)], sems.at[1]))
     copies[-1].start()
     start = tuple(sums[i : i + 1, :] for i in range(3))
-    total, by_frame, by_row = box_sums(weight, sel, boxes, place, start)
+    total, by_frame, by_row = box_sums(weight, sel, boxes, place, count, start)
     if final:
         slots = stats.shape[1]
         cells = float(BOX_F * BOX_R * BOX_C)
@@ -292,79 +369,88 @@
     return pl.BlockSpec(memory_space=pltpu.VMEM)
 
 
-def halo_rows(lower, upper):
+def hbm():
+    return pl.BlockSpec(memory_space=pltpu.HBM)
+
+
+def row_exchange(sources, strips):
     column = lax.axis_size("row")
-    above = lax.ppermute(lower, "row", [(i, i + 1) for i in range(column - 1)])
-    below = lax.ppermute(upper, "row", [(i + 1, i) for i in range(column - 1)])
-    middle = jnp.zeros((below.shape[0], SUB - 4, below.shape[2]), jnp.float32)
-    return jnp.concatenate([below, middle, above], axis=1)
-
-
-def on_device(frames, thresholds, spot_boxes):
+    frames = sum(v.shape[0] for v in sources)
+    rows = shape(strips, 2 * frames + 2 * ZPAD, LANES)
+    z1, z2 = pl.pallas_call(
+        rows_kernel,
+        out_shape=(rows, rows),
+        in_specs=[vmem()] * len(sources),
+        out_specs=(vmem(), vmem()),
+        compiler_params=pltpu.CompilerParams(vmem_limit_bytes=1 << 20),
+    )(*sources)
+    pairs = [(i, i + 1) for i in range(0, column - 1, 2)]
+    others = [(i, i + 1) for i in range(1, column - 1, 2)]
+    both = lambda ps: ps + [(j, i) for i, j in ps]
+    return lax.ppermute(z1, "row", both(pairs)), lax.ppermute(z2, "row", both(others))
+
+
+def steps(frames, thresholds, spot_boxes):
     count, rows, columns = frames.shape
     slots = spot_boxes.shape[1]
     early = count - REACH
-    tiles, strips = rows // SUB, columns // LANES
+    strips = columns // LANES
     ring = lax.axis_size("omega")
-    place = lax.axis_index("omega")
-    even = place % 2 == 0
     partner = [(i, i ^ 1) for i in range(ring)]
     other = [(i, (i - 1) % ring if i % 2 == 0 else (i + 1) % ring) for i in range(ring)]
 
-    tiled = frames.reshape(count, tiles, SUB, columns)
-    far = lax.dynamic_slice_in_dim(tiled, jnp.where(even, 0, count - REACH), REACH, axis=0)
-    b0 = lax.ppermute(far[:, :: tiles - 1], "omega", other).reshape(REACH, 2 * SUB, columns)
-    near = lax.dynamic_slice_in_dim(frames, jnp.where(even, count - REACH, 0), REACH, axis=0)
+    in_hbm = pltpu.with_memory_space_constraint(frames, pltpu.HBM)
+    small = pltpu.CompilerParams(vmem_limit_bytes=1 << 20)
+    edges = pl.pallas_call(
+        edge_kernel,
+        out_shape=shape(REACH, 2 * SUB, columns),
+        in_specs=[hbm()],
+        out_specs=vmem(),
+        scratch_shapes=[pltpu.SemaphoreType.DMA((2,))],
+        compiler_params=small,
+        name="edge",
+    )(in_hbm)
+    b0 = lax.ppermute(edges, "omega", other)
+    near, *pieces = pl.pallas_call(
+        pack_kernel,
+        out_shape=(shape(REACH, rows, columns),)
+        + tuple(shape(end - begin, rows - 2 * SUB, columns) for begin, end in PIECES),
+        in_specs=[hbm()],
+        out_specs=(vmem(),) * (1 + len(PIECES)),
+        scratch_shapes=[pltpu.SemaphoreType.DMA((1 + len(PIECES),))],
+        compiler_params=small,
+        name="pack",
+    )(in_hbm)
     a = lax.ppermute(near, "omega", partner)
-    pieces = []
-    for begin, end in PIECES:
-        piece = lax.dynamic_slice_in_dim(frames, jnp.where(even, begin, count - end), end - begin, axis=0)
-        pieces.append(lax.ppermute(piece[:, SUB : rows - SUB], "omega", other))
-
-    own_lower, own_upper = frames[:, rows - 2 :], frames[:, :2]
-    a_lower, a_upper = a[:, rows - 2 :], a[:, :2]
-    h1 = halo_rows(jnp.concatenate([own_lower, a_lower]), jnp.concatenate([own_upper, a_upper]))
-    h2 = halo_rows(b0[:, 2 * SUB - 2 :], b0[:, :2])
-
-    row_place = lax.axis_index("row")
-    flags = jnp.stack([even, row_place == 0, row_place == lax.axis_size("row") - 1]).astype(jnp.int32)
+    pieces = [lax.ppermute(piece, "omega", other) for piece in pieces]
+    z1, z2 = row_exchange([frames, a], strips)
+    far1, far2 = row_exchange([b0], strips)
+
     level = jnp.broadcast_to((thresholds.astype(jnp.float32) / 64.0)[:, None], (rows, LANES))
-    live = spot_boxes[0] >= 0
-    f0 = jnp.where(live, spot_boxes[0] - place * count, -BOX_F - count)
-    r0 = spot_boxes[1] - row_place * rows
-    boxes = jnp.stack([jnp.concatenate([f0, f0]), jnp.concatenate([r0, r0])])
-    step = jnp.arange(columns)[:, None] - spot_boxes[2][None, :]
-    inside = (step >= 0) & (step < BOX_C) & live[None, :]
-    sel = jnp.where(
-        jnp.concatenate([inside, inside], axis=1),
-        jnp.concatenate([jnp.ones_like(step), 2 * step - (BOX_C - 1)], axis=1),
-        0,
-    ).astype(jnp.bfloat16)
-
-    smem = pl.BlockSpec(memory_space=pltpu.SMEM)
-    anywhere = pl.BlockSpec(memory_space=pl.ANY)
+    boxes = jnp.concatenate([spot_boxes, spot_boxes], axis=1)
+
     padded = rows + 2 * TOP
-    params = pltpu.CompilerParams(vmem_limit_bytes=56 << 20)
-    weight, part, edge, sums = pl.pallas_call(
+    weight, part, edge, sums, sel = pl.pallas_call(
         functools.partial(early_kernel, early=early),
         out_shape=(
             shape(count, rows, columns),
             shape(REACH, strips, rows + SUB, LANES),
             shape(2, strips, padded, LANES),
             shape(3, 2 * slots),
+            jax.ShapeDtypeStruct((columns, 2 * slots), jnp.bfloat16),
         ),
-        in_specs=[smem] + [vmem()] * 6,
-        out_specs=(anywhere, vmem(), anywhere, vmem()),
+        in_specs=[vmem()] * 6,
+        out_specs=(hbm(), vmem(), vmem(), vmem(), vmem()),
         scratch_shapes=[
             pltpu.VMEM((early + 2, strips, padded, LANES), jnp.float32),
             pltpu.VMEM((early + 2, strips, padded, LANES), jnp.float32),
             pltpu.VMEM((early, rows, columns), jnp.float32),
             pltpu.SemaphoreType.DMA((2,)),
         ],
-        compiler_params=params,
+        compiler_params=pltpu.CompilerParams(vmem_limit_bytes=14 << 20),
         cost_estimate=pl.CostEstimate(flops=40 * frames.size, bytes_accessed=16 << 20, transcendentals=0),
         name="early",
-    )(flags, frames, a, h1, level, sel, boxes)
+    )(frames, a, z1, z2, level, boxes)
     for (begin, end), piece in zip(PIECES, pieces):
         final = end == REACH
         late = end - begin
@@ -380,8 +466,8 @@
                     shape(3, 2 * slots),
                 )
             ),
-            in_specs=[smem] + [vmem()] * 9 + [anywhere],
-            out_specs=(anywhere,) + ((vmem(),) if final else (vmem(), anywhere, vmem())),
+            in_specs=[vmem()] * 10 + [hbm()],
+            out_specs=(hbm(),) + ((vmem(),) if final else (vmem(), vmem(), vmem())),
             input_output_aliases={10: 0},
             scratch_shapes=[
                 pltpu.VMEM((late, strips, padded, LANES), jnp.float32),
@@ -389,10 +475,9 @@
                 pltpu.VMEM((late, rows, columns), jnp.float32),
                 pltpu.SemaphoreType.DMA((2,)),
             ],
-            compiler_params=params,
+            compiler_params=pltpu.CompilerParams(vmem_limit_bytes=14 << 20),
             cost_estimate=pl.CostEstimate(flops=8 * late * rows * columns, bytes_accessed=4 << 20, transcendentals=0),
-            name=f"late_{begin}",
-        )(flags, part, edge, piece, b0, h2, level, sel, boxes, sums, weight)
+        )(part, edge, piece, b0, far1, far2, level, sel, boxes, sums, weight)
         if final:
             weight, stats = results
         else:
@@ -402,7 +487,7 @@
 
 def solution(mesh):
     return jax.shard_map(
-        on_device,
+        steps,
         mesh=mesh,
         in_specs=(P("omega", "row", None), P("row"), P(None, ("omega", "row"))),
         out_specs=(P("omega", "row", None), P(None, ("omega", "row"))),

time: 68 us -> 60.1 us (0.88)
  the two profiles are of different devices: /device:TPU:0 before, /device:TPU:11 now
where the time goes in v3:
time: 60.1 us; the launch traced here: 59.9 us
  waiting for transfers between devices  23.4 us (39%)
  Pallas kernels  21.6 us (36%)
  starting transfers between devices  14 us (23%)
  between operations  0.76 us (1%)
    ppermute x1, waiting for transfers between devices, steps(): b0 = lax.ppermute(edges, 'omega', other)  23.4 us
    pallas_call x1, Pallas kernels, steps(): pl.pallas_call(functools.partial(early_kernel, early=early), out_shape=(s...  10 us
    ppermute x2, starting transfers between devices, row_exchange(): lax.ppermute(z2, 'row', both(others))  8.64 us
    pallas_call x2, Pallas kernels, steps(): pl.pallas_call(functools.partial(late_kernel, count=count, piece=(begin,...  8.43 us
    ppermute x2, starting transfers between devices, steps(): pieces = [lax.ppermute(piece, 'omega', other) for piece in pieces]  2.65 us
    pallas_call x1, Pallas kernels, steps(): pl.pallas_call(pack_kernel, out_shape=(shape(REACH, rows, columns),) + tu...  1.89 us
    ppermute x1, starting transfers between devices, steps(): b0 = lax.ppermute(edges, 'omega', other)  1.53 us
  transfers between devices with their start and end apart: 8, of which 1 were waited for; matrix products, arithmetic and copies ran while one was open for 0% of the time, Pallas kernels for 27%

profile of v3, /device:TPU:11, one launch (start us, length us, event | category | flops | bytes accessed | tf_op | source)
XLA Modules:
  0.0 59.9 jit_solution(2884644198607375846)
XLA Ops:
  0.6 0.0 copy-start
  0.6 1.9 %pack.1 = (f32[6,64,1024]{2,1,0:T(8,128)S(1)}, f32[5,48,1024]{2,1,0:T(8,128)S(1)}, f32[1,48,1024]{2,1,0:T(8,128)S(1)}) custom-call(f32[16,64,1024]{2,1,0:T(8,128)} %x.5), custom_call_target="tpu_custom_call" | custom-call | tf_op jit(solution)/shard_map/pack/pallas_call | solution.py:414
  2.5 0.7 %collective-permute-start = (f32[6,64,1024]{2,1,0:T(8,128)S(1)}, f32[6,64,1024]{2,1,0:T(8,128)S(1)}, u32[]{:S(2)}, u32[]{:S(2)}) collective-permute-start(f32[6,64,1024]{2,1,0:T(8,128)S(1)} %get-tuple-element.18), channel_id=1, source_target_pairs={{0,4},{4,0},{8,12},{12,8},{16,20},{20,16},{24,28},{28,24},{1,5},{5... | collective-permute-start | bytes 4718600 | tf_op jit(solution)/shard_map/ppermute | solution.py:424
  3.3 0.0 copy-start.2
  3.3 1.2 %collective-permute-start.3 = (f32[5,48,1024]{2,1,0:T(8,128)S(1)}, f32[5,48,1024]{2,1,0:T(8,128)S(1)}, u32[]{:S(2)}, u32[]{:S(2)}) collective-permute-start(f32[5,48,1024]{2,1,0:T(8,128)S(1)} %get-tuple-element.23), channel_id=1, source_target_pairs={{0,28},{4,8},{8,4},{12,16},{16,12},{20,24},{24,20},{28,0},{1,29},{... | collective-permute-start | bytes 2949128 | tf_op jit(solution)/shard_map/ppermute | solution.py:425
  4.5 1.0 %edge.1 = f32[6,16,1024]{2,1,0:T(8,128)S(1)} custom-call(f32[16,64,1024]{2,1,0:T(8,128)} %x.5), custom_call_target="tpu_custom_call" | custom-call | tf_op jit(solution)/shard_map/edge/pallas_call | solution.py:404
  5.5 0.0 copy-start.1
  5.5 1.5 %collective-permute-start.4 = (f32[6,16,1024]{2,1,0:T(8,128)S(1)}, f32[6,16,1024]{2,1,0:T(8,128)S(1)}, u32[]{:S(2)}, u32[]{:S(2)}) collective-permute-start(f32[6,16,1024]{2,1,0:T(8,128)S(1)} %edge.1), channel_id=1, source_target_pairs={{0,28},{4,8},{8,4},{12,16},{16,12},{20,24},{24,20},{28,0},{1,29},{... | collective-permute-start | bytes 1179656 | tf_op jit(solution)/shard_map/ppermute | solution.py:413
  7.0 0.0 collective-permute-done.refs_1_.a
  7.0 0.0 copy-done
  7.1 0.2 shard_map.50
  7.2 0.2 collective-permute-start.1
  7.5 1.5 %collective-permute-start.7 = (f32[1,48,1024]{2,1,0:T(8,128)S(1)}, f32[1,48,1024]{2,1,0:T(8,128)S(1)}, u32[]{:S(2)}, u32[]{:S(2)}) collective-permute-start(f32[1,48,1024]{2,1,0:T(8,128)S(1)} %get-tuple-element.31), channel_id=1, source_target_pairs={{0,28},{4,8},{8,4},{12,16},{16,12},{20,24},{24,20},{28,0},{1,29},{... | collective-permute-start | bytes 589832 | tf_op jit(solution)/shard_map/ppermute | solution.py:425
  8.9 4.3 %collective-permute-start.2 = (f32[8,56,128]{2,1,0:T(8,128)S(1)}, f32[8,56,128]{2,1,0:T(8,128)S(1)}, u32[]{:S(2)}, u32[]{:S(2)}) collective-permute-start(f32[8,56,128]{2,1,0:T(8,128)S(1)} %get-tuple-element.20), channel_id=1, source_target_pairs={{1,2},{2,1},{5,6},{6,5},{9,10},{10,9},{13,14},{14,13},{17,18},{18,... | collective-permute-start | bytes 688136 | tf_op jit(solution)/shard_map/ppermute | solution.py:390
  13.3 0.0 copy-done.2
  13.3 23.4 %collective-permute-done.4.refs_0_.b0 = f32[6,16,1024]{2,1,0:T(8,128)S(1)} collective-permute-done((f32[6,16,1024]{2,1,0:T(8,128)S(1)}, f32[6,16,1024]{2,1,0:T(8,128)S(1)}, u32[]{:S(2)}, u32[]{:S(2)}) %collective-permute-start.4) | collective-permute-done | bytes 393248 | tf_op jit(solution)/shard_map/ppermute | solution.py:413
  36.7 0.1 shard_map.51
  36.7 0.2 collective-permute-start.5
  36.9 0.0 collective-permute-done.1.z1
  37.0 4.3 %collective-permute-start.6 = (f32[8,24,128]{2,1,0:T(8,128)S(1)}, f32[8,24,128]{2,1,0:T(8,128)S(1)}, u32[]{:S(2)}, u32[]{:S(2)}) collective-permute-start(f32[8,24,128]{2,1,0:T(8,128)S(1)} %get-tuple-element.25), channel_id=1, source_target_pairs={{1,2},{2,1},{5,6},{6,5},{9,10},{10,9},{13,14},{14,13},{17,18},{18,... | collective-permute-start | bytes 294920 | tf_op jit(solution)/shard_map/ppermute | solution.py:390
  41.3 0.0 copy-done.1
  41.3 0.1 pad_add_fusion.boxes
  41.4 0.0 collective-permute-done.2.z2
  41.4 0.1 broadcast_in_dim.2.level
  41.4 10.0 %early.1 = (f32[16,64,1024]{2,1,0:T(8,128)}, f32[6,8,72,128]{3,2,1,0:T(8,128)S(1)}, f32[2,8,80,128]{3,2,1,0:T(8,128)S(1)}, f32[3,64]{1,0:T(4,128)S(1)}, bf16[1024,64]{1,0:T(8,128)(2,1)S(1)}) custom-call(f32[16,64,1024]{2,1,0:T(8,128)S(1)} %copy-done, f32[6,64,1024]{2,1,0:T(8,128)S(1)} %collective-permute-done.refs_1_.a, ...), custom_call_target="tpu_custom_call" | custom-call | flops 41943040 | bytes 16777216 | tf_op jit(solution)/shard_map/early/pallas_call | solution.py:433
  51.5 0.0 collective-permute-done.5.z1
  51.5 0.0 collective-permute-done.6.z2
  51.5 0.0 collective-permute-done.3.b
  51.5 5.1 %shard_map.52 = (f32[16,64,1024]{2,1,0:T(8,128)}, f32[1,8,72,128]{3,2,1,0:T(8,128)S(1)}, f32[2,8,80,128]{3,2,1,0:T(8,128)S(1)}, f32[3,64]{1,0:T(4,128)S(1)}) custom-call(f32[6,8,72,128]{3,2,1,0:T(8,128)S(1)} %get-tuple-element.21.part, f32[2,8,80,128]{3,2,1,0:T(8,128)S(1)} %get-tuple-element.22.edge, ...), custom_call_target="tpu_custom_call", output_to_operand_aliasing={{0}: (10, {})} | custom-call | flops 2621440 | bytes 4194304 | tf_op jit(solution)/shard_map/pallas_call | solution.py:457
  56.6 0.0 collective-permute-done.7.b
  56.6 3.4 %shard_map.53 = (f32[16,64,1024]{2,1,0:T(8,128)}, f32[4,32]{1,0:T(4,128)}) custom-call(f32[1,8,72,128]{3,2,1,0:T(8,128)S(1)} %get-tuple-element.29.part, f32[2,8,80,128]{3,2,1,0:T(8,128)S(1)} %get-tuple-element.30.edge, f32[1,48,1024]{2,1,0:T(8,128)S(1)} %collective-permute-done.7.b, ...), custom_call_target="tpu_custom_call", output_to_operand_aliasing={{0}: (10, {})} | custom-call | flops 524288 | bytes 4194304 | tf_op jit(solution)/shard_map/pallas_call | solution.py:457
  (1 shorter events, 0.0 us)
Async XLA Ops:
  0.6 6.4 %copy-start = (f32[16,64,1024]{2,1,0:T(8,128)S(1)}, f32[16,64,1024]{2,1,0:T(8,128)}, u32[]{:S(2)}) copy-start(f32[16,64,1024]{2,1,0:T(8,128)} %x.5) | copy-start | bytes 12582916
  2.5 4.5 %collective-permute-start = (f32[6,64,1024]{2,1,0:T(8,128)S(1)}, f32[6,64,1024]{2,1,0:T(8,128)S(1)}, u32[]{:S(2)}, u32[]{:S(2)}) collective-permute-start(f32[6,64,1024]{2,1,0:T(8,128)S(1)} %get-tuple-element.18), channel_id=1, source_target_pairs={{0,4},{4,0},{8,12},{12,8},{16,20},{20,16},{24,28},{28,24},{1,5},{5... | collective-permute-start | bytes 4718600 | tf_op jit(solution)/shard_map/ppermute | solution.py:424
  3.3 10.0 %copy-start.2 = (s32[64]{0:T(128)S(1)}, s32[64]{0:T(128)}, u32[]{:S(2)}) copy-start(s32[64]{0:T(128)} %param.4) | copy-start | bytes 772
  3.3 48.2 %collective-permute-start.3 = (f32[5,48,1024]{2,1,0:T(8,128)S(1)}, f32[5,48,1024]{2,1,0:T(8,128)S(1)}, u32[]{:S(2)}, u32[]{:S(2)}) collective-permute-start(f32[5,48,1024]{2,1,0:T(8,128)S(1)} %get-tuple-element.23), channel_id=1, source_target_pairs={{0,28},{4,8},{8,4},{12,16},{16,12},{20,24},{24,20},{28,0},{1,29},{... | collective-permute-start | bytes 2949128 | tf_op jit(solution)/shard_map/ppermute | solution.py:425
  5.5 35.8 %copy-start.1 = (s32[3,32]{1,0:T(4,128)S(1)}, s32[3,32]{1,0:T(4,128)}, u32[]{:S(2)}) copy-start(s32[3,32]{1,0:T(4,128)} %param.5) | copy-start | bytes 1156
  5.5 31.1 %collective-permute-start.4 = (f32[6,16,1024]{2,1,0:T(8,128)S(1)}, f32[6,16,1024]{2,1,0:T(8,128)S(1)}, u32[]{:S(2)}, u32[]{:S(2)}) collective-permute-start(f32[6,16,1024]{2,1,0:T(8,128)S(1)} %edge.1), channel_id=1, source_target_pairs={{0,28},{4,8},{8,4},{12,16},{16,12},{20,24},{24,20},{28,0},{1,29},{... | collective-permute-start | bytes 1179656 | tf_op jit(solution)/shard_map/ppermute | solution.py:413
  7.2 29.7 %collective-permute-start.1 = (f32[8,56,128]{2,1,0:T(8,128)S(1)}, f32[8,56,128]{2,1,0:T(8,128)S(1)}, u32[]{:S(2)}, u32[]{:S(2)}) collective-permute-start(f32[8,56,128]{2,1,0:T(8,128)S(1)} %get-tuple-element.19), channel_id=1, source_target_pairs={{0,1},{2,3},{1,0},{3,2},{4,5},{6,7},{5,4},{7,6},{8,9},{10,11},{9,8... | collective-permute-start | bytes 688136 | tf_op jit(solution)/shard_map/ppermute | solution.py:390
  7.5 49.1 %collective-permute-start.7 = (f32[1,48,1024]{2,1,0:T(8,128)S(1)}, f32[1,48,1024]{2,1,0:T(8,128)S(1)}, u32[]{:S(2)}, u32[]{:S(2)}) collective-permute-start(f32[1,48,1024]{2,1,0:T(8,128)S(1)} %get-tuple-element.31), channel_id=1, source_target_pairs={{0,28},{4,8},{8,4},{12,16},{16,12},{20,24},{24,20},{28,0},{1,29},{... | collective-permute-start | bytes 589832 | tf_op jit(solution)/shard_map/ppermute | solution.py:425
  8.9 32.4 %collective-permute-start.2 = (f32[8,56,128]{2,1,0:T(8,128)S(1)}, f32[8,56,128]{2,1,0:T(8,128)S(1)}, u32[]{:S(2)}, u32[]{:S(2)}) collective-permute-start(f32[8,56,128]{2,1,0:T(8,128)S(1)} %get-tuple-element.20), channel_id=1, source_target_pairs={{1,2},{2,1},{5,6},{6,5},{9,10},{10,9},{13,14},{14,13},{17,18},{18,... | collective-permute-start | bytes 688136 | tf_op jit(solution)/shard_map/ppermute | solution.py:390
  36.7 14.8 %collective-permute-start.5 = (f32[8,24,128]{2,1,0:T(8,128)S(1)}, f32[8,24,128]{2,1,0:T(8,128)S(1)}, u32[]{:S(2)}, u32[]{:S(2)}) collective-permute-start(f32[8,24,128]{2,1,0:T(8,128)S(1)} %get-tuple-element.24), channel_id=1, source_target_pairs={{0,1},{2,3},{1,0},{3,2},{4,5},{6,7},{5,4},{7,6},{8,9},{10,11},{9,8... | collective-permute-start | bytes 294920 | tf_op jit(solution)/shard_map/ppermute | solution.py:390
  37.0 14.5 %collective-permute-start.6 = (f32[8,24,128]{2,1,0:T(8,128)S(1)}, f32[8,24,128]{2,1,0:T(8,128)S(1)}, u32[]{:S(2)}, u32[]{:S(2)}) collective-permute-start(f32[8,24,128]{2,1,0:T(8,128)S(1)} %get-tuple-element.25), channel_id=1, source_target_pairs={{1,2},{2,1},{5,6},{6,5},{9,10},{10,9},{13,14},{14,13},{17,18},{18,... | collective-permute-start | bytes 294920 | tf_op jit(solution)/shard_map/ppermute | solution.py:390

commit v4 on v3

--- a/solution.py
+++ b/solution.py
@@ -21,7 +21,7 @@
 NEG = -1e30
 ZPAD = 6
 TOP = 8
-PIECES = ((0, 5), (5, 6))
+PIECES = ((0, 4), (4, 5), (5, 6))
 SCALE = 1.0 / (SPAN * 64.0)
 
 
@@ -40,6 +40,11 @@
 def previous_column(strips, lane, edge):
     rolled = [edge] + [pltpu.roll(v, 1, 1) for v in strips]
     return [jnp.where(lane == 0, rolled[j], rolled[j + 1]) for j in range(len(strips))]
+
+
+def column_tops(strips, lane):
+    tops = [jnp.maximum(a, b) for a, b in zip(strips, next_column(strips, lane, strips[-1]))]
+    return [jnp.maximum(a, b) for a, b in zip(tops, previous_column(tops, lane, tops[0]))]
 
 
 def iotas():
@@ -95,36 +100,54 @@
     lax.fori_loop(0, count, body, 0)
 
 
-def weigh(smooth_of, level, weight, place, count, rows, strips):
+def row_tops(ref, i, base, strips):
+    loads = ([ref[i, j, pl.ds(base + e, SUB), :] for e in (-1, 0, 1)] for j in range(strips))
+    return [jnp.maximum(jnp.maximum(a, b), c) for a, b, c in loads]
+
+
+def weight_of(s, top, floor):
+    return jnp.exp((SHARP * SCALE) * (s - top)) * jnp.maximum(s * SCALE - floor, 0.0)
+
+
+def weigh(smooth_of, level, weight, place, count, rows, strips, tail=None):
     _, lane = iotas()
 
     def body(t, carry):
         base = t * SUB + TOP
         at = pl.ds(pl.multiple_of(t * SUB, SUB), SUB)
-
-        def row_tops(i):
-            ref, index = smooth_of(i)
-            loads = ([ref[index, j, pl.ds(base + e, SUB), :] for e in (-1, 0, 1)] for j in range(strips))
-            return [jnp.maximum(jnp.maximum(a, b), c) for a, b, c in loads]
-
-        here = row_tops(1)
-        before = [jnp.maximum(a, b) for a, b in zip(row_tops(0), here)]
+        tops_of = lambda i: row_tops(*smooth_of(i), base, strips)
+        here = tops_of(1)
+        before = [jnp.maximum(a, b) for a, b in zip(tops_of(0), here)]
         floor = level[at, :]
         for i in range(1, count + 1):
-            after = row_tops(i + 1)
+            after = tops_of(i + 1)
             pairs = [jnp.maximum(a, b) for a, b in zip(here, after)]
             highs = [jnp.maximum(a, b) for a, b in zip(before, pairs)]
             here, before = after, pairs
-            tops = [jnp.maximum(a, b) for a, b in zip(highs, next_column(highs, lane, highs[-1]))]
-            tops = [jnp.maximum(a, b) for a, b in zip(tops, previous_column(tops, lane, tops[0]))]
+            tops = column_tops(highs, lane)
             ref, index = smooth_of(i)
             for j in range(strips):
                 s = ref[index, j, pl.ds(base, SUB), :]
-                w = jnp.exp((SHARP * SCALE) * (s - tops[j])) * jnp.maximum(s * SCALE - floor, 0.0)
-                weight[place(i), at, pl.ds(j * LANES, LANES)] = w
+                weight[place(i), at, pl.ds(j * LANES, LANES)] = weight_of(s, tops[j], floor)
+        if tail is not None:
+            for j, v in enumerate(column_tops(before, lane)):
+                tail[j, at, :] = v
         return carry
 
     lax.fori_loop(0, rows // SUB, body, 0)
+
+
+def weigh_last(smooth, centre, tail, level, weight, rows, strips):
+    _, lane = iotas()
+    for t in range(rows // SUB):
+        base = t * SUB + TOP
+        at = pl.ds(t * SUB, SUB)
+        tops = column_tops(row_tops(smooth, 0, base, strips), lane)
+        floor = level[at, :]
+        for j in range(strips):
+            s = centre[j, pl.ds(base, SUB), :]
+            top = jnp.maximum(tops[j], tail[j, at, :])
+            weight[0, at, pl.ds(j * LANES, LANES)] = weight_of(s, top, floor)
 
 
 def box_sums(weight, sel, boxes, first, frames, start):
@@ -166,7 +189,10 @@
     head = (sub < SUB // 2) == even
     one = z1[j, pl.ds(2 * index + shift1, SUB), :]
     two = z2[j, pl.ds(2 * index + ZPAD - shift1, SUB), :]
-    return jnp.where(head, one, two)
+    place = lax.axis_index("row")
+    inside = (sub >= SUB // 2) | (place != lax.axis_size("row") - 1)
+    inside = inside & ((sub < SUB // 2) | (place != 0))
+    return jnp.where(inside, jnp.where(head, one, two), 0.0)
 
 
 def edge_kernel(x, b0, sems):
@@ -283,12 +309,19 @@
     copy.wait()
 
 
-def late_kernel(part, edge, b, b0, z1, z2, level, sel, boxes, sums, _, out, *rest, count, piece):
+def late_kernel(part, b, b0, z1, z2, level, sel, boxes, sums, *rest, count, piece):
     begin, end = piece
     late = end - begin
     final = end == REACH
+    ahead = end == REACH - 1
+    if final:
+        edge, tail, _, out, *rest = rest
+    else:
+        edge, _, out, *rest = rest
     if final:
         stats, first, smooth, weight, sems = rest
+    elif ahead:
+        new_part, new_edge, tail, new_sums, first, smooth, weight, sems = rest
     else:
         new_part, new_edge, new_sums, first, smooth, weight, sems = rest
     rows, columns = out.shape[1], out.shape[2]
@@ -330,18 +363,24 @@
     lax.fori_loop(0, strips, body, 0)
     smooth_stage(first, smooth, late, 0, rows, strips)
     copies = []
-    if not final:
-        copies.append(pltpu.make_async_copy(smooth.at[pl.ds(late - 2, 2)], new_edge, sems.at[0]))
+    if final:
+        weigh_last(smooth, edge, tail, level, weight, rows, strips)
+    else:
+        if ahead:
+            copies.append(pltpu.make_async_copy(smooth.at[late - 1], new_edge, sems.at[0]))
+        else:
+            copies.append(pltpu.make_async_copy(smooth.at[pl.ds(late - 2, 2)], new_edge, sems.at[0]))
         copies[0].start()
-    weigh(
-        lambda i: (edge, i) if i < 2 else (smooth, i - 2),
-        level,
-        weight,
-        lambda i: jnp.where(even, late - i, i - 1),
-        late,
-        rows,
-        strips,
-    )
+        weigh(
+            lambda i: (edge, i) if i < 2 else (smooth, i - 2),
+            level,
+            weight,
+            lambda i: jnp.where(even, late - i, i - 1),
+            late,
+            rows,
+            strips,
+            tail if ahead else None,
+        )
     place = jnp.where(even, REACH - end, early + begin)
     copies.append(pltpu.make_async_copy(weight, out.at[pl.ds(place, late)], sems.at[1]))
     copies[-1].start()
@@ -374,7 +413,7 @@
 
 
 def row_exchange(sources, strips):
-    column = lax.axis_size("row")
+    ring, column = lax.axis_size("omega"), lax.axis_size("row")
     frames = sum(v.shape[0] for v in sources)
     rows = shape(strips, 2 * frames + 2 * ZPAD, LANES)
     z1, z2 = pl.pallas_call(
@@ -384,10 +423,18 @@
         out_specs=(vmem(), vmem()),
         compiler_params=pltpu.CompilerParams(vmem_limit_bytes=1 << 20),
     )(*sources)
-    pairs = [(i, i + 1) for i in range(0, column - 1, 2)]
-    others = [(i, i + 1) for i in range(1, column - 1, 2)]
-    both = lambda ps: ps + [(j, i) for i, j in ps]
-    return lax.ppermute(z1, "row", both(pairs)), lax.ppermute(z2, "row", both(others))
+    both = ("omega", "row")
+    return (lax.ppermute(z1, both, row_pairs(ring, column, 0)), lax.ppermute(z2, both, row_pairs(ring, column, 1)))
+
+
+def row_pairs(ring, column, start):
+    pairs = []
+    for i in range(ring):
+        for r in range(column):
+            mate = r + 1 if (r - start) % 2 == 0 else r - 1
+            there = (i, mate) if 0 <= mate < column else (i ^ 1, r)
+            pairs.append((i * column + r, there[0] * column + there[1]))
+    return pairs
 
 
 def steps(frames, thresholds, spot_boxes):
@@ -451,24 +498,21 @@
         cost_estimate=pl.CostEstimate(flops=40 * frames.size, bytes_accessed=16 << 20, transcendentals=0),
         name="early",
     )(frames, a, z1, z2, level, boxes)
+    edge = [edge]
     for (begin, end), piece in zip(PIECES, pieces):
         final = end == REACH
+        ahead = end == REACH - 1
         late = end - begin
-        results = pl.pallas_call(
+        handed = (shape(4, slots),)
+        if not final:
+            edges = (shape(strips, padded, LANES), shape(strips, rows, LANES)) if ahead else (shape(2, strips, padded, LANES),)
+            handed = (shape(REACH - end, strips, rows + SUB, LANES), *edges, shape(3, 2 * slots))
+        weight, *rest = pl.pallas_call(
             functools.partial(late_kernel, count=count, piece=(begin, end)),
-            out_shape=(shape(count, rows, columns),)
-            + (
-                (shape(4, slots),)
-                if final
-                else (
-                    shape(REACH - end, strips, rows + SUB, LANES),
-                    shape(2, strips, padded, LANES),
-                    shape(3, 2 * slots),
-                )
-            ),
-            in_specs=[vmem()] * 10 + [hbm()],
-            out_specs=(hbm(),) + ((vmem(),) if final else (vmem(), vmem(), vmem())),
-            input_output_aliases={10: 0},
+            out_shape=(shape(count, rows, columns), *handed),
+            in_specs=[vmem()] * (9 + len(edge)) + [hbm()],
+            out_specs=(hbm(),) + (vmem(),) * len(handed),
+            input_output_aliases={9 + len(edge): 0},
             scratch_shapes=[
                 pltpu.VMEM((late, strips, padded, LANES), jnp.float32),
                 pltpu.VMEM((late, strips, padded, LANES), jnp.float32),
@@ -477,11 +521,11 @@
             ],
             compiler_params=pltpu.CompilerParams(vmem_limit_bytes=14 << 20),
             cost_estimate=pl.CostEstimate(flops=8 * late * rows * columns, bytes_accessed=4 << 20, transcendentals=0),
-        )(part, edge, piece, b0, far1, far2, level, sel, boxes, sums, weight)
+        )(part, piece, b0, far1, far2, level, sel, boxes, sums, *edge, weight)
         if final:
-            weight, stats = results
+            (stats,) = rest
         else:
-            weight, part, edge, sums = results
+            part, *edge, sums = rest
     return weight, stats
 
 

time: 60.1 us -> 57.3 us (0.953)
  the two profiles are of different devices: /device:TPU:11 before, /device:TPU:0 now
where the time goes in v4:
time: 57.3 us; the launch traced here: 57 us
  Pallas kernels  22.4 us (39%)
  waiting for transfers between devices  21.1 us (37%)
  starting transfers between devices  12.6 us (22%)
  between operations  0.77 us (1%)
    ppermute x1, waiting for transfers between devices, steps(): b0 = lax.ppermute(edges, 'omega', other)  21 us
    pallas_call x1, Pallas kernels, steps(): pl.pallas_call(functools.partial(early_kernel, early=early), out_shape=(s...  10 us
    pallas_call x3, Pallas kernels, steps(): pl.pallas_call(functools.partial(late_kernel, count=count, piece=(begin,...  9.21 us
    ppermute x3, starting transfers between devices, steps(): pieces = [lax.ppermute(piece, 'omega', other) for piece in pieces]  8.54 us
    ppermute x2, starting transfers between devices, row_exchange(): lax.ppermute(z1, both, row_pairs(ring, column, 0))  3.42 us
    pallas_call x1, Pallas kernels, steps(): pl.pallas_call(pack_kernel, out_shape=(shape(REACH, rows, columns),) + tu...  1.9 us
  transfers between devices with their start and end apart: 9, of which 1 were waited for; matrix products, arithmetic and copies ran while one was open for 0% of the time, Pallas kernels for 32%

profile of v4, /device:TPU:0, one launch (start us, length us, event | category | flops | bytes accessed | tf_op | source)
XLA Modules:
  0.0 57.0 jit_solution(3320374339852773211)
XLA Ops:
  0.6 0.0 copy-start
  0.6 1.9 %pack.1 = (f32[6,64,1024]{2,1,0:T(8,128)S(1)}, f32[4,48,1024]{2,1,0:T(8,128)S(1)}, f32[1,48,1024]{2,1,0:T(8,128)S(1)}, f32[1,48,1024]{2,1,0:T(8,128)S(1)}) custom-call(f32[16,64,1024]{2,1,0:T(8,128)} %x.5), custom_call_target="tpu_custom_call" | custom-call | tf_op jit(solution)/shard_map/pack/pallas_call | solution.py:461
  2.5 0.6 collective-permute-start
  3.1 0.0 copy-start.2
  3.1 3.5 %collective-permute-start.3 = (f32[4,48,1024]{2,1,0:T(8,128)S(1)}, f32[4,48,1024]{2,1,0:T(8,128)S(1)}, u32[]{:S(2)}, u32[]{:S(2)}) collective-permute-start(f32[4,48,1024]{2,1,0:T(8,128)S(1)} %get-tuple-element.28), channel_id=1, source_target_pairs={{0,28},{4,8},{8,4},{12,16},{16,12},{20,24},{24,20},{28,0},{1,29},{... | collective-permute-start | bytes 2359304 | tf_op jit(solution)/shard_map/ppermute | solution.py:472
  6.7 1.0 %edge.1 = f32[6,16,1024]{2,1,0:T(8,128)S(1)} custom-call(f32[16,64,1024]{2,1,0:T(8,128)} %x.5), custom_call_target="tpu_custom_call" | custom-call | tf_op jit(solution)/shard_map/edge/pallas_call | solution.py:451
  7.7 0.0 copy-start.1
  7.7 0.1 collective-permute-start.4
  7.8 0.0 collective-permute-done.refs_1_.a
  7.8 0.0 copy-done
  7.8 0.2 shard_map.50
  8.0 1.8 %collective-permute-start.1 = (f32[8,56,128]{2,1,0:T(8,128)S(1)}, f32[8,56,128]{2,1,0:T(8,128)S(1)}, u32[]{:S(2)}, u32[]{:S(2)}) collective-permute-start(f32[8,56,128]{2,1,0:T(8,128)S(1)} %get-tuple-element.25), channel_id=1, source_target_pairs={{0,1},{1,0},{2,3},{3,2},{4,5},{5,4},{6,7},{7,6},{8,9},{9,8},{10,11... | collective-permute-start | bytes 688136 | tf_op jit(solution)/shard_map/ppermute | solution.py:427
  9.8 0.0 collective-permute-start.2
  9.8 2.2 %collective-permute-start.7 = (f32[1,48,1024]{2,1,0:T(8,128)S(1)}, f32[1,48,1024]{2,1,0:T(8,128)S(1)}, u32[]{:S(2)}, u32[]{:S(2)}) collective-permute-start(f32[1,48,1024]{2,1,0:T(8,128)S(1)} %get-tuple-element.36), channel_id=1, source_target_pairs={{0,28},{4,8},{8,4},{12,16},{16,12},{20,24},{24,20},{28,0},{1,29},{... | collective-permute-start | bytes 589832 | tf_op jit(solution)/shard_map/ppermute | solution.py:472
  12.0 21.0 %collective-permute-done.4.refs_0_.b0 = f32[6,16,1024]{2,1,0:T(8,128)S(1)} collective-permute-done((f32[6,16,1024]{2,1,0:T(8,128)S(1)}, f32[6,16,1024]{2,1,0:T(8,128)S(1)}, u32[]{:S(2)}, u32[]{:S(2)}) %collective-permute-start.4) | collective-permute-done | bytes 393248 | tf_op jit(solution)/shard_map/ppermute | solution.py:460
  33.0 2.8 %collective-permute-start.8 = (f32[1,48,1024]{2,1,0:T(8,128)S(1)}, f32[1,48,1024]{2,1,0:T(8,128)S(1)}, u32[]{:S(2)}, u32[]{:S(2)}) collective-permute-start(f32[1,48,1024]{2,1,0:T(8,128)S(1)} %get-tuple-element.41), channel_id=1, source_target_pairs={{0,28},{4,8},{8,4},{12,16},{16,12},{20,24},{24,20},{28,0},{1,29},{... | collective-permute-start | bytes 589832 | tf_op jit(solution)/shard_map/ppermute | solution.py:472
  35.8 0.0 copy-done.2
  35.8 0.1 shard_map.51
  35.9 0.0 collective-permute-done.1.z1
  35.9 1.6 %collective-permute-start.5 = (f32[8,24,128]{2,1,0:T(8,128)S(1)}, f32[8,24,128]{2,1,0:T(8,128)S(1)}, u32[]{:S(2)}, u32[]{:S(2)}) collective-permute-start(f32[8,24,128]{2,1,0:T(8,128)S(1)} %get-tuple-element.29), channel_id=1, source_target_pairs={{0,1},{1,0},{2,3},{3,2},{4,5},{5,4},{6,7},{7,6},{8,9},{9,8},{10,11... | collective-permute-start | bytes 294920 | tf_op jit(solution)/shard_map/ppermute | solution.py:427
  37.5 0.0 collective-permute-done.2.z2
  37.5 0.0 collective-permute-start.6
  37.5 0.0 copy-done.1
  37.5 0.1 pad_add_fusion.boxes
  37.6 0.1 broadcast_in_dim.2.level
  37.7 10.0 %early.1 = (f32[16,64,1024]{2,1,0:T(8,128)}, f32[6,8,72,128]{3,2,1,0:T(8,128)S(1)}, f32[2,8,80,128]{3,2,1,0:T(8,128)S(1)}, f32[3,64]{1,0:T(4,128)S(1)}, bf16[1024,64]{1,0:T(8,128)(2,1)S(1)}) custom-call(f32[16,64,1024]{2,1,0:T(8,128)S(1)} %copy-done, f32[6,64,1024]{2,1,0:T(8,128)S(1)} %collective-permute-done.refs_1_.a, ...), custom_call_target="tpu_custom_call" | custom-call | flops 41943040 | bytes 16777216 | tf_op jit(solution)/shard_map/early/pallas_call | solution.py:480
  47.7 0.0 collective-permute-done.5.z1
  47.7 0.0 collective-permute-done.6.z2
  47.8 0.0 collective-permute-done.3.b
  47.8 4.4 %shard_map.52 = (f32[16,64,1024]{2,1,0:T(8,128)}, f32[2,8,72,128]{3,2,1,0:T(8,128)S(1)}, f32[2,8,80,128]{3,2,1,0:T(8,128)S(1)}, f32[3,64]{1,0:T(4,128)S(1)}) custom-call(f32[6,8,72,128]{3,2,1,0:T(8,128)S(1)} %get-tuple-element.27.part, f32[4,48,1024]{2,1,0:T(8,128)S(1)} %collective-permute-done.3.b, ...), custom_call_target="tpu_custom_call", output_to_operand_aliasing={{0}: (10, {})} | custom-call | flops 2097152 | bytes 4194304 | tf_op jit(solution)/shard_map/pallas_call | solution.py:510
  52.2 0.0 collective-permute-done.7.b
  52.2 2.7 %shard_map.53 = (f32[16,64,1024]{2,1,0:T(8,128)}, f32[1,8,72,128]{3,2,1,0:T(8,128)S(1)}, f32[8,80,128]{2,1,0:T(8,128)S(1)}, f32[8,64,128]{2,1,0:T(8,128)S(1)}, f32[3,64]{1,0:T(4,128)S(1)}) custom-call(f32[2,8,72,128]{3,2,1,0:T(8,128)S(1)} %get-tuple-element.35.part, f32[1,48,1024]{2,1,0:T(8,128)S(1)} %collective-permute-done.7.b, ...), custom_call_target="tpu_custom_call", output_to_operand_aliasing={{0}: (10, {})} | custom-call | flops 524288 | bytes 4194304 | tf_op jit(solution)/shard_map/pallas_call | solution.py:510
  54.9 0.0 collective-permute-done.8.b
  54.9 2.1 %shard_map.54 = (f32[16,64,1024]{2,1,0:T(8,128)}, f32[4,32]{1,0:T(4,128)}) custom-call(f32[1,8,72,128]{3,2,1,0:T(8,128)S(1)} %get-tuple-element.40.part, f32[1,48,1024]{2,1,0:T(8,128)S(1)} %collective-permute-done.8.b, f32[6,16,1024]{2,1,0:T(8,128)S(1)} %collective-permute-done.4.refs_0_.b0, ...), custom_call_target="tpu_custom_call", output_to_operand_aliasing={{0}: (11, {})} | custom-call | flops 524288 | bytes 4194304 | tf_op jit(solution)/shard_map/pallas_call | solution.py:510
  (1 shorter events, 0.0 us)
Async XLA Ops:
  0.6 7.2 %copy-start = (f32[16,64,1024]{2,1,0:T(8,128)S(1)}, f32[16,64,1024]{2,1,0:T(8,128)}, u32[]{:S(2)}) copy-start(f32[16,64,1024]{2,1,0:T(8,128)} %x.5) | copy-start | bytes 12582916
  2.5 5.2 %collective-permute-start = (f32[6,64,1024]{2,1,0:T(8,128)S(1)}, f32[6,64,1024]{2,1,0:T(8,128)S(1)}, u32[]{:S(2)}, u32[]{:S(2)}) collective-permute-start(f32[6,64,1024]{2,1,0:T(8,128)S(1)} %get-tuple-element.24), channel_id=1, source_target_pairs={{0,4},{4,0},{8,12},{12,8},{16,20},{20,16},{24,28},{28,24},{1,5},{5... | collective-permute-start | bytes 4718600 | tf_op jit(solution)/shard_map/ppermute | solution.py:471
  3.1 32.7 %copy-start.2 = (s32[64]{0:T(128)S(1)}, s32[64]{0:T(128)}, u32[]{:S(2)}) copy-start(s32[64]{0:T(128)} %param.4) | copy-start | bytes 772
  3.1 44.6 %collective-permute-start.3 = (f32[4,48,1024]{2,1,0:T(8,128)S(1)}, f32[4,48,1024]{2,1,0:T(8,128)S(1)}, u32[]{:S(2)}, u32[]{:S(2)}) collective-permute-start(f32[4,48,1024]{2,1,0:T(8,128)S(1)} %get-tuple-element.28), channel_id=1, source_target_pairs={{0,28},{4,8},{8,4},{12,16},{16,12},{20,24},{24,20},{28,0},{1,29},{... | collective-permute-start | bytes 2359304 | tf_op jit(solution)/shard_map/ppermute | solution.py:472
  7.7 29.8 %copy-start.1 = (s32[3,32]{1,0:T(4,128)S(1)}, s32[3,32]{1,0:T(4,128)}, u32[]{:S(2)}) copy-start(s32[3,32]{1,0:T(4,128)} %param.5) | copy-start | bytes 1156
  7.7 25.3 %collective-permute-start.4 = (f32[6,16,1024]{2,1,0:T(8,128)S(1)}, f32[6,16,1024]{2,1,0:T(8,128)S(1)}, u32[]{:S(2)}, u32[]{:S(2)}) collective-permute-start(f32[6,16,1024]{2,1,0:T(8,128)S(1)} %edge.1), channel_id=1, source_target_pairs={{0,28},{4,8},{8,4},{12,16},{16,12},{20,24},{24,20},{28,0},{1,29},{... | collective-permute-start | bytes 1179656 | tf_op jit(solution)/shard_map/ppermute | solution.py:460
  8.0 27.9 %collective-permute-start.1 = (f32[8,56,128]{2,1,0:T(8,128)S(1)}, f32[8,56,128]{2,1,0:T(8,128)S(1)}, u32[]{:S(2)}, u32[]{:S(2)}) collective-permute-start(f32[8,56,128]{2,1,0:T(8,128)S(1)} %get-tuple-element.25), channel_id=1, source_target_pairs={{0,1},{1,0},{2,3},{3,2},{4,5},{5,4},{6,7},{7,6},{8,9},{9,8},{10,11... | collective-permute-start | bytes 688136 | tf_op jit(solution)/shard_map/ppermute | solution.py:427
  9.8 27.8 %collective-permute-start.2 = (f32[8,56,128]{2,1,0:T(8,128)S(1)}, f32[8,56,128]{2,1,0:T(8,128)S(1)}, u32[]{:S(2)}, u32[]{:S(2)}) collective-permute-start(f32[8,56,128]{2,1,0:T(8,128)S(1)} %get-tuple-element.26), channel_id=1, source_target_pairs={{0,4},{1,2},{2,1},{3,7},{4,0},{5,6},{6,5},{7,3},{8,12},{9,10},{10,... | collective-permute-start | bytes 688136 | tf_op jit(solution)/shard_map/ppermute | solution.py:427
  9.8 42.4 %collective-permute-start.7 = (f32[1,48,1024]{2,1,0:T(8,128)S(1)}, f32[1,48,1024]{2,1,0:T(8,128)S(1)}, u32[]{:S(2)}, u32[]{:S(2)}) collective-permute-start(f32[1,48,1024]{2,1,0:T(8,128)S(1)} %get-tuple-element.36), channel_id=1, source_target_pairs={{0,28},{4,8},{8,4},{12,16},{16,12},{20,24},{24,20},{28,0},{1,29},{... | collective-permute-start | bytes 589832 | tf_op jit(solution)/shard_map/ppermute | solution.py:472
  33.0 21.9 %collective-permute-start.8 = (f32[1,48,1024]{2,1,0:T(8,128)S(1)}, f32[1,48,1024]{2,1,0:T(8,128)S(1)}, u32[]{:S(2)}, u32[]{:S(2)}) collective-permute-start(f32[1,48,1024]{2,1,0:T(8,128)S(1)} %get-tuple-element.41), channel_id=1, source_target_pairs={{0,28},{4,8},{8,4},{12,16},{16,12},{20,24},{24,20},{28,0},{1,29},{... | collective-permute-start | bytes 589832 | tf_op jit(solution)/shard_map/ppermute | solution.py:472
  35.9 11.8 %collective-permute-start.5 = (f32[8,24,128]{2,1,0:T(8,128)S(1)}, f32[8,24,128]{2,1,0:T(8,128)S(1)}, u32[]{:S(2)}, u32[]{:S(2)}) collective-permute-start(f32[8,24,128]{2,1,0:T(8,128)S(1)} %get-tuple-element.29), channel_id=1, source_target_pairs={{0,1},{1,0},{2,3},{3,2},{4,5},{5,4},{6,7},{7,6},{8,9},{9,8},{10,11... | collective-permute-start | bytes 294920 | tf_op jit(solution)/shard_map/ppermute | solution.py:427
  37.5 10.2 %collective-permute-start.6 = (f32[8,24,128]{2,1,0:T(8,128)S(1)}, f32[8,24,128]{2,1,0:T(8,128)S(1)}, u32[]{:S(2)}, u32[]{:S(2)}) collective-permute-start(f32[8,24,128]{2,1,0:T(8,128)S(1)} %get-tuple-element.30), channel_id=1, source_target_pairs={{0,4},{1,2},{2,1},{3,7},{4,0},{5,6},{6,5},{7,3},{8,12},{9,10},{10,... | collective-permute-start | bytes 294920 | tf_op jit(solution)/shard_map/ppermute | solution.py:427

commit v5 on v4

--- a/solution.py
+++ b/solution.py
@@ -72,29 +72,33 @@
     ref[i, j, pl.ds(TOP + (len(tiles) - 1) * SUB, SUB), :] = tiles[-1]
 
 
+def window_starts(rows):
+    return [-1 + SUB * k for k in range(rows // SUB)] + [rows + 1 - SUB]
+
+
+def smooth_window(first, i, smooth, o, start, rows, strips):
+    sub, lane = iotas()
+    place = lax.axis_index("row")
+    zero = jnp.zeros((SUB, LANES), jnp.float32)
+    seconds = []
+    for j in range(strips):
+        a, b, c = (first[i, j, pl.ds(TOP + start + e, SUB), :] for e in (-1, 0, 1))
+        seconds.append((a + b) + (b + c))
+    pairs = [a + b for a, b in zip(seconds, next_column(seconds, lane, zero))]
+    sums = [a + b for a, b in zip(pairs, previous_column(pairs, lane, seconds[0]))]
+    for j in range(strips):
+        v = sums[j]
+        if start < 0:
+            v = jnp.where((sub == 0) & (place == 0), NEG, v)
+        if start + SUB > rows:
+            v = jnp.where((sub == SUB - 1) & (place == lax.axis_size("row") - 1), NEG, v)
+        smooth[o, j, pl.ds(TOP + start, SUB), :] = v
+
+
 def smooth_stage(first, smooth, count, shift, rows, strips):
-    sub, lane = iotas()
-    starts = [-1 + SUB * k for k in range(rows // SUB)] + [rows + 1 - SUB]
-    place = lax.axis_index("row")
-    above = (sub == 0) & (place == 0)
-    below = (sub == SUB - 1) & (place == lax.axis_size("row") - 1)
-    zero = jnp.zeros((SUB, LANES), jnp.float32)
-
     def body(i, carry):
-        for k, start in enumerate(starts):
-            seconds = []
-            for j in range(strips):
-                a, b, c = (first[i, j, pl.ds(TOP + start + e, SUB), :] for e in (-1, 0, 1))
-                seconds.append((a + b) + (b + c))
-            pairs = [a + b for a, b in zip(seconds, next_column(seconds, lane, zero))]
-            sums = [a + b for a, b in zip(pairs, previous_column(pairs, lane, seconds[0]))]
-            for j in range(strips):
-                v = sums[j]
-                if k == 0:
-                    v = jnp.where(above, NEG, v)
-                if k == len(starts) - 1:
-                    v = jnp.where(below, NEG, v)
-                smooth[i + shift, j, pl.ds(TOP + start, SUB), :] = v
+        for start in window_starts(rows):
+            smooth_window(first, i, smooth, i + shift, start, rows, strips)
         return carry
 
     lax.fori_loop(0, count, body, 0)
@@ -137,9 +141,13 @@
     lax.fori_loop(0, rows // SUB, body, 0)
 
 
-def weigh_last(smooth, centre, tail, level, weight, rows, strips):
+def weigh_last(first, smooth, centre, tail, level, weight, rows, strips):
     _, lane = iotas()
-    for t in range(rows // SUB):
+    for k, start in enumerate(window_starts(rows)):
+        smooth_window(first, 0, smooth, 0, start, rows, strips)
+        if k == 0:
+            continue
+        t = k - 1
         base = t * SUB + TOP
         at = pl.ds(t * SUB, SUB)
         tops = column_tops(row_tops(smooth, 0, base, strips), lane)
@@ -243,18 +251,21 @@
                 k += 2
 
 
-def early_kernel(
-    x, a, z1, z2, level, boxes, out, part, edge, sums, sel, first, smooth, weight, sems, *, early
-):
-    count, rows, columns = x.shape
-    tiles, strips = rows // SUB, columns // LANES
-    even = is_even()
+def table_kernel(boxes, sel):
     slots = boxes.shape[1] // 2
     step = lax.broadcasted_iota(jnp.int32, sel.shape, 0) - boxes[2:3, :]
     odd = lax.broadcasted_iota(jnp.int32, sel.shape, 1) >= slots
     value = jnp.where(odd, 2 * step - (BOX_C - 1), 1).astype(jnp.float32)
     inside = (step >= 0) & (step < BOX_C) & (boxes[0:1, :] >= 0)
     sel[...] = jnp.where(inside, value, 0.0).astype(jnp.bfloat16)
+
+
+def early_kernel(
+    x, a, z1, z2, level, sel, boxes, out, part, edge, sums, first, smooth, weight, sems, *, early
+):
+    count, rows, columns = x.shape
+    tiles, strips = rows // SUB, columns // LANES
+    even = is_even()
 
     def body(j, carry):
         at = pl.ds(pl.multiple_of(j * LANES, LANES), LANES)
@@ -319,7 +330,7 @@
     else:
         edge, _, out, *rest = rest
     if final:
-        stats, first, smooth, weight, sems = rest
+        stats, first, smooth, weight, sems, figures = rest
     elif ahead:
         new_part, new_edge, tail, new_sums, first, smooth, weight, sems = rest
     else:
@@ -331,7 +342,7 @@
     early = count - REACH
 
     def body(j, carry):
-        at = pl.ds(pl.multiple_of(j * LANES, LANES), LANES)
+        at = pl.ds(j * LANES if final else pl.multiple_of(j * LANES, LANES), LANES)
 
         def load(q):
             index = jnp.where(even, end - 1 - q, q - begin)
@@ -360,12 +371,16 @@
                     new_part[i - late, j, rows_of(t), :] = v
         return carry
 
-    lax.fori_loop(0, strips, body, 0)
-    smooth_stage(first, smooth, late, 0, rows, strips)
+    if final:
+        for j in range(strips):
+            body(j, 0)
+    else:
+        lax.fori_loop(0, strips, body, 0)
     copies = []
     if final:
-        weigh_last(smooth, edge, tail, level, weight, rows, strips)
+        weigh_last(first, smooth, edge, tail, level, weight, rows, strips)
     else:
+        smooth_stage(first, smooth, late, 0, rows, strips)
         if ahead:
             copies.append(pltpu.make_async_copy(smooth.at[late - 1], new_edge, sems.at[0]))
         else:
@@ -389,10 +404,12 @@
     if final:
         slots = stats.shape[1]
         cells = float(BOX_F * BOX_R * BOX_C)
-        stats[0:1, :] = total[:, :slots] / cells
-        stats[1:2, :] = by_frame[:, :slots] / (cells * (BOX_F - 1))
-        stats[2:3, :] = by_row[:, :slots] / (cells * (BOX_R - 1))
-        stats[3:4, :] = total[:, slots:] / (cells * (BOX_C - 1))
+        figures[0:1, :] = total[:, :slots] / cells
+        figures[1:2, :] = by_frame[:, :slots] / (cells * (BOX_F - 1))
+        figures[2:3, :] = by_row[:, :slots] / (cells * (BOX_R - 1))
+        figures[3:4, :] = total[:, slots:] / (cells * (BOX_C - 1))
+        copies.append(pltpu.make_async_copy(figures, stats, sems.at[0]))
+        copies[-1].start()
     else:
         for i, v in enumerate((total, by_frame, by_row)):
             new_sums[i : i + 1, :] = v
@@ -477,17 +494,24 @@
     boxes = jnp.concatenate([spot_boxes, spot_boxes], axis=1)
 
     padded = rows + 2 * TOP
-    weight, part, edge, sums, sel = pl.pallas_call(
+    sel = pl.pallas_call(
+        table_kernel,
+        out_shape=jax.ShapeDtypeStruct((columns, 2 * slots), jnp.bfloat16),
+        in_specs=[vmem()],
+        out_specs=vmem(),
+        compiler_params=small,
+        name="table",
+    )(boxes)
+    weight, part, edge, sums = pl.pallas_call(
         functools.partial(early_kernel, early=early),
         out_shape=(
             shape(count, rows, columns),
             shape(REACH, strips, rows + SUB, LANES),
             shape(2, strips, padded, LANES),
             shape(3, 2 * slots),
-            jax.ShapeDtypeStruct((columns, 2 * slots), jnp.bfloat16),
         ),
-        in_specs=[vmem()] * 6,
-        out_specs=(hbm(), vmem(), vmem(), vmem(), vmem()),
+        in_specs=[vmem()] * 7,
+        out_specs=(hbm(), vmem(), vmem(), vmem()),
         scratch_shapes=[
             pltpu.VMEM((early + 2, strips, padded, LANES), jnp.float32),
             pltpu.VMEM((early + 2, strips, padded, LANES), jnp.float32),
@@ -497,7 +521,7 @@
         compiler_params=pltpu.CompilerParams(vmem_limit_bytes=14 << 20),
         cost_estimate=pl.CostEstimate(flops=40 * frames.size, bytes_accessed=16 << 20, transcendentals=0),
         name="early",
-    )(frames, a, z1, z2, level, boxes)
+    )(frames, a, z1, z2, level, sel, boxes)
     edge = [edge]
     for (begin, end), piece in zip(PIECES, pieces):
         final = end == REACH
@@ -511,14 +535,15 @@
             functools.partial(late_kernel, count=count, piece=(begin, end)),
             out_shape=(shape(count, rows, columns), *handed),
             in_specs=[vmem()] * (9 + len(edge)) + [hbm()],
-            out_specs=(hbm(),) + (vmem(),) * len(handed),
+            out_specs=(hbm(),) + (hbm() if final else vmem(),) * len(handed),
             input_output_aliases={9 + len(edge): 0},
             scratch_shapes=[
                 pltpu.VMEM((late, strips, padded, LANES), jnp.float32),
                 pltpu.VMEM((late, strips, padded, LANES), jnp.float32),
                 pltpu.VMEM((late, rows, columns), jnp.float32),
                 pltpu.SemaphoreType.DMA((2,)),
-            ],
+            ]
+            + ([pltpu.VMEM((4, slots), jnp.float32)] if final else []),
             compiler_params=pltpu.CompilerParams(vmem_limit_bytes=14 << 20),
             cost_estimate=pl.CostEstimate(flops=8 * late * rows * columns, bytes_accessed=4 << 20, transcendentals=0),
         )(part, piece, b0, far1, far2, level, sel, boxes, sums, *edge, weight)

time: 57.3 us -> 56.6 us (0.988)
  Pallas kernels: 22.4 us -> 21.7 us
    pallas_call x3, Pallas kernels: 9.21 us -> 8.51 us  [steps(): pl.pallas_call(functools.partial(late_kernel, count=count, piece=(begin,...]
  transfers between devices with their start and end apart: 9 -> 9, of which waited for: 1 -> 1; matrix products, arithmetic and copies ran while one was open for 0% -> 0% of each run, Pallas kernels for 32% -> 33%
where the time goes in v5:
time: 56.6 us; the launch traced here: 56.3 us
  Pallas kernels  21.7 us (38%)
  waiting for transfers between devices  21.1 us (37%)
  starting transfers between devices  12.6 us (22%)
  between operations  0.77 us (1%)
    ppermute x1, waiting for transfers between devices, steps(): b0 = lax.ppermute(edges, 'omega', other)  21 us
    pallas_call x1, Pallas kernels, steps(): pl.pallas_call(functools.partial(early_kernel, early=early), out_shape=(s...  9.84 us
    ppermute x3, starting transfers between devices, steps(): pieces = [lax.ppermute(piece, 'omega', other) for piece in pieces]  8.54 us
    pallas_call x3, Pallas kernels, steps(): pl.pallas_call(functools.partial(late_kernel, count=count, piece=(begin,...  8.51 us
    ppermute x2, starting transfers between devices, row_exchange(): lax.ppermute(z1, both, row_pairs(ring, column, 0))  3.42 us
    pallas_call x1, Pallas kernels, steps(): pl.pallas_call(pack_kernel, out_shape=(shape(REACH, rows, columns),) + tu...  1.9 us
  transfers between devices with their start and end apart: 9, of which 1 were waited for; matrix products, arithmetic and copies ran while one was open for 0% of the time, Pallas kernels for 33%

profile of v5, /device:TPU:0, one launch (start us, length us, event | category | flops | bytes accessed | tf_op | source)
XLA Modules:
  0.0 56.3 jit_solution(8056145865750863758)
XLA Ops:
  0.6 0.0 copy-start
  0.6 1.9 %pack.1 = (f32[6,64,1024]{2,1,0:T(8,128)S(1)}, f32[4,48,1024]{2,1,0:T(8,128)S(1)}, f32[1,48,1024]{2,1,0:T(8,128)S(1)}, f32[1,48,1024]{2,1,0:T(8,128)S(1)}) custom-call(f32[16,64,1024]{2,1,0:T(8,128)} %x.5), custom_call_target="tpu_custom_call" | custom-call | tf_op jit(solution)/shard_map/pack/pallas_call | solution.py:478
  2.5 0.6 collective-permute-start
  3.1 0.0 copy-start.2
  3.1 3.5 %collective-permute-start.3 = (f32[4,48,1024]{2,1,0:T(8,128)S(1)}, f32[4,48,1024]{2,1,0:T(8,128)S(1)}, u32[]{:S(2)}, u32[]{:S(2)}) collective-permute-start(f32[4,48,1024]{2,1,0:T(8,128)S(1)} %get-tuple-element.27), channel_id=1, source_target_pairs={{0,28},{4,8},{8,4},{12,16},{16,12},{20,24},{24,20},{28,0},{1,29},{... | collective-permute-start | bytes 2359304 | tf_op jit(solution)/shard_map/ppermute | solution.py:489
  6.7 1.0 %edge.1 = f32[6,16,1024]{2,1,0:T(8,128)S(1)} custom-call(f32[16,64,1024]{2,1,0:T(8,128)} %x.5), custom_call_target="tpu_custom_call" | custom-call | tf_op jit(solution)/shard_map/edge/pallas_call | solution.py:468
  7.7 0.0 copy-start.1
  7.7 0.1 collective-permute-start.4
  7.8 0.0 collective-permute-done.refs_1_.a
  7.8 0.0 copy-done
  7.8 0.2 shard_map.50
  8.0 1.8 %collective-permute-start.1 = (f32[8,56,128]{2,1,0:T(8,128)S(1)}, f32[8,56,128]{2,1,0:T(8,128)S(1)}, u32[]{:S(2)}, u32[]{:S(2)}) collective-permute-start(f32[8,56,128]{2,1,0:T(8,128)S(1)} %get-tuple-element.24), channel_id=1, source_target_pairs={{0,1},{1,0},{2,3},{3,2},{4,5},{5,4},{6,7},{7,6},{8,9},{9,8},{10,11... | collective-permute-start | bytes 688136 | tf_op jit(solution)/shard_map/ppermute | solution.py:444
  9.8 0.0 collective-permute-start.2
  9.8 2.2 %collective-permute-start.7 = (f32[1,48,1024]{2,1,0:T(8,128)S(1)}, f32[1,48,1024]{2,1,0:T(8,128)S(1)}, u32[]{:S(2)}, u32[]{:S(2)}) collective-permute-start(f32[1,48,1024]{2,1,0:T(8,128)S(1)} %get-tuple-element.34), channel_id=1, source_target_pairs={{0,28},{4,8},{8,4},{12,16},{16,12},{20,24},{24,20},{28,0},{1,29},{... | collective-permute-start | bytes 589832 | tf_op jit(solution)/shard_map/ppermute | solution.py:489
  12.0 21.0 %collective-permute-done.4.refs_0_.b0 = f32[6,16,1024]{2,1,0:T(8,128)S(1)} collective-permute-done((f32[6,16,1024]{2,1,0:T(8,128)S(1)}, f32[6,16,1024]{2,1,0:T(8,128)S(1)}, u32[]{:S(2)}, u32[]{:S(2)}) %collective-permute-start.4) | collective-permute-done | bytes 393248 | tf_op jit(solution)/shard_map/ppermute | solution.py:477
  33.0 2.8 %collective-permute-start.8 = (f32[1,48,1024]{2,1,0:T(8,128)S(1)}, f32[1,48,1024]{2,1,0:T(8,128)S(1)}, u32[]{:S(2)}, u32[]{:S(2)}) collective-permute-start(f32[1,48,1024]{2,1,0:T(8,128)S(1)} %get-tuple-element.39), channel_id=1, source_target_pairs={{0,28},{4,8},{8,4},{12,16},{16,12},{20,24},{24,20},{28,0},{1,29},{... | collective-permute-start | bytes 589832 | tf_op jit(solution)/shard_map/ppermute | solution.py:489
  35.8 0.0 copy-done.2
  35.8 0.1 shard_map.51
  35.9 0.0 collective-permute-done.1.z1
  35.9 1.6 %collective-permute-start.5 = (f32[8,24,128]{2,1,0:T(8,128)S(1)}, f32[8,24,128]{2,1,0:T(8,128)S(1)}, u32[]{:S(2)}, u32[]{:S(2)}) collective-permute-start(f32[8,24,128]{2,1,0:T(8,128)S(1)} %get-tuple-element.28), channel_id=1, source_target_pairs={{0,1},{1,0},{2,3},{3,2},{4,5},{5,4},{6,7},{7,6},{8,9},{9,8},{10,11... | collective-permute-start | bytes 294920 | tf_op jit(solution)/shard_map/ppermute | solution.py:444
  37.5 0.0 collective-permute-done.2.z2
  37.5 0.0 collective-permute-start.6
  37.5 0.0 copy-done.1
  37.5 0.1 pad_add_fusion.boxes
  37.6 0.2 table.1.sel
  37.8 0.1 broadcast_in_dim.2.level
  37.9 9.8 %early.1 = (f32[16,64,1024]{2,1,0:T(8,128)}, f32[6,8,72,128]{3,2,1,0:T(8,128)S(1)}, f32[2,8,80,128]{3,2,1,0:T(8,128)S(1)}, f32[3,64]{1,0:T(4,128)S(1)}) custom-call(f32[16,64,1024]{2,1,0:T(8,128)S(1)} %copy-done, f32[6,64,1024]{2,1,0:T(8,128)S(1)} %collective-permute-done.refs_1_.a, f32[8,56,128]{2,1,0:T(8,128)S(1)} %collective-permute-done.1.z1, ...), custom_call_target="tpu_custom_call" | custom-call | flops 41943040 | bytes 16777216 | tf_op jit(solution)/shard_map/early/pallas_call | solution.py:505
  47.7 0.0 collective-permute-done.5.z1
  47.8 0.0 collective-permute-done.6.z2
  47.8 0.0 collective-permute-done.3.b
  47.8 4.4 %shard_map.52 = (f32[16,64,1024]{2,1,0:T(8,128)}, f32[2,8,72,128]{3,2,1,0:T(8,128)S(1)}, f32[2,8,80,128]{3,2,1,0:T(8,128)S(1)}, f32[3,64]{1,0:T(4,128)S(1)}) custom-call(f32[6,8,72,128]{3,2,1,0:T(8,128)S(1)} %get-tuple-element.26.part, f32[4,48,1024]{2,1,0:T(8,128)S(1)} %collective-permute-done.3.b, ...), custom_call_target="tpu_custom_call", output_to_operand_aliasing={{0}: (10, {})} | custom-call | flops 2097152 | bytes 4194304 | tf_op jit(solution)/shard_map/pallas_call | solution.py:534
  52.2 0.0 collective-permute-done.7.b
  52.2 2.7 %shard_map.53 = (f32[16,64,1024]{2,1,0:T(8,128)}, f32[1,8,72,128]{3,2,1,0:T(8,128)S(1)}, f32[8,80,128]{2,1,0:T(8,128)S(1)}, f32[8,64,128]{2,1,0:T(8,128)S(1)}, f32[3,64]{1,0:T(4,128)S(1)}) custom-call(f32[2,8,72,128]{3,2,1,0:T(8,128)S(1)} %get-tuple-element.33.part, f32[1,48,1024]{2,1,0:T(8,128)S(1)} %collective-permute-done.7.b, ...), custom_call_target="tpu_custom_call", output_to_operand_aliasing={{0}: (10, {})} | custom-call | flops 524288 | bytes 4194304 | tf_op jit(solution)/shard_map/pallas_call | solution.py:534
  54.9 0.0 collective-permute-done.8.b
  54.9 1.4 %shard_map.54 = (f32[16,64,1024]{2,1,0:T(8,128)}, f32[4,32]{1,0:T(4,128)}) custom-call(f32[1,8,72,128]{3,2,1,0:T(8,128)S(1)} %get-tuple-element.38.part, f32[1,48,1024]{2,1,0:T(8,128)S(1)} %collective-permute-done.8.b, f32[6,16,1024]{2,1,0:T(8,128)S(1)} %collective-permute-done.4.refs_0_.b0, ...), custom_call_target="tpu_custom_call", output_to_operand_aliasing={{0}: (11, {})} | custom-call | flops 524288 | bytes 4194304 | tf_op jit(solution)/shard_map/pallas_call | solution.py:534
  (1 shorter events, 0.0 us)
Async XLA Ops:
  0.6 7.2 %copy-start = (f32[16,64,1024]{2,1,0:T(8,128)S(1)}, f32[16,64,1024]{2,1,0:T(8,128)}, u32[]{:S(2)}) copy-start(f32[16,64,1024]{2,1,0:T(8,128)} %x.5) | copy-start | bytes 12582916
  2.5 5.2 %collective-permute-start = (f32[6,64,1024]{2,1,0:T(8,128)S(1)}, f32[6,64,1024]{2,1,0:T(8,128)S(1)}, u32[]{:S(2)}, u32[]{:S(2)}) collective-permute-start(f32[6,64,1024]{2,1,0:T(8,128)S(1)} %get-tuple-element.23), channel_id=1, source_target_pairs={{0,4},{4,0},{8,12},{12,8},{16,20},{20,16},{24,28},{28,24},{1,5},{5... | collective-permute-start | bytes 4718600 | tf_op jit(solution)/shard_map/ppermute | solution.py:488
  3.1 32.7 %copy-start.2 = (s32[64]{0:T(128)S(1)}, s32[64]{0:T(128)}, u32[]{:S(2)}) copy-start(s32[64]{0:T(128)} %param.4) | copy-start | bytes 772
  3.1 44.7 %collective-permute-start.3 = (f32[4,48,1024]{2,1,0:T(8,128)S(1)}, f32[4,48,1024]{2,1,0:T(8,128)S(1)}, u32[]{:S(2)}, u32[]{:S(2)}) collective-permute-start(f32[4,48,1024]{2,1,0:T(8,128)S(1)} %get-tuple-element.27), channel_id=1, source_target_pairs={{0,28},{4,8},{8,4},{12,16},{16,12},{20,24},{24,20},{28,0},{1,29},{... | collective-permute-start | bytes 2359304 | tf_op jit(solution)/shard_map/ppermute | solution.py:489
  7.7 29.8 %copy-start.1 = (s32[3,32]{1,0:T(4,128)S(1)}, s32[3,32]{1,0:T(4,128)}, u32[]{:S(2)}) copy-start(s32[3,32]{1,0:T(4,128)} %param.5) | copy-start | bytes 1156
  7.7 25.3 %collective-permute-start.4 = (f32[6,16,1024]{2,1,0:T(8,128)S(1)}, f32[6,16,1024]{2,1,0:T(8,128)S(1)}, u32[]{:S(2)}, u32[]{:S(2)}) collective-permute-start(f32[6,16,1024]{2,1,0:T(8,128)S(1)} %edge.1), channel_id=1, source_target_pairs={{0,28},{4,8},{8,4},{12,16},{16,12},{20,24},{24,20},{28,0},{1,29},{... | collective-permute-start | bytes 1179656 | tf_op jit(solution)/shard_map/ppermute | solution.py:477
  8.0 27.9 %collective-permute-start.1 = (f32[8,56,128]{2,1,0:T(8,128)S(1)}, f32[8,56,128]{2,1,0:T(8,128)S(1)}, u32[]{:S(2)}, u32[]{:S(2)}) collective-permute-start(f32[8,56,128]{2,1,0:T(8,128)S(1)} %get-tuple-element.24), channel_id=1, source_target_pairs={{0,1},{1,0},{2,3},{3,2},{4,5},{5,4},{6,7},{7,6},{8,9},{9,8},{10,11... | collective-permute-start | bytes 688136 | tf_op jit(solution)/shard_map/ppermute | solution.py:444
  9.8 27.8 %collective-permute-start.2 = (f32[8,56,128]{2,1,0:T(8,128)S(1)}, f32[8,56,128]{2,1,0:T(8,128)S(1)}, u32[]{:S(2)}, u32[]{:S(2)}) collective-permute-start(f32[8,56,128]{2,1,0:T(8,128)S(1)} %get-tuple-element.25), channel_id=1, source_target_pairs={{0,4},{1,2},{2,1},{3,7},{4,0},{5,6},{6,5},{7,3},{8,12},{9,10},{10,... | collective-permute-start | bytes 688136 | tf_op jit(solution)/shard_map/ppermute | solution.py:444
  9.8 42.4 %collective-permute-start.7 = (f32[1,48,1024]{2,1,0:T(8,128)S(1)}, f32[1,48,1024]{2,1,0:T(8,128)S(1)}, u32[]{:S(2)}, u32[]{:S(2)}) collective-permute-start(f32[1,48,1024]{2,1,0:T(8,128)S(1)} %get-tuple-element.34), channel_id=1, source_target_pairs={{0,28},{4,8},{8,4},{12,16},{16,12},{20,24},{24,20},{28,0},{1,29},{... | collective-permute-start | bytes 589832 | tf_op jit(solution)/shard_map/ppermute | solution.py:489
  33.0 21.9 %collective-permute-start.8 = (f32[1,48,1024]{2,1,0:T(8,128)S(1)}, f32[1,48,1024]{2,1,0:T(8,128)S(1)}, u32[]{:S(2)}, u32[]{:S(2)}) collective-permute-start(f32[1,48,1024]{2,1,0:T(8,128)S(1)} %get-tuple-element.39), channel_id=1, source_target_pairs={{0,28},{4,8},{8,4},{12,16},{16,12},{20,24},{24,20},{28,0},{1,29},{... | collective-permute-start | bytes 589832 | tf_op jit(solution)/shard_map/ppermute | solution.py:489
  35.9 11.9 %collective-permute-start.5 = (f32[8,24,128]{2,1,0:T(8,128)S(1)}, f32[8,24,128]{2,1,0:T(8,128)S(1)}, u32[]{:S(2)}, u32[]{:S(2)}) collective-permute-start(f32[8,24,128]{2,1,0:T(8,128)S(1)} %get-tuple-element.28), channel_id=1, source_target_pairs={{0,1},{1,0},{2,3},{3,2},{4,5},{5,4},{6,7},{7,6},{8,9},{9,8},{10,11... | collective-permute-start | bytes 294920 | tf_op jit(solution)/shard_map/ppermute | solution.py:444
  37.5 10.2 %collective-permute-start.6 = (f32[8,24,128]{2,1,0:T(8,128)S(1)}, f32[8,24,128]{2,1,0:T(8,128)S(1)}, u32[]{:S(2)}, u32[]{:S(2)}) collective-permute-start(f32[8,24,128]{2,1,0:T(8,128)S(1)} %get-tuple-element.29), channel_id=1, source_target_pairs={{0,4},{1,2},{2,1},{3,7},{4,0},{5,6},{6,5},{7,3},{8,12},{9,10},{10,... | collective-permute-start | bytes 294920 | tf_op jit(solution)/shard_map/ppermute | solution.py:444

commit v6 on v5

--- a/solution.py
+++ b/solution.py
@@ -42,6 +42,11 @@
     return [jnp.where(lane == 0, rolled[j], rolled[j + 1]) for j in range(len(strips))]
 
 
+def column_sums(strips, lane):
+    pairs = [a + b for a, b in zip(strips, next_column(strips, lane, jnp.zeros_like(strips[0])))]
+    return [a + b for a, b in zip(pairs, previous_column(pairs, lane, strips[0]))]
+
+
 def column_tops(strips, lane):
     tops = [jnp.maximum(a, b) for a, b in zip(strips, next_column(strips, lane, strips[-1]))]
     return [jnp.maximum(a, b) for a, b in zip(tops, previous_column(tops, lane, tops[0]))]
@@ -79,13 +84,11 @@
 def smooth_window(first, i, smooth, o, start, rows, strips):
     sub, lane = iotas()
     place = lax.axis_index("row")
-    zero = jnp.zeros((SUB, LANES), jnp.float32)
     seconds = []
     for j in range(strips):
         a, b, c = (first[i, j, pl.ds(TOP + start + e, SUB), :] for e in (-1, 0, 1))
         seconds.append((a + b) + (b + c))
-    pairs = [a + b for a, b in zip(seconds, next_column(seconds, lane, zero))]
-    sums = [a + b for a, b in zip(pairs, previous_column(pairs, lane, seconds[0]))]
+    sums = column_sums(seconds, lane)
     for j in range(strips):
         v = sums[j]
         if start < 0:
@@ -141,10 +144,22 @@
     lax.fori_loop(0, rows // SUB, body, 0)
 
 
-def weigh_last(first, smooth, centre, tail, level, weight, rows, strips):
+def weigh_last(ready, fresh, padded, smooth, centre, tail, level, weight, rows, strips):
     _, lane = iotas()
-    for k, start in enumerate(window_starts(rows)):
-        smooth_window(first, 0, smooth, 0, start, rows, strips)
+    tap = float(frame_taps()[-1])
+    starts = window_starts(rows)
+    zero = jnp.zeros((SUB, LANES), jnp.float32)
+    for j in range(strips):
+        for t in range(rows // SUB):
+            inner = 0 < t < rows // SUB - 1
+            padded[j, pl.ds(TOP + t * SUB, SUB), :] = fresh[j, rows_of(t - 1), :] if inner else zero
+    for k, start in enumerate(starts):
+        for j in range(strips):
+            v = ready[j, pl.ds(TOP + start, SUB), :]
+            if 0 < k < len(starts) - 1:
+                a, b, c = (padded[j, pl.ds(TOP + start + e, SUB), :] for e in (-1, 0, 1))
+                v = v + tap * ((a + b) + (b + c))
+            smooth[0, j, pl.ds(TOP + start, SUB), :] = v
         if k == 0:
             continue
         t = k - 1
@@ -216,19 +231,30 @@
         copy.wait()
 
 
-def pack_kernel(x, near, *rest):
+def pack_kernel(x, near, rims, *rest):
     count, rows, _ = x.shape
     *pieces, sems = rest
     even = is_even()
     copies = [pltpu.make_async_copy(x.at[pl.ds(jnp.where(even, count - REACH, 0), REACH)], near, sems.at[0])]
+    *targets, filtered, last = pieces
     for k, (begin, end) in enumerate(PIECES):
         start = jnp.where(even, begin, count - end)
         source = x.at[pl.ds(start, end - begin), pl.ds(SUB, rows - 2 * SUB)]
-        copies.append(pltpu.make_async_copy(source, pieces[k], sems.at[k + 1]))
+        copies.append(pltpu.make_async_copy(source, (*targets, last)[k], sems.at[k + 1]))
+    for k, (row, to) in enumerate(((0, 0), (rows - SUB, SUB))):
+        copies.append(
+            pltpu.make_async_copy(x.at[:, pl.ds(row, SUB)], rims.at[:, pl.ds(to, SUB)], sems.at[len(PIECES) + 1 + k])
+        )
     for copy in copies:
         copy.start()
     for copy in copies:
         copy.wait()
+    _, lane = iotas()
+    strips = filtered.shape[0]
+    for t in range(rows // SUB - 2):
+        values = [last[0, rows_of(t), pl.ds(j * LANES, LANES)] for j in range(strips)]
+        for j, v in enumerate(column_sums(values, lane)):
+            filtered[j, rows_of(t), :] = v
 
 
 def rows_kernel(*refs):
@@ -320,21 +346,11 @@
     copy.wait()
 
 
-def late_kernel(part, b, b0, z1, z2, level, sel, boxes, sums, *rest, count, piece):
+def late_kernel(part, b, b0, z1, z2, level, sel, boxes, sums, edge, _, out, new_part, *rest, count, piece):
     begin, end = piece
     late = end - begin
-    final = end == REACH
     ahead = end == REACH - 1
-    if final:
-        edge, tail, _, out, *rest = rest
-    else:
-        edge, _, out, *rest = rest
-    if final:
-        stats, first, smooth, weight, sems, figures = rest
-    elif ahead:
-        new_part, new_edge, tail, new_sums, first, smooth, weight, sems = rest
-    else:
-        new_part, new_edge, new_sums, first, smooth, weight, sems = rest
+    new_edge, *tails, new_sums, first, smooth, weight, sems = rest
     rows, columns = out.shape[1], out.shape[2]
     tiles, strips = rows // SUB, columns // LANES
     even = is_even()
@@ -342,16 +358,21 @@
     early = count - REACH
 
     def body(j, carry):
-        at = pl.ds(j * LANES if final else pl.multiple_of(j * LANES, LANES), LANES)
+        at = pl.ds(pl.multiple_of(j * LANES, LANES), LANES)
+
+        def load_edges(q):
+            where = jnp.where(even, REACH - 1 - q, q)
+            return b0[where, rows_of(0), at], [b0[where, rows_of(1), at], halo_tile(z1, z2, where, j)]
 
         def load(q):
             index = jnp.where(even, end - 1 - q, q - begin)
-            where = jnp.where(even, REACH - 1 - q, q)
-            return (
-                [b0[where, rows_of(0), at]]
-                + [b[index, rows_of(t), at] for t in range(tiles - 2)]
-                + [b0[where, rows_of(1), at], halo_tile(z1, z2, where, j)]
-            )
+            head, last = load_edges(q)
+            return [head] + [b[index, rows_of(t), at] for t in range(tiles - 2)] + last
+
+        def add(total, tap, values):
+            if tap == -1.0:
+                return [u - v for u, v in zip(total, values)]
+            return [u + tap * v for u, v in zip(total, values)]
 
         fresh = {q: load(q) for q in range(begin, end)}
         for i in range(REACH - begin):
@@ -359,60 +380,65 @@
             for q in range(begin, end):
                 distance = REACH - 1 + q - begin - i
                 if abs(distance) < REACH:
-                    tap = float(taps[abs(distance)])
-                    if tap == -1.0:
-                        total = [u - v for u, v in zip(total, fresh[q])]
-                    else:
-                        total = [u + tap * v for u, v in zip(total, fresh[q])]
-            if i < late:
+                    total = add(total, float(taps[abs(distance)]), fresh[q])
+            if ahead and i == late:
+                head, last = load_edges(end)
+                tap = float(taps[REACH - 1])
+                total = add(total[:1], tap, [head]) + total[1 : tiles - 1] + add(total[tiles - 1 :], tap, last)
+            if i < late or ahead:
                 store_rows(first, i, j, total)
             else:
                 for t, v in enumerate(total):
                     new_part[i - late, j, rows_of(t), :] = v
         return carry
 
-    if final:
-        for j in range(strips):
-            body(j, 0)
+    lax.fori_loop(0, strips, body, 0)
+    smooth_stage(first, smooth, late + 1 if ahead else late, 0, rows, strips)
+    if ahead:
+        copies = [
+            pltpu.make_async_copy(smooth.at[late - 1], new_edge, sems.at[0]),
+            pltpu.make_async_copy(smooth.at[late], new_part, sems.at[2]),
+        ]
     else:
-        lax.fori_loop(0, strips, body, 0)
-    copies = []
-    if final:
-        weigh_last(first, smooth, edge, tail, level, weight, rows, strips)
-    else:
-        smooth_stage(first, smooth, late, 0, rows, strips)
-        if ahead:
-            copies.append(pltpu.make_async_copy(smooth.at[late - 1], new_edge, sems.at[0]))
-        else:
-            copies.append(pltpu.make_async_copy(smooth.at[pl.ds(late - 2, 2)], new_edge, sems.at[0]))
-        copies[0].start()
-        weigh(
-            lambda i: (edge, i) if i < 2 else (smooth, i - 2),
-            level,
-            weight,
-            lambda i: jnp.where(even, late - i, i - 1),
-            late,
-            rows,
-            strips,
-            tail if ahead else None,
-        )
+        copies = [pltpu.make_async_copy(smooth.at[pl.ds(late - 2, 2)], new_edge, sems.at[0])]
+    for copy in copies:
+        copy.start()
+    weigh(
+        lambda i: (edge, i) if i < 2 else (smooth, i - 2),
+        level,
+        weight,
+        lambda i: jnp.where(even, late - i, i - 1),
+        late,
+        rows,
+        strips,
+        *tails,
+    )
     place = jnp.where(even, REACH - end, early + begin)
     copies.append(pltpu.make_async_copy(weight, out.at[pl.ds(place, late)], sems.at[1]))
     copies[-1].start()
     start = tuple(sums[i : i + 1, :] for i in range(3))
+    for i, v in enumerate(box_sums(weight, sel, boxes, place, count, start)):
+        new_sums[i : i + 1, :] = v
+    for copy in copies:
+        copy.wait()
+
+
+def last_kernel(ready, fresh, level, sel, boxes, sums, centre, tail, _, out, stats, padded, smooth, weight, figures, sems):
+    count, rows, columns = out.shape
+    weigh_last(ready, fresh, padded, smooth, centre, tail, level, weight, rows, columns // LANES)
+    place = jnp.where(is_even(), 0, count - 1)
+    copies = [pltpu.make_async_copy(weight, out.at[pl.ds(place, 1)], sems.at[1])]
+    copies[0].start()
+    start = tuple(sums[i : i + 1, :] for i in range(3))
     total, by_frame, by_row = box_sums(weight, sel, boxes, place, count, start)
-    if final:
-        slots = stats.shape[1]
-        cells = float(BOX_F * BOX_R * BOX_C)
-        figures[0:1, :] = total[:, :slots] / cells
-        figures[1:2, :] = by_frame[:, :slots] / (cells * (BOX_F - 1))
-        figures[2:3, :] = by_row[:, :slots] / (cells * (BOX_R - 1))
-        figures[3:4, :] = total[:, slots:] / (cells * (BOX_C - 1))
-        copies.append(pltpu.make_async_copy(figures, stats, sems.at[0]))
-        copies[-1].start()
-    else:
-        for i, v in enumerate((total, by_frame, by_row)):
-            new_sums[i : i + 1, :] = v
+    slots = stats.shape[1]
+    cells = float(BOX_F * BOX_R * BOX_C)
+    figures[0:1, :] = total[:, :slots] / cells
+    figures[1:2, :] = by_frame[:, :slots] / (cells * (BOX_F - 1))
+    figures[2:3, :] = by_row[:, :slots] / (cells * (BOX_R - 1))
+    figures[3:4, :] = total[:, slots:] / (cells * (BOX_C - 1))
+    copies.append(pltpu.make_async_copy(figures, stats, sems.at[0]))
+    copies[1].start()
     for copy in copies:
         copy.wait()
 
@@ -475,19 +501,23 @@
         name="edge",
     )(in_hbm)
     b0 = lax.ppermute(edges, "omega", other)
-    near, *pieces = pl.pallas_call(
+    near, rims, *pieces = pl.pallas_call(
         pack_kernel,
-        out_shape=(shape(REACH, rows, columns),)
-        + tuple(shape(end - begin, rows - 2 * SUB, columns) for begin, end in PIECES),
+        out_shape=(shape(REACH, rows, columns), shape(count, 2 * SUB, columns))
+        + tuple(shape(end - begin, rows - 2 * SUB, columns) for begin, end in PIECES[:-1])
+        + (shape(strips, rows - 2 * SUB, LANES),),
         in_specs=[hbm()],
-        out_specs=(vmem(),) * (1 + len(PIECES)),
-        scratch_shapes=[pltpu.SemaphoreType.DMA((1 + len(PIECES),))],
+        out_specs=(vmem(),) * (2 + len(PIECES)),
+        scratch_shapes=[
+            pltpu.VMEM((1, rows - 2 * SUB, columns), jnp.float32),
+            pltpu.SemaphoreType.DMA((3 + len(PIECES),)),
+        ],
         compiler_params=small,
         name="pack",
     )(in_hbm)
     a = lax.ppermute(near, "omega", partner)
     pieces = [lax.ppermute(piece, "omega", other) for piece in pieces]
-    z1, z2 = row_exchange([frames, a], strips)
+    z1, z2 = row_exchange([rims, a], strips)
     far1, far2 = row_exchange([b0], strips)
 
     level = jnp.broadcast_to((thresholds.astype(jnp.float32) / 64.0)[:, None], (rows, LANES))
@@ -522,35 +552,48 @@
         cost_estimate=pl.CostEstimate(flops=40 * frames.size, bytes_accessed=16 << 20, transcendentals=0),
         name="early",
     )(frames, a, z1, z2, level, sel, boxes)
-    edge = [edge]
-    for (begin, end), piece in zip(PIECES, pieces):
-        final = end == REACH
-        ahead = end == REACH - 1
+    tails = ()
+    params = pltpu.CompilerParams(vmem_limit_bytes=14 << 20)
+    for (begin, end), piece in zip(PIECES[:-1], pieces[:-1]):
         late = end - begin
-        handed = (shape(4, slots),)
-        if not final:
-            edges = (shape(strips, padded, LANES), shape(strips, rows, LANES)) if ahead else (shape(2, strips, padded, LANES),)
-            handed = (shape(REACH - end, strips, rows + SUB, LANES), *edges, shape(3, 2 * slots))
-        weight, *rest = pl.pallas_call(
+        if end == REACH - 1:
+            made = late + 1
+            handed = (shape(strips, padded, LANES), shape(strips, padded, LANES), shape(strips, rows, LANES))
+        else:
+            made = late
+            handed = (shape(REACH - end, strips, rows + SUB, LANES), shape(2, strips, padded, LANES))
+        weight, part, edge, *tails, sums = pl.pallas_call(
             functools.partial(late_kernel, count=count, piece=(begin, end)),
-            out_shape=(shape(count, rows, columns), *handed),
-            in_specs=[vmem()] * (9 + len(edge)) + [hbm()],
-            out_specs=(hbm(),) + (hbm() if final else vmem(),) * len(handed),
-            input_output_aliases={9 + len(edge): 0},
+            out_shape=(shape(count, rows, columns), *handed, shape(3, 2 * slots)),
+            in_specs=[vmem()] * 10 + [hbm()],
+            out_specs=(hbm(),) + (vmem(),) * (1 + len(handed)),
+            input_output_aliases={10: 0},
             scratch_shapes=[
-                pltpu.VMEM((late, strips, padded, LANES), jnp.float32),
-                pltpu.VMEM((late, strips, padded, LANES), jnp.float32),
+                pltpu.VMEM((made, strips, padded, LANES), jnp.float32),
+                pltpu.VMEM((made, strips, padded, LANES), jnp.float32),
                 pltpu.VMEM((late, rows, columns), jnp.float32),
-                pltpu.SemaphoreType.DMA((2,)),
-            ]
-            + ([pltpu.VMEM((4, slots), jnp.float32)] if final else []),
-            compiler_params=pltpu.CompilerParams(vmem_limit_bytes=14 << 20),
+                pltpu.SemaphoreType.DMA((3,)),
+            ],
+            compiler_params=params,
             cost_estimate=pl.CostEstimate(flops=8 * late * rows * columns, bytes_accessed=4 << 20, transcendentals=0),
-        )(part, piece, b0, far1, far2, level, sel, boxes, sums, *edge, weight)
-        if final:
-            (stats,) = rest
-        else:
-            part, *edge, sums = rest
+        )(part, piece, b0, far1, far2, level, sel, boxes, sums, edge, weight)
+    weight, stats = pl.pallas_call(
+        last_kernel,
+        out_shape=(shape(count, rows, columns), shape(4, slots)),
+        in_specs=[vmem()] * 8 + [hbm()],
+        out_specs=(hbm(), hbm()),
+        input_output_aliases={8: 0},
+        scratch_shapes=[
+            pltpu.VMEM((strips, padded, LANES), jnp.float32),
+            pltpu.VMEM((1, strips, padded, LANES), jnp.float32),
+            pltpu.VMEM((1, rows, columns), jnp.float32),
+            pltpu.VMEM((4, slots), jnp.float32),
+            pltpu.SemaphoreType.DMA((2,)),
+        ],
+        compiler_params=params,
+        cost_estimate=pl.CostEstimate(flops=8 * rows * columns, bytes_accessed=4 << 20, transcendentals=0),
+        name="last",
+    )(part, pieces[-1], level, sel, boxes, sums, edge, *tails, weight)
     return weight, stats
 
 

time: 56.6 us -> 57.3 us (1.012)
  Pallas kernels: 21.7 us -> 22.4 us
    pallas_call x1 -> x2, Pallas kernels: 1.9 us -> 3.52 us  [the longest x1 2.29 us: steps(): pl.pallas_call(pack_kernel, out_shape=(shape(REACH, rows, columns), shape...]
    pallas_call x3 -> x2, Pallas kernels: 8.51 us -> 7.55 us  [steps(): pl.pallas_call(functools.partial(late_kernel, count=count, piece=(begin,...]
where the time goes in v6:
time: 57.3 us; the launch traced here: 57 us
  Pallas kernels  22.4 us (39%)
  waiting for transfers between devices  21.1 us (37%)
  starting transfers between devices  12.6 us (22%)
  between operations  0.76 us (1%)
    ppermute x1, waiting for transfers between devices, steps(): b0 = lax.ppermute(edges, 'omega', other)  21.1 us
    pallas_call x1, Pallas kernels, steps(): pl.pallas_call(functools.partial(early_kernel, early=early), out_shape=(s...  9.83 us
    ppermute x3, starting transfers between devices, steps(): pieces = [lax.ppermute(piece, 'omega', other) for piece in pieces]  8.2 us
    pallas_call x2, Pallas kernels, steps(): pl.pallas_call(functools.partial(late_kernel, count=count, piece=(begin,...  7.55 us
    ppermute x2, starting transfers between devices, row_exchange(): lax.ppermute(z1, both, row_pairs(ring, column, 0))  3.42 us
    pallas_call x1, Pallas kernels, steps(): pl.pallas_call(pack_kernel, out_shape=(shape(REACH, rows, columns), shape...  2.29 us
    pallas_call x1, Pallas kernels, steps(): pl.pallas_call(last_kernel, out_shape=(shape(count, rows, columns), shape...  1.23 us
  transfers between devices with their start and end apart: 9, of which 1 were waited for; matrix products, arithmetic and copies ran while one was open for 0% of the time, Pallas kernels for 33%

profile of v6, /device:TPU:0, one launch (start us, length us, event | category | flops | bytes accessed | tf_op | source)
XLA Modules:
  0.0 57.0 jit_solution(4876789442812819471)
XLA Ops:
  0.6 2.3 %pack.1 = (f32[6,64,1024]{2,1,0:T(8,128)S(1)}, f32[16,16,1024]{2,1,0:T(8,128)S(1)}, f32[4,48,1024]{2,1,0:T(8,128)S(1)}, f32[1,48,1024]{2,1,0:T(8,128)S(1)}, f32[8,48,128]{2,1,0:T(8,128)S(1)}) custom-call(f32[16,64,1024]{2,1,0:T(8,128)} %x.5), custom_call_target="tpu_custom_call" | custom-call | tf_op jit(solution)/shard_map/pack/pallas_call | solution.py:504
  2.9 0.0 copy-start.2
  2.9 0.0 copy-start.1
  2.9 0.0 copy-start
  3.0 0.6 collective-permute-start
  3.5 3.5 %collective-permute-start.3 = (f32[4,48,1024]{2,1,0:T(8,128)S(1)}, f32[4,48,1024]{2,1,0:T(8,128)S(1)}, u32[]{:S(2)}, u32[]{:S(2)}) collective-permute-start(f32[4,48,1024]{2,1,0:T(8,128)S(1)} %get-tuple-element.29), channel_id=1, source_target_pairs={{0,28},{4,8},{8,4},{12,16},{16,12},{20,24},{24,20},{28,0},{1,29},{... | collective-permute-start | bytes 2359304 | tf_op jit(solution)/shard_map/ppermute | solution.py:519
  7.1 1.0 %edge.1 = f32[6,16,1024]{2,1,0:T(8,128)S(1)} custom-call(f32[16,64,1024]{2,1,0:T(8,128)} %x.5), custom_call_target="tpu_custom_call" | custom-call | tf_op jit(solution)/shard_map/edge/pallas_call | solution.py:494
  8.1 0.4 collective-permute-start.4
  8.6 0.0 collective-permute-done.refs_1_.a
  8.6 0.2 shard_map.50
  8.7 1.8 %collective-permute-start.1 = (f32[8,56,128]{2,1,0:T(8,128)S(1)}, f32[8,56,128]{2,1,0:T(8,128)S(1)}, u32[]{:S(2)}, u32[]{:S(2)}) collective-permute-start(f32[8,56,128]{2,1,0:T(8,128)S(1)} %get-tuple-element.26), channel_id=1, source_target_pairs={{0,1},{1,0},{2,3},{3,2},{4,5},{5,4},{6,7},{7,6},{8,9},{9,8},{10,11... | collective-permute-start | bytes 688136 | tf_op jit(solution)/shard_map/ppermute | solution.py:470
  10.5 0.0 collective-permute-start.2
  10.5 1.8 %collective-permute-start.7 = (f32[1,48,1024]{2,1,0:T(8,128)S(1)}, f32[1,48,1024]{2,1,0:T(8,128)S(1)}, u32[]{:S(2)}, u32[]{:S(2)}) collective-permute-start(f32[1,48,1024]{2,1,0:T(8,128)S(1)} %get-tuple-element.36), channel_id=1, source_target_pairs={{0,28},{4,8},{8,4},{12,16},{16,12},{20,24},{24,20},{28,0},{1,29},{... | collective-permute-start | bytes 589832 | tf_op jit(solution)/shard_map/ppermute | solution.py:519
  12.4 21.1 %collective-permute-done.4.refs_0_.b0 = f32[6,16,1024]{2,1,0:T(8,128)S(1)} collective-permute-done((f32[6,16,1024]{2,1,0:T(8,128)S(1)}, f32[6,16,1024]{2,1,0:T(8,128)S(1)}, u32[]{:S(2)}, u32[]{:S(2)}) %collective-permute-start.4) | collective-permute-done | bytes 393248 | tf_op jit(solution)/shard_map/ppermute | solution.py:503
  33.4 2.8 %collective-permute-start.8 = (f32[8,48,128]{2,1,0:T(8,128)S(1)}, f32[8,48,128]{2,1,0:T(8,128)S(1)}, u32[]{:S(2)}, u32[]{:S(2)}) collective-permute-start(f32[8,48,128]{2,1,0:T(8,128)S(1)} %get-tuple-element.41), channel_id=1, source_target_pairs={{0,28},{4,8},{8,4},{12,16},{16,12},{20,24},{24,20},{28,0},{1,29},{... | collective-permute-start | bytes 589832 | tf_op jit(solution)/shard_map/ppermute | solution.py:519
  36.2 0.0 copy-done.2
  36.2 0.1 shard_map.51
  36.3 0.0 collective-permute-done.1.z1
  36.3 1.6 %collective-permute-start.5 = (f32[8,24,128]{2,1,0:T(8,128)S(1)}, f32[8,24,128]{2,1,0:T(8,128)S(1)}, u32[]{:S(2)}, u32[]{:S(2)}) collective-permute-start(f32[8,24,128]{2,1,0:T(8,128)S(1)} %get-tuple-element.30), channel_id=1, source_target_pairs={{0,1},{1,0},{2,3},{3,2},{4,5},{5,4},{6,7},{7,6},{8,9},{9,8},{10,11... | collective-permute-start | bytes 294920 | tf_op jit(solution)/shard_map/ppermute | solution.py:470
  37.9 0.0 collective-permute-done.2.z2
  37.9 0.0 collective-permute-start.6
  37.9 0.0 copy-done.1
  38.0 0.1 pad_add_fusion.boxes
  38.0 0.2 table.1.sel
  38.2 0.1 broadcast_in_dim.2.level
  38.3 0.0 copy-done
  38.3 9.8 %early.1 = (f32[16,64,1024]{2,1,0:T(8,128)}, f32[6,8,72,128]{3,2,1,0:T(8,128)S(1)}, f32[2,8,80,128]{3,2,1,0:T(8,128)S(1)}, f32[3,64]{1,0:T(4,128)S(1)}) custom-call(f32[16,64,1024]{2,1,0:T(8,128)S(1)} %copy-done, f32[6,64,1024]{2,1,0:T(8,128)S(1)} %collective-permute-done.refs_1_.a, f32[8,56,128]{2,1,0:T(8,128)S(1)} %collective-permute-done.1.z1, ...), custom_call_target="tpu_custom_call" | custom-call | flops 41943040 | bytes 16777216 | tf_op jit(solution)/shard_map/early/pallas_call | solution.py:535
  48.2 0.0 collective-permute-done.5.z1
  48.2 0.0 collective-permute-done.6.z2
  48.2 0.0 collective-permute-done.3.b
  48.2 4.4 %shard_map.52 = (f32[16,64,1024]{2,1,0:T(8,128)}, f32[2,8,72,128]{3,2,1,0:T(8,128)S(1)}, f32[2,8,80,128]{3,2,1,0:T(8,128)S(1)}, f32[3,64]{1,0:T(4,128)S(1)}) custom-call(f32[6,8,72,128]{3,2,1,0:T(8,128)S(1)} %get-tuple-element.28.part, f32[4,48,1024]{2,1,0:T(8,128)S(1)} %collective-permute-done.3.b, ...), custom_call_target="tpu_custom_call", output_to_operand_aliasing={{0}: (10, {})} | custom-call | flops 2097152 | bytes 4194304 | tf_op jit(solution)/shard_map/pallas_call | solution.py:565
  52.6 0.0 collective-permute-done.7.b
  52.6 3.2 %shard_map.53 = (f32[16,64,1024]{2,1,0:T(8,128)}, f32[8,80,128]{2,1,0:T(8,128)S(1)}, f32[8,80,128]{2,1,0:T(8,128)S(1)}, f32[8,64,128]{2,1,0:T(8,128)S(1)}, f32[3,64]{1,0:T(4,128)S(1)}) custom-call(f32[2,8,72,128]{3,2,1,0:T(8,128)S(1)} %get-tuple-element.35.part, f32[1,48,1024]{2,1,0:T(8,128)S(1)} %collective-permute-done.7.b, ...), custom_call_target="tpu_custom_call", output_to_operand_aliasing={{0}: (10, {})} | custom-call | flops 524288 | bytes 4194304 | tf_op jit(solution)/shard_map/pallas_call | solution.py:565
  55.8 0.0 collective-permute-done.8.fresh
  55.8 1.2 %last.1 = (f32[16,64,1024]{2,1,0:T(8,128)}, f32[4,32]{1,0:T(4,128)}) custom-call(f32[8,80,128]{2,1,0:T(8,128)S(1)} %get-tuple-element.40.ready, f32[8,48,128]{2,1,0:T(8,128)S(1)} %collective-permute-done.8.fresh, f32[64,128]{1,0:T(8,128)S(1)} %broadcast_in_dim.2.level, bf16[1024,64]{1,0:T(8,128)(2,1)S(1)} %table.1.sel, ...), custom_call_target="tpu_custom_call", output_to_operand_aliasing={{0}: (8, {})} | custom-call | flops 524288 | bytes 4194304 | tf_op jit(solution)/shard_map/last/pallas_call | solution.py:580
  (1 shorter events, 0.0 us)
Async XLA Ops:
  2.9 33.3 %copy-start.2 = (s32[64]{0:T(128)S(1)}, s32[64]{0:T(128)}, u32[]{:S(2)}) copy-start(s32[64]{0:T(128)} %param.4) | copy-start | bytes 772
  2.9 35.0 %copy-start.1 = (s32[3,32]{1,0:T(4,128)S(1)}, s32[3,32]{1,0:T(4,128)}, u32[]{:S(2)}) copy-start(s32[3,32]{1,0:T(4,128)} %param.5) | copy-start | bytes 1156
  2.9 35.4 %copy-start = (f32[16,64,1024]{2,1,0:T(8,128)S(1)}, f32[16,64,1024]{2,1,0:T(8,128)}, u32[]{:S(2)}) copy-start(f32[16,64,1024]{2,1,0:T(8,128)} %x.5) | copy-start | bytes 12582916
  3.0 5.6 %collective-permute-start = (f32[6,64,1024]{2,1,0:T(8,128)S(1)}, f32[6,64,1024]{2,1,0:T(8,128)S(1)}, u32[]{:S(2)}, u32[]{:S(2)}) collective-permute-start(f32[6,64,1024]{2,1,0:T(8,128)S(1)} %get-tuple-element.24), channel_id=1, source_target_pairs={{0,4},{4,0},{8,12},{12,8},{16,20},{20,16},{24,28},{28,24},{1,5},{5... | collective-permute-start | bytes 4718600 | tf_op jit(solution)/shard_map/ppermute | solution.py:518
  3.5 44.7 %collective-permute-start.3 = (f32[4,48,1024]{2,1,0:T(8,128)S(1)}, f32[4,48,1024]{2,1,0:T(8,128)S(1)}, u32[]{:S(2)}, u32[]{:S(2)}) collective-permute-start(f32[4,48,1024]{2,1,0:T(8,128)S(1)} %get-tuple-element.29), channel_id=1, source_target_pairs={{0,28},{4,8},{8,4},{12,16},{16,12},{20,24},{24,20},{28,0},{1,29},{... | collective-permute-start | bytes 2359304 | tf_op jit(solution)/shard_map/ppermute | solution.py:519
  8.1 25.3 %collective-permute-start.4 = (f32[6,16,1024]{2,1,0:T(8,128)S(1)}, f32[6,16,1024]{2,1,0:T(8,128)S(1)}, u32[]{:S(2)}, u32[]{:S(2)}) collective-permute-start(f32[6,16,1024]{2,1,0:T(8,128)S(1)} %edge.1), channel_id=1, source_target_pairs={{0,28},{4,8},{8,4},{12,16},{16,12},{20,24},{24,20},{28,0},{1,29},{... | collective-permute-start | bytes 1179656 | tf_op jit(solution)/shard_map/ppermute | solution.py:503
  8.7 27.6 %collective-permute-start.1 = (f32[8,56,128]{2,1,0:T(8,128)S(1)}, f32[8,56,128]{2,1,0:T(8,128)S(1)}, u32[]{:S(2)}, u32[]{:S(2)}) collective-permute-start(f32[8,56,128]{2,1,0:T(8,128)S(1)} %get-tuple-element.26), channel_id=1, source_target_pairs={{0,1},{1,0},{2,3},{3,2},{4,5},{5,4},{6,7},{7,6},{8,9},{9,8},{10,11... | collective-permute-start | bytes 688136 | tf_op jit(solution)/shard_map/ppermute | solution.py:470
  10.5 27.4 %collective-permute-start.2 = (f32[8,56,128]{2,1,0:T(8,128)S(1)}, f32[8,56,128]{2,1,0:T(8,128)S(1)}, u32[]{:S(2)}, u32[]{:S(2)}) collective-permute-start(f32[8,56,128]{2,1,0:T(8,128)S(1)} %get-tuple-element.27), channel_id=1, source_target_pairs={{0,4},{1,2},{2,1},{3,7},{4,0},{5,6},{6,5},{7,3},{8,12},{9,10},{10,... | collective-permute-start | bytes 688136 | tf_op jit(solution)/shard_map/ppermute | solution.py:470
  10.5 42.1 %collective-permute-start.7 = (f32[1,48,1024]{2,1,0:T(8,128)S(1)}, f32[1,48,1024]{2,1,0:T(8,128)S(1)}, u32[]{:S(2)}, u32[]{:S(2)}) collective-permute-start(f32[1,48,1024]{2,1,0:T(8,128)S(1)} %get-tuple-element.36), channel_id=1, source_target_pairs={{0,28},{4,8},{8,4},{12,16},{16,12},{20,24},{24,20},{28,0},{1,29},{... | collective-permute-start | bytes 589832 | tf_op jit(solution)/shard_map/ppermute | solution.py:519
  33.4 22.4 %collective-permute-start.8 = (f32[8,48,128]{2,1,0:T(8,128)S(1)}, f32[8,48,128]{2,1,0:T(8,128)S(1)}, u32[]{:S(2)}, u32[]{:S(2)}) collective-permute-start(f32[8,48,128]{2,1,0:T(8,128)S(1)} %get-tuple-element.41), channel_id=1, source_target_pairs={{0,28},{4,8},{8,4},{12,16},{16,12},{20,24},{24,20},{28,0},{1,29},{... | collective-permute-start | bytes 589832 | tf_op jit(solution)/shard_map/ppermute | solution.py:519
  36.3 11.9 %collective-permute-start.5 = (f32[8,24,128]{2,1,0:T(8,128)S(1)}, f32[8,24,128]{2,1,0:T(8,128)S(1)}, u32[]{:S(2)}, u32[]{:S(2)}) collective-permute-start(f32[8,24,128]{2,1,0:T(8,128)S(1)} %get-tuple-element.30), channel_id=1, source_target_pairs={{0,1},{1,0},{2,3},{3,2},{4,5},{5,4},{6,7},{7,6},{8,9},{9,8},{10,11... | collective-permute-start | bytes 294920 | tf_op jit(solution)/shard_map/ppermute | solution.py:470
  37.9 10.2 %collective-permute-start.6 = (f32[8,24,128]{2,1,0:T(8,128)S(1)}, f32[8,24,128]{2,1,0:T(8,128)S(1)}, u32[]{:S(2)}, u32[]{:S(2)}) collective-permute-start(f32[8,24,128]{2,1,0:T(8,128)S(1)} %get-tuple-element.31), channel_id=1, source_target_pairs={{0,4},{1,2},{2,1},{3,7},{4,0},{5,6},{6,5},{7,3},{8,12},{9,10},{10,... | collective-permute-start | bytes 294920 | tf_op jit(solution)/shard_map/ppermute | solution.py:470

commit v7 on v6

--- a/solution.py
+++ b/solution.py
@@ -144,23 +144,31 @@
     lax.fori_loop(0, rows // SUB, body, 0)
 
 
-def weigh_last(ready, fresh, padded, smooth, centre, tail, level, weight, rows, strips):
+def weigh_last(ready, freshes, padded, smooth, centre, tail, level, weight, rows, strips, first, end):
     _, lane = iotas()
     tap = float(frame_taps()[-1])
     starts = window_starts(rows)
+    tiles = rows // SUB
+    cut = freshes[0].shape[1] // SUB
     zero = jnp.zeros((SUB, LANES), jnp.float32)
     for j in range(strips):
-        for t in range(rows // SUB):
-            inner = 0 < t < rows // SUB - 1
-            padded[j, pl.ds(TOP + t * SUB, SUB), :] = fresh[j, rows_of(t - 1), :] if inner else zero
-    for k, start in enumerate(starts):
+        for t in range(max(first - 1, 0), min(end + 1, tiles)):
+            if t == 0 or t == tiles - 1:
+                v = zero
+            elif t <= cut:
+                v = freshes[0][j, rows_of(t - 1), :]
+            else:
+                v = freshes[1][j, rows_of(t - 1 - cut), :]
+            padded[j, pl.ds(TOP + t * SUB, SUB), :] = v
+    for k in range(first, end + 1):
+        start = starts[k]
         for j in range(strips):
             v = ready[j, pl.ds(TOP + start, SUB), :]
             if 0 < k < len(starts) - 1:
                 a, b, c = (padded[j, pl.ds(TOP + start + e, SUB), :] for e in (-1, 0, 1))
                 v = v + tap * ((a + b) + (b + c))
             smooth[0, j, pl.ds(TOP + start, SUB), :] = v
-        if k == 0:
+        if k == first:
             continue
         t = k - 1
         base = t * SUB + TOP
@@ -170,17 +178,17 @@
         for j in range(strips):
             s = centre[j, pl.ds(base, SUB), :]
             top = jnp.maximum(tops[j], tail[j, at, :])
-            weight[0, at, pl.ds(j * LANES, LANES)] = weight_of(s, top, floor)
-
-
-def box_sums(weight, sel, boxes, first, frames, start):
+            weight[0, rows_of(t - first), pl.ds(j * LANES, LANES)] = weight_of(s, top, floor)
+
+
+def box_sums(weight, sel, boxes, first, frames, start, top=0, height=None):
     count, rows, columns = weight.shape
     group = 2 if count % 2 == 0 else 1
     slots2 = sel.shape[1]
     frame_base = lax.axis_index("omega") * frames
     live = boxes[0:1, :] >= 0
     f0 = jnp.where(live, boxes[0:1, :] - frame_base, -BOX_F - frames)
-    r0 = boxes[1:2, :] - lax.axis_index("row") * rows
+    r0 = boxes[1:2, :] - lax.axis_index("row") * (height or rows) - top
     row = lax.broadcasted_iota(jnp.int32, (rows, slots2), 0) - r0
     row_pick = jnp.where((row >= 0) & (row < BOX_R), 1.0, 0.0)
     row_odd = row_pick * (2 * row - (BOX_R - 1)).astype(jnp.float32)
@@ -236,7 +244,7 @@
     *pieces, sems = rest
     even = is_even()
     copies = [pltpu.make_async_copy(x.at[pl.ds(jnp.where(even, count - REACH, 0), REACH)], near, sems.at[0])]
-    *targets, filtered, last = pieces
+    *targets, filtered1, filtered2, last = pieces
     for k, (begin, end) in enumerate(PIECES):
         start = jnp.where(even, begin, count - end)
         source = x.at[pl.ds(start, end - begin), pl.ds(SUB, rows - 2 * SUB)]
@@ -250,11 +258,12 @@
     for copy in copies:
         copy.wait()
     _, lane = iotas()
-    strips = filtered.shape[0]
+    strips, part, _ = filtered1.shape
     for t in range(rows // SUB - 2):
         values = [last[0, rows_of(t), pl.ds(j * LANES, LANES)] for j in range(strips)]
+        target, to = (filtered1, t) if t < part // SUB else (filtered2, t - part // SUB)
         for j, v in enumerate(column_sums(values, lane)):
-            filtered[j, rows_of(t), :] = v
+            target[j, rows_of(to), :] = v
 
 
 def rows_kernel(*refs):
@@ -346,12 +355,21 @@
     copy.wait()
 
 
-def late_kernel(part, b, b0, z1, z2, level, sel, boxes, sums, edge, _, out, new_part, *rest, count, piece):
+def late_kernel(part, b, b0, z1, z2, level, sel, boxes, sums, edge, *rest, count, piece):
     begin, end = piece
     late = end - begin
     ahead = end == REACH - 1
-    new_edge, *tails, new_sums, first, smooth, weight, sems = rest
-    rows, columns = out.shape[1], out.shape[2]
+    if ahead:
+        new_part, *rest = rest
+    else:
+        _, out, new_part, *rest = rest
+    if ahead:
+        new_edge, tail, weight, new_sums, first, smooth, sems = rest
+        tails = (tail,)
+    else:
+        new_edge, new_sums, first, smooth, weight, sems = rest
+        tails = ()
+    rows, columns = level.shape[0], b0.shape[2]
     tiles, strips = rows // SUB, columns // LANES
     even = is_even()
     taps = frame_taps()
@@ -414,8 +432,9 @@
         *tails,
     )
     place = jnp.where(even, REACH - end, early + begin)
-    copies.append(pltpu.make_async_copy(weight, out.at[pl.ds(place, late)], sems.at[1]))
-    copies[-1].start()
+    if not ahead:
+        copies.append(pltpu.make_async_copy(weight, out.at[pl.ds(place, late)], sems.at[1]))
+        copies[-1].start()
     start = tuple(sums[i : i + 1, :] for i in range(3))
     for i, v in enumerate(box_sums(weight, sel, boxes, place, count, start)):
         new_sums[i : i + 1, :] = v
@@ -423,22 +442,46 @@
         copy.wait()
 
 
-def last_kernel(ready, fresh, level, sel, boxes, sums, centre, tail, _, out, stats, padded, smooth, weight, figures, sems):
+def last_kernel1(ready, fresh, level, sel, boxes, sums, centre, tail, weight, new_sums, padded, smooth, *, count):
+    rows = level.shape[0]
+    end = weight.shape[1] // SUB
+    weigh_last(ready, (fresh,), padded, smooth, centre, tail, level, weight, rows, sel.shape[0] // LANES, 0, end)
+    place = jnp.where(is_even(), 0, count - 1)
+    start = tuple(sums[i : i + 1, :] for i in range(3))
+    for i, v in enumerate(box_sums(weight, sel, boxes, place, count, start, 0, rows)):
+        new_sums[i : i + 1, :] = v
+
+
+def last_kernel2(
+    ready, fresh1, fresh2, level, sel, boxes, sums, centre, tail, before, upper, _, out, stats, padded, smooth, weight,
+    figures, sems
+):
     count, rows, columns = out.shape
-    weigh_last(ready, fresh, padded, smooth, centre, tail, level, weight, rows, columns // LANES)
-    place = jnp.where(is_even(), 0, count - 1)
-    copies = [pltpu.make_async_copy(weight, out.at[pl.ds(place, 1)], sems.at[1])]
+    done = upper.shape[1]
+    even = is_even()
+    place = jnp.where(even, 0, count - 1)
+    copies = [
+        pltpu.make_async_copy(before, out.at[pl.ds(jnp.where(even, 1, count - 2), 1)], sems.at[0]),
+        pltpu.make_async_copy(upper, out.at[pl.ds(place, 1), pl.ds(0, done)], sems.at[1]),
+        pltpu.make_async_copy(weight, out.at[pl.ds(place, 1), pl.ds(done, rows - done)], sems.at[2]),
+        pltpu.make_async_copy(figures, stats, sems.at[3]),
+    ]
     copies[0].start()
+    copies[1].start()
+    weigh_last(
+        ready, (fresh1, fresh2), padded, smooth, centre, tail, level, weight, rows, columns // LANES, done // SUB,
+        rows // SUB
+    )
+    copies[2].start()
     start = tuple(sums[i : i + 1, :] for i in range(3))
-    total, by_frame, by_row = box_sums(weight, sel, boxes, place, count, start)
+    total, by_frame, by_row = box_sums(weight, sel, boxes, place, count, start, done, rows)
     slots = stats.shape[1]
     cells = float(BOX_F * BOX_R * BOX_C)
     figures[0:1, :] = total[:, :slots] / cells
     figures[1:2, :] = by_frame[:, :slots] / (cells * (BOX_F - 1))
     figures[2:3, :] = by_row[:, :slots] / (cells * (BOX_R - 1))
     figures[3:4, :] = total[:, slots:] / (cells * (BOX_C - 1))
-    copies.append(pltpu.make_async_copy(figures, stats, sems.at[0]))
-    copies[1].start()
+    copies[3].start()
     for copy in copies:
         copy.wait()
 
@@ -485,6 +528,7 @@
     slots = spot_boxes.shape[1]
     early = count - REACH
     strips = columns // LANES
+    cut = (rows // SUB - 2) * 2 // 3
     ring = lax.axis_size("omega")
     partner = [(i, i ^ 1) for i in range(ring)]
     other = [(i, (i - 1) % ring if i % 2 == 0 else (i + 1) % ring) for i in range(ring)]
@@ -505,9 +549,9 @@
         pack_kernel,
         out_shape=(shape(REACH, rows, columns), shape(count, 2 * SUB, columns))
         + tuple(shape(end - begin, rows - 2 * SUB, columns) for begin, end in PIECES[:-1])
-        + (shape(strips, rows - 2 * SUB, LANES),),
+        + (shape(strips, cut * SUB, LANES), shape(strips, rows - (2 + cut) * SUB, LANES)),
         in_specs=[hbm()],
-        out_specs=(vmem(),) * (2 + len(PIECES)),
+        out_specs=(vmem(),) * (3 + len(PIECES)),
         scratch_shapes=[
             pltpu.VMEM((1, rows - 2 * SUB, columns), jnp.float32),
             pltpu.SemaphoreType.DMA((3 + len(PIECES),)),
@@ -552,48 +596,64 @@
         cost_estimate=pl.CostEstimate(flops=40 * frames.size, bytes_accessed=16 << 20, transcendentals=0),
         name="early",
     )(frames, a, z1, z2, level, sel, boxes)
-    tails = ()
     params = pltpu.CompilerParams(vmem_limit_bytes=14 << 20)
-    for (begin, end), piece in zip(PIECES[:-1], pieces[:-1]):
+    strip = shape(strips, padded, LANES)
+    for (begin, end), piece in zip(PIECES[:-1], pieces):
         late = end - begin
-        if end == REACH - 1:
-            made = late + 1
-            handed = (shape(strips, padded, LANES), shape(strips, padded, LANES), shape(strips, rows, LANES))
+        ahead = end == REACH - 1
+        made = late + 1 if ahead else late
+        edges = shape(2, strips, padded, LANES)
+        values = (part, piece, b0, far1, far2, level, sel, boxes, sums, edge)
+        if ahead:
+            handed = (strip, strip, shape(strips, rows, LANES), shape(late, rows, columns))
         else:
-            made = late
-            handed = (shape(REACH - end, strips, rows + SUB, LANES), shape(2, strips, padded, LANES))
-        weight, part, edge, *tails, sums = pl.pallas_call(
+            handed = (shape(count, rows, columns), shape(REACH - end, strips, rows + SUB, LANES), edges)
+            values = (*values, weight)
+        scratch = [pltpu.VMEM((made, strips, padded, LANES), jnp.float32)] * 2
+        if not ahead:
+            scratch = scratch + [pltpu.VMEM((late, rows, columns), jnp.float32)]
+        results = pl.pallas_call(
             functools.partial(late_kernel, count=count, piece=(begin, end)),
-            out_shape=(shape(count, rows, columns), *handed, shape(3, 2 * slots)),
-            in_specs=[vmem()] * 10 + [hbm()],
-            out_specs=(hbm(),) + (vmem(),) * (1 + len(handed)),
-            input_output_aliases={10: 0},
-            scratch_shapes=[
-                pltpu.VMEM((made, strips, padded, LANES), jnp.float32),
-                pltpu.VMEM((made, strips, padded, LANES), jnp.float32),
-                pltpu.VMEM((late, rows, columns), jnp.float32),
-                pltpu.SemaphoreType.DMA((3,)),
-            ],
+            out_shape=(*handed, shape(3, 2 * slots)),
+            in_specs=[vmem()] * 10 + ([] if ahead else [hbm()]),
+            out_specs=(vmem() if ahead else hbm(),) + (vmem(),) * len(handed),
+            input_output_aliases={} if ahead else {10: 0},
+            scratch_shapes=scratch + [pltpu.SemaphoreType.DMA((3,))],
             compiler_params=params,
             cost_estimate=pl.CostEstimate(flops=8 * late * rows * columns, bytes_accessed=4 << 20, transcendentals=0),
-        )(part, piece, b0, far1, far2, level, sel, boxes, sums, edge, weight)
+        )(*values)
+        if ahead:
+            part, edge, tail, before, sums = results
+        else:
+            weight, part, edge, sums = results
+    done = cut * SUB
+    upper, sums = pl.pallas_call(
+        functools.partial(last_kernel1, count=count),
+        out_shape=(shape(1, done, columns), shape(3, 2 * slots)),
+        in_specs=[vmem()] * 8,
+        out_specs=(vmem(), vmem()),
+        scratch_shapes=[pltpu.VMEM((strips, padded, LANES), jnp.float32), pltpu.VMEM((1, strips, padded, LANES), jnp.float32)],
+        compiler_params=params,
+        cost_estimate=pl.CostEstimate(flops=4 * rows * columns, bytes_accessed=2 << 20, transcendentals=0),
+        name="last1",
+    )(part, pieces[-2], level, sel, boxes, sums, edge, tail)
     weight, stats = pl.pallas_call(
-        last_kernel,
+        last_kernel2,
         out_shape=(shape(count, rows, columns), shape(4, slots)),
-        in_specs=[vmem()] * 8 + [hbm()],
+        in_specs=[vmem()] * 11 + [hbm()],
         out_specs=(hbm(), hbm()),
-        input_output_aliases={8: 0},
+        input_output_aliases={11: 0},
         scratch_shapes=[
             pltpu.VMEM((strips, padded, LANES), jnp.float32),
             pltpu.VMEM((1, strips, padded, LANES), jnp.float32),
-            pltpu.VMEM((1, rows, columns), jnp.float32),
+            pltpu.VMEM((1, rows - done, columns), jnp.float32),
             pltpu.VMEM((4, slots), jnp.float32),
-            pltpu.SemaphoreType.DMA((2,)),
+            pltpu.SemaphoreType.DMA((4,)),
         ],
         compiler_params=params,
-        cost_estimate=pl.CostEstimate(flops=8 * rows * columns, bytes_accessed=4 << 20, transcendentals=0),
-        name="last",
-    )(part, pieces[-1], level, sel, boxes, sums, edge, *tails, weight)
+        cost_estimate=pl.CostEstimate(flops=4 * rows * columns, bytes_accessed=2 << 20, transcendentals=0),
+        name="last2",
+    )(part, pieces[-2], pieces[-1], level, sel, boxes, sums, edge, tail, before, upper, weight)
     return weight, stats
 
 

time: 57.3 us -> 48.8 us (0.85)
  waiting for transfers between devices: 21.1 us -> 12.2 us
    ppermute x1, waiting for transfers between devices: 21.1 us -> 9.43 us  [steps(): b0 = lax.ppermute(edges, 'omega', other)]
    ppermute x1, starting transfers between devices: 0.45 us -> 3.69 us  [steps(): b0 = lax.ppermute(edges, 'omega', other)]
    ppermute x2, waiting for transfers between devices: 0.01 us -> 2.77 us  [row_exchange(): lax.ppermute(z1, both, row_pairs(ring, column, 0))]
    ppermute x3 -> x4, starting transfers between devices: 8.2 us -> 6.51 us  [steps(): pieces = [lax.ppermute(piece, 'omega', other) for piece in pieces]]
    ppermute x2, starting transfers between devices: 3.42 us -> 2.16 us  [row_exchange(): lax.ppermute(z1, both, row_pairs(ring, column, 0))]
    pallas_call x1 -> x2, Pallas kernels: 1.23 us -> 1.52 us  [the longest x1 1.11 us: steps(): pl.pallas_call(last_kernel2, out_shape=(shape(count, rows, columns), shap...]
  transfers between devices with their start and end apart: 9 -> 10, of which waited for: 1 -> 3; matrix products, arithmetic and copies ran while one was open for 0% -> 0% of each run, Pallas kernels for 33% -> 39%
where the time goes in v7:
time: 48.8 us; the launch traced here: 48.5 us
  Pallas kernels  22.5 us (46%)
  starting transfers between devices  12.9 us (26%)
  waiting for transfers between devices  12.2 us (25%)
  between operations  0.76 us (2%)
    pallas_call x1, Pallas kernels, steps(): pl.pallas_call(functools.partial(early_kernel, early=early), out_shape=(s...  9.83 us
    ppermute x1, waiting for transfers between devices, steps(): b0 = lax.ppermute(edges, 'omega', other)  9.43 us
    pallas_call x2, Pallas kernels, steps(): pl.pallas_call(functools.partial(late_kernel, count=count, piece=(begin,...  7.05 us
    ppermute x4, starting transfers between devices, steps(): pieces = [lax.ppermute(piece, 'omega', other) for piece in pieces]  6.51 us
    ppermute x1, starting transfers between devices, steps(): b0 = lax.ppermute(edges, 'omega', other)  3.69 us
    ppermute x2, waiting for transfers between devices, row_exchange(): lax.ppermute(z1, both, row_pairs(ring, column, 0))  2.77 us
    pallas_call x1, Pallas kernels, steps(): pl.pallas_call(pack_kernel, out_shape=(shape(REACH, rows, columns), shape...  2.29 us
    ppermute x2, starting transfers between devices, row_exchange(): lax.ppermute(z1, both, row_pairs(ring, column, 0))  2.16 us
  transfers between devices with their start and end apart: 10, of which 3 were waited for; matrix products, arithmetic and copies ran while one was open for 0% of the time, Pallas kernels for 39%

profile of v7, /device:TPU:0, one launch (start us, length us, event | category | flops | bytes accessed | tf_op | source)
XLA Modules:
  0.0 48.5 jit_solution(3782303465201899168)
XLA Ops:
  0.6 2.3 %pack.1 = (f32[6,64,1024]{2,1,0:T(8,128)S(1)}, f32[16,16,1024]{2,1,0:T(8,128)S(1)}, f32[4,48,1024]{2,1,0:T(8,128)S(1)}, f32[1,48,1024]{2,1,0:T(8,128)S(1)}, f32[...) custom-call(f32[16,64,1024]{2,1,0:T(8,128)} %x.5), custom_call_target="tpu_custom_call" | custom-call | tf_op jit(solution)/shard_map/pack/pallas_call | solution.py:548
  2.9 0.0 copy-start.2
  2.9 0.0 copy-start.1
  2.9 0.0 copy-start
  3.0 0.6 %collective-permute-start = (f32[6,64,1024]{2,1,0:T(8,128)S(1)}, f32[6,64,1024]{2,1,0:T(8,128)S(1)}, u32[]{:S(2)}, u32[]{:S(2)}) collective-permute-start(f32[6,64,1024]{2,1,0:T(8,128)S(1)} %get-tuple-element.27), channel_id=1, source_target_pairs={{0,4},{4,0},{8,12},{12,8},{16,20},{20,16},{24,28},{28,24},{1,5},{5... | collective-permute-start | bytes 4718600 | tf_op jit(solution)/shard_map/ppermute | solution.py:562
  3.5 1.3 %edge.1 = f32[6,16,1024]{2,1,0:T(8,128)S(1)} custom-call(f32[16,64,1024]{2,1,0:T(8,128)} %x.5), custom_call_target="tpu_custom_call" | custom-call | tf_op jit(solution)/shard_map/edge/pallas_call | solution.py:538
  4.9 3.7 %collective-permute-start.4 = (f32[6,16,1024]{2,1,0:T(8,128)S(1)}, f32[6,16,1024]{2,1,0:T(8,128)S(1)}, u32[]{:S(2)}, u32[]{:S(2)}) collective-permute-start(f32[6,16,1024]{2,1,0:T(8,128)S(1)} %edge.1), channel_id=1, source_target_pairs={{0,28},{4,8},{8,4},{12,16},{16,12},{20,24},{24,20},{28,0},{1,29},{... | collective-permute-start | bytes 1179656 | tf_op jit(solution)/shard_map/ppermute | solution.py:547
  8.5 0.1 collective-permute-start.3
  8.6 9.4 %collective-permute-done.4.refs_0_.b0 = f32[6,16,1024]{2,1,0:T(8,128)S(1)} collective-permute-done((f32[6,16,1024]{2,1,0:T(8,128)S(1)}, f32[6,16,1024]{2,1,0:T(8,128)S(1)}, u32[]{:S(2)}, u32[]{:S(2)}) %collective-permute-start.4) | collective-permute-done | bytes 393248 | tf_op jit(solution)/shard_map/ppermute | solution.py:547
  18.1 0.1 shard_map.51
  18.1 1.6 %collective-permute-start.5 = (f32[8,24,128]{2,1,0:T(8,128)S(1)}, f32[8,24,128]{2,1,0:T(8,128)S(1)}, u32[]{:S(2)}, u32[]{:S(2)}) collective-permute-start(f32[8,24,128]{2,1,0:T(8,128)S(1)} %get-tuple-element.33), channel_id=1, source_target_pairs={{0,1},{1,0},{2,3},{3,2},{4,5},{5,4},{6,7},{7,6},{8,9},{9,8},{10,11... | collective-permute-start | bytes 294920 | tf_op jit(solution)/shard_map/ppermute | solution.py:513
  19.8 0.0 collective-permute-done.refs_1_.a
  19.8 0.2 shard_map.50
  19.9 0.5 %collective-permute-start.1 = (f32[8,56,128]{2,1,0:T(8,128)S(1)}, f32[8,56,128]{2,1,0:T(8,128)S(1)}, u32[]{:S(2)}, u32[]{:S(2)}) collective-permute-start(f32[8,56,128]{2,1,0:T(8,128)S(1)} %get-tuple-element.29), channel_id=1, source_target_pairs={{0,1},{1,0},{2,3},{3,2},{4,5},{5,4},{6,7},{7,6},{8,9},{9,8},{10,11... | collective-permute-start | bytes 688136 | tf_op jit(solution)/shard_map/ppermute | solution.py:513
  20.4 0.0 collective-permute-start.2
  20.4 2.2 %collective-permute-start.8 = (f32[8,32,128]{2,1,0:T(8,128)S(1)}, f32[8,32,128]{2,1,0:T(8,128)S(1)}, u32[]{:S(2)}, u32[]{:S(2)}) collective-permute-start(f32[8,32,128]{2,1,0:T(8,128)S(1)} %get-tuple-element.43), channel_id=1, source_target_pairs={{0,28},{4,8},{8,4},{12,16},{16,12},{20,24},{24,20},{28,0},{1,29},{... | collective-permute-start | bytes 393224 | tf_op jit(solution)/shard_map/ppermute | solution.py:563
  22.7 0.5 %collective-permute-done.5.z1 = f32[8,24,128]{2,1,0:T(8,128)S(1)} collective-permute-done((f32[8,24,128]{2,1,0:T(8,128)S(1)}, f32[8,24,128]{2,1,0:T(8,128)S(1)}, u32[]{:S(2)}, u32[]{:S(2)}) %collective-permute-start.5) | collective-permute-done | bytes 98336 | tf_op jit(solution)/shard_map/ppermute | solution.py:513
  23.2 2.2 %collective-permute-start.7 = (f32[1,48,1024]{2,1,0:T(8,128)S(1)}, f32[1,48,1024]{2,1,0:T(8,128)S(1)}, u32[]{:S(2)}, u32[]{:S(2)}) collective-permute-start(f32[1,48,1024]{2,1,0:T(8,128)S(1)} %get-tuple-element.39), channel_id=1, source_target_pairs={{0,28},{4,8},{8,4},{12,16},{16,12},{20,24},{24,20},{28,0},{1,29},{... | collective-permute-start | bytes 589832 | tf_op jit(solution)/shard_map/ppermute | solution.py:563
  25.4 0.0 copy-done.2
  25.4 2.3 %collective-permute-done.1.z1 = f32[8,56,128]{2,1,0:T(8,128)S(1)} collective-permute-done((f32[8,56,128]{2,1,0:T(8,128)S(1)}, f32[8,56,128]{2,1,0:T(8,128)S(1)}, u32[]{:S(2)}, u32[]{:S(2)}) %collective-permute-start.1) | collective-permute-done | bytes 229408 | tf_op jit(solution)/shard_map/ppermute | solution.py:513
  27.7 2.0 %collective-permute-start.9 = (f32[8,16,128]{2,1,0:T(8,128)S(1)}, f32[8,16,128]{2,1,0:T(8,128)S(1)}, u32[]{:S(2)}, u32[]{:S(2)}) collective-permute-start(f32[8,16,128]{2,1,0:T(8,128)S(1)} %get-tuple-element.44), channel_id=1, source_target_pairs={{0,28},{4,8},{8,4},{12,16},{16,12},{20,24},{24,20},{28,0},{1,29},{... | collective-permute-start | bytes 196616 | tf_op jit(solution)/shard_map/ppermute | solution.py:563
  29.7 0.0 collective-permute-done.2.z2
  29.7 0.0 collective-permute-start.6
  29.7 0.0 copy-done.1
  29.7 0.1 pad_add_fusion.boxes
  29.7 0.2 table.1.sel
  30.0 0.1 broadcast_in_dim.2.level
  30.0 0.0 copy-done
  30.0 9.8 %early.1 = (f32[16,64,1024]{2,1,0:T(8,128)}, f32[6,8,72,128]{3,2,1,0:T(8,128)S(1)}, f32[2,8,80,128]{3,2,1,0:T(8,128)S(1)}, f32[3,64]{1,0:T(4,128)S(1)}) custom-call(f32[16,64,1024]{2,1,0:T(8,128)S(1)} %copy-done, f32[6,64,1024]{2,1,0:T(8,128)S(1)} %collective-permute-done.refs_1_.a, f32[8,56,128]{2,1,0:T(8,128)S(1)} %collective-permute-done.1.z1, ...), custom_call_target="tpu_custom_call" | custom-call | flops 41943040 | bytes 16777216 | tf_op jit(solution)/shard_map/early/pallas_call | solution.py:579
  39.9 0.0 collective-permute-done.6.z2
  39.9 0.0 collective-permute-done.3.b
  39.9 4.4 %shard_map.52 = (f32[16,64,1024]{2,1,0:T(8,128)}, f32[2,8,72,128]{3,2,1,0:T(8,128)S(1)}, f32[2,8,80,128]{3,2,1,0:T(8,128)S(1)}, f32[3,64]{1,0:T(4,128)S(1)}) custom-call(f32[6,8,72,128]{3,2,1,0:T(8,128)S(1)} %get-tuple-element.31.part, f32[4,48,1024]{2,1,0:T(8,128)S(1)} %collective-permute-done.3.b, ...), custom_call_target="tpu_custom_call", output_to_operand_aliasing={{0}: (10, {})} | custom-call | flops 2097152 | bytes 4194304 | tf_op jit(solution)/shard_map/pallas_call | solution.py:615
  44.3 0.0 collective-permute-done.7.b
  44.3 2.7 %shard_map.53 = (f32[8,80,128]{2,1,0:T(8,128)S(1)}, f32[8,80,128]{2,1,0:T(8,128)S(1)}, f32[8,64,128]{2,1,0:T(8,128)S(1)}, f32[1,64,1024]{2,1,0:T(8,128)S(1)}, f32[3,64]{1,0:T(4,128)S(1)}) custom-call(f32[2,8,72,128]{3,2,1,0:T(8,128)S(1)} %get-tuple-element.38.part, f32[1,48,1024]{2,1,0:T(8,128)S(1)} %collective-permute-done.7.b, ...), custom_call_target="tpu_custom_call" | custom-call | flops 524288 | bytes 4194304 | tf_op jit(solution)/shard_map/pallas_call | solution.py:615
  47.0 0.0 collective-permute-done.8.fresh.fresh1
  47.0 0.4 last1.1
  47.4 0.0 collective-permute-done.9.fresh2
  47.4 1.1 %last2.1 = (f32[16,64,1024]{2,1,0:T(8,128)}, f32[4,32]{1,0:T(4,128)}) custom-call(f32[8,80,128]{2,1,0:T(8,128)S(1)} %get-tuple-element.42.ready, f32[8,32,128]{2,1,0:T(8,128)S(1)} %collective-permute-done.8.fresh.fresh1, f32[8,16,128]{2,1,0:T(8,128)S(1)} %collective-permute-done.9.fresh2, ...), custom_call_target="tpu_custom_call", output_to_operand_aliasing={{0}: (11, {})} | custom-call | flops 262144 | bytes 2097152 | tf_op jit(solution)/shard_map/last2/pallas_call | solution.py:640
  (1 shorter events, 0.0 us)
Async XLA Ops:
  2.9 22.5 %copy-start.2 = (s32[64]{0:T(128)S(1)}, s32[64]{0:T(128)}, u32[]{:S(2)}) copy-start(s32[64]{0:T(128)} %param.4) | copy-start | bytes 772
  2.9 26.7 %copy-start.1 = (s32[3,32]{1,0:T(4,128)S(1)}, s32[3,32]{1,0:T(4,128)}, u32[]{:S(2)}) copy-start(s32[3,32]{1,0:T(4,128)} %param.5) | copy-start | bytes 1156
  2.9 27.1 %copy-start = (f32[16,64,1024]{2,1,0:T(8,128)S(1)}, f32[16,64,1024]{2,1,0:T(8,128)}, u32[]{:S(2)}) copy-start(f32[16,64,1024]{2,1,0:T(8,128)} %x.5) | copy-start | bytes 12582916
  3.0 16.8 %collective-permute-start = (f32[6,64,1024]{2,1,0:T(8,128)S(1)}, f32[6,64,1024]{2,1,0:T(8,128)S(1)}, u32[]{:S(2)}, u32[]{:S(2)}) collective-permute-start(f32[6,64,1024]{2,1,0:T(8,128)S(1)} %get-tuple-element.27), channel_id=1, source_target_pairs={{0,4},{4,0},{8,12},{12,8},{16,20},{20,16},{24,28},{28,24},{1,5},{5... | collective-permute-start | bytes 4718600 | tf_op jit(solution)/shard_map/ppermute | solution.py:562
  4.9 13.2 %collective-permute-start.4 = (f32[6,16,1024]{2,1,0:T(8,128)S(1)}, f32[6,16,1024]{2,1,0:T(8,128)S(1)}, u32[]{:S(2)}, u32[]{:S(2)}) collective-permute-start(f32[6,16,1024]{2,1,0:T(8,128)S(1)} %edge.1), channel_id=1, source_target_pairs={{0,28},{4,8},{8,4},{12,16},{16,12},{20,24},{24,20},{28,0},{1,29},{... | collective-permute-start | bytes 1179656 | tf_op jit(solution)/shard_map/ppermute | solution.py:547
  8.5 31.3 %collective-permute-start.3 = (f32[4,48,1024]{2,1,0:T(8,128)S(1)}, f32[4,48,1024]{2,1,0:T(8,128)S(1)}, u32[]{:S(2)}, u32[]{:S(2)}) collective-permute-start(f32[4,48,1024]{2,1,0:T(8,128)S(1)} %get-tuple-element.32), channel_id=1, source_target_pairs={{0,28},{4,8},{8,4},{12,16},{16,12},{20,24},{24,20},{28,0},{1,29},{... | collective-permute-start | bytes 2359304 | tf_op jit(solution)/shard_map/ppermute | solution.py:563
  18.1 5.1 %collective-permute-start.5 = (f32[8,24,128]{2,1,0:T(8,128)S(1)}, f32[8,24,128]{2,1,0:T(8,128)S(1)}, u32[]{:S(2)}, u32[]{:S(2)}) collective-permute-start(f32[8,24,128]{2,1,0:T(8,128)S(1)} %get-tuple-element.33), channel_id=1, source_target_pairs={{0,1},{1,0},{2,3},{3,2},{4,5},{5,4},{6,7},{7,6},{8,9},{9,8},{10,11... | collective-permute-start | bytes 294920 | tf_op jit(solution)/shard_map/ppermute | solution.py:513
  19.9 7.8 %collective-permute-start.1 = (f32[8,56,128]{2,1,0:T(8,128)S(1)}, f32[8,56,128]{2,1,0:T(8,128)S(1)}, u32[]{:S(2)}, u32[]{:S(2)}) collective-permute-start(f32[8,56,128]{2,1,0:T(8,128)S(1)} %get-tuple-element.29), channel_id=1, source_target_pairs={{0,1},{1,0},{2,3},{3,2},{4,5},{5,4},{6,7},{7,6},{8,9},{9,8},{10,11... | collective-permute-start | bytes 688136 | tf_op jit(solution)/shard_map/ppermute | solution.py:513
  20.4 9.2 %collective-permute-start.2 = (f32[8,56,128]{2,1,0:T(8,128)S(1)}, f32[8,56,128]{2,1,0:T(8,128)S(1)}, u32[]{:S(2)}, u32[]{:S(2)}) collective-permute-start(f32[8,56,128]{2,1,0:T(8,128)S(1)} %get-tuple-element.30), channel_id=1, source_target_pairs={{0,4},{1,2},{2,1},{3,7},{4,0},{5,6},{6,5},{7,3},{8,12},{9,10},{10,... | collective-permute-start | bytes 688136 | tf_op jit(solution)/shard_map/ppermute | solution.py:513
  20.4 26.5 %collective-permute-start.8 = (f32[8,32,128]{2,1,0:T(8,128)S(1)}, f32[8,32,128]{2,1,0:T(8,128)S(1)}, u32[]{:S(2)}, u32[]{:S(2)}) collective-permute-start(f32[8,32,128]{2,1,0:T(8,128)S(1)} %get-tuple-element.43), channel_id=1, source_target_pairs={{0,28},{4,8},{8,4},{12,16},{16,12},{20,24},{24,20},{28,0},{1,29},{... | collective-permute-start | bytes 393224 | tf_op jit(solution)/shard_map/ppermute | solution.py:563
  23.2 21.1 %collective-permute-start.7 = (f32[1,48,1024]{2,1,0:T(8,128)S(1)}, f32[1,48,1024]{2,1,0:T(8,128)S(1)}, u32[]{:S(2)}, u32[]{:S(2)}) collective-permute-start(f32[1,48,1024]{2,1,0:T(8,128)S(1)} %get-tuple-element.39), channel_id=1, source_target_pairs={{0,28},{4,8},{8,4},{12,16},{16,12},{20,24},{24,20},{28,0},{1,29},{... | collective-permute-start | bytes 589832 | tf_op jit(solution)/shard_map/ppermute | solution.py:563
  27.7 19.7 %collective-permute-start.9 = (f32[8,16,128]{2,1,0:T(8,128)S(1)}, f32[8,16,128]{2,1,0:T(8,128)S(1)}, u32[]{:S(2)}, u32[]{:S(2)}) collective-permute-start(f32[8,16,128]{2,1,0:T(8,128)S(1)} %get-tuple-element.44), channel_id=1, source_target_pairs={{0,28},{4,8},{8,4},{12,16},{16,12},{20,24},{24,20},{28,0},{1,29},{... | collective-permute-start | bytes 196616 | tf_op jit(solution)/shard_map/ppermute | solution.py:563
  29.7 10.2 %collective-permute-start.6 = (f32[8,24,128]{2,1,0:T(8,128)S(1)}, f32[8,24,128]{2,1,0:T(8,128)S(1)}, u32[]{:S(2)}, u32[]{:S(2)}) collective-permute-start(f32[8,24,128]{2,1,0:T(8,128)S(1)} %get-tuple-element.34), channel_id=1, source_target_pairs={{0,4},{1,2},{2,1},{3,7},{4,0},{5,6},{6,5},{7,3},{8,12},{9,10},{10,... | collective-permute-start | bytes 294920 | tf_op jit(solution)/shard_map/ppermute | solution.py:513

commit v8 on v7

--- a/solution.py
+++ b/solution.py
@@ -198,8 +198,9 @@
         high = w.astype(jnp.bfloat16)
         low = (w - high.astype(jnp.float32)).astype(jnp.bfloat16)
         table = sel[...]
-        folded = jnp.dot(high, table, preferred_element_type=jnp.float32)
-        folded = folded + jnp.dot(low, table, preferred_element_type=jnp.float32)
+        both = jnp.concatenate([high, low], axis=0)
+        folded = jnp.dot(both, table, preferred_element_type=jnp.float32)
+        folded = folded[: group * rows] + folded[group * rows :]
         for k in range(group):
             part = folded[k * rows : (k + 1) * rows]
             frame = first + i * group + k - f0
@@ -230,7 +231,8 @@
     count, rows, _ = x.shape
     start = jnp.where(is_even(), 0, count - REACH)
     copies = [
-        pltpu.make_async_copy(x.at[pl.ds(start, REACH), pl.ds(row, SUB)], b0.at[:, pl.ds(to, SUB)], sems.at[k])
+        pltpu.make_async_copy(x.at[start + i, pl.ds(row, SUB)], b0.at[i, pl.ds(to, SUB)], sems.at[2 * i + k])
+        for i in range(REACH)
         for k, (row, to) in enumerate(((0, 0), (rows - SUB, SUB)))
     ]
     for copy in copies:
@@ -528,7 +530,7 @@
     slots = spot_boxes.shape[1]
     early = count - REACH
     strips = columns // LANES
-    cut = (rows // SUB - 2) * 2 // 3
+    cut = rows // SUB - 3
     ring = lax.axis_size("omega")
     partner = [(i, i ^ 1) for i in range(ring)]
     other = [(i, (i - 1) % ring if i % 2 == 0 else (i + 1) % ring) for i in range(ring)]
@@ -540,7 +542,7 @@
         out_shape=shape(REACH, 2 * SUB, columns),
         in_specs=[hbm()],
         out_specs=vmem(),
-        scratch_shapes=[pltpu.SemaphoreType.DMA((2,))],
+        scratch_shapes=[pltpu.SemaphoreType.DMA((2 * REACH,))],
         compiler_params=small,
         name="edge",
     )(in_hbm)

time: 48.8 us -> 48.7 us (level)
  no operation moved by 1% of the time
where the time goes in v8:
time: 48.7 us; the launch traced here: 48.4 us
  Pallas kernels  22.4 us (46%)
  starting transfers between devices  12.9 us (26%)
  waiting for transfers between devices  12.2 us (25%)
  between operations  0.76 us (2%)
    pallas_call x1, Pallas kernels, steps(): pl.pallas_call(functools.partial(early_kernel, early=early), out_shape=(s...  9.8 us
    ppermute x1, waiting for transfers between devices, steps(): b0 = lax.ppermute(edges, 'omega', other)  9.43 us
    pallas_call x2, Pallas kernels, steps(): pl.pallas_call(functools.partial(late_kernel, count=count, piece=(begin,...  7.04 us
    ppermute x4, starting transfers between devices, steps(): pieces = [lax.ppermute(piece, 'omega', other) for piece in pieces]  6.51 us
    ppermute x1, starting transfers between devices, steps(): b0 = lax.ppermute(edges, 'omega', other)  3.69 us
    ppermute x2, waiting for transfers between devices, row_exchange(): lax.ppermute(z1, both, row_pairs(ring, column, 0))  2.77 us
    pallas_call x1, Pallas kernels, steps(): pl.pallas_call(pack_kernel, out_shape=(shape(REACH, rows, columns), shape...  2.29 us
    ppermute x2, starting transfers between devices, row_exchange(): lax.ppermute(z1, both, row_pairs(ring, column, 0))  2.16 us
  transfers between devices with their start and end apart: 10, of which 3 were waited for; matrix products, arithmetic and copies ran while one was open for 0% of the time, Pallas kernels for 39%

profile of v8, /device:TPU:0, one launch (start us, length us, event | category | flops | bytes accessed | tf_op | source)
XLA Modules:
  0.0 48.4 jit_solution(3537574068160948165)
XLA Ops:
  0.6 2.3 %pack.1 = (f32[6,64,1024]{2,1,0:T(8,128)S(1)}, f32[16,16,1024]{2,1,0:T(8,128)S(1)}, f32[4,48,1024]{2,1,0:T(8,128)S(1)}, f32[1,48,1024]{2,1,0:T(8,128)S(1)}, f32[...) custom-call(f32[16,64,1024]{2,1,0:T(8,128)} %x.5), custom_call_target="tpu_custom_call" | custom-call | tf_op jit(solution)/shard_map/pack/pallas_call | solution.py:550
  2.9 0.0 copy-start.2
  2.9 0.0 copy-start.1
  2.9 0.0 copy-start
  3.0 0.6 %collective-permute-start = (f32[6,64,1024]{2,1,0:T(8,128)S(1)}, f32[6,64,1024]{2,1,0:T(8,128)S(1)}, u32[]{:S(2)}, u32[]{:S(2)}) collective-permute-start(f32[6,64,1024]{2,1,0:T(8,128)S(1)} %get-tuple-element.27), channel_id=1, source_target_pairs={{0,4},{4,0},{8,12},{12,8},{16,20},{20,16},{24,28},{28,24},{1,5},{5... | collective-permute-start | bytes 4718600 | tf_op jit(solution)/shard_map/ppermute | solution.py:564
  3.5 1.3 %edge.1 = f32[6,16,1024]{2,1,0:T(8,128)S(1)} custom-call(f32[16,64,1024]{2,1,0:T(8,128)} %x.5), custom_call_target="tpu_custom_call" | custom-call | tf_op jit(solution)/shard_map/edge/pallas_call | solution.py:540
  4.8 3.7 %collective-permute-start.4 = (f32[6,16,1024]{2,1,0:T(8,128)S(1)}, f32[6,16,1024]{2,1,0:T(8,128)S(1)}, u32[]{:S(2)}, u32[]{:S(2)}) collective-permute-start(f32[6,16,1024]{2,1,0:T(8,128)S(1)} %edge.1), channel_id=1, source_target_pairs={{0,28},{4,8},{8,4},{12,16},{16,12},{20,24},{24,20},{28,0},{1,29},{... | collective-permute-start | bytes 1179656 | tf_op jit(solution)/shard_map/ppermute | solution.py:549
  8.5 0.1 collective-permute-start.3
  8.6 9.4 %collective-permute-done.4.refs_0_.b0 = f32[6,16,1024]{2,1,0:T(8,128)S(1)} collective-permute-done((f32[6,16,1024]{2,1,0:T(8,128)S(1)}, f32[6,16,1024]{2,1,0:T(8,128)S(1)}, u32[]{:S(2)}, u32[]{:S(2)}) %collective-permute-start.4) | collective-permute-done | bytes 393248 | tf_op jit(solution)/shard_map/ppermute | solution.py:549
  18.1 0.1 shard_map.51
  18.1 1.6 %collective-permute-start.5 = (f32[8,24,128]{2,1,0:T(8,128)S(1)}, f32[8,24,128]{2,1,0:T(8,128)S(1)}, u32[]{:S(2)}, u32[]{:S(2)}) collective-permute-start(f32[8,24,128]{2,1,0:T(8,128)S(1)} %get-tuple-element.33), channel_id=1, source_target_pairs={{0,1},{1,0},{2,3},{3,2},{4,5},{5,4},{6,7},{7,6},{8,9},{9,8},{10,11... | collective-permute-start | bytes 294920 | tf_op jit(solution)/shard_map/ppermute | solution.py:515
  19.7 0.0 collective-permute-done.refs_1_.a
  19.8 0.2 shard_map.50
  19.9 0.5 %collective-permute-start.1 = (f32[8,56,128]{2,1,0:T(8,128)S(1)}, f32[8,56,128]{2,1,0:T(8,128)S(1)}, u32[]{:S(2)}, u32[]{:S(2)}) collective-permute-start(f32[8,56,128]{2,1,0:T(8,128)S(1)} %get-tuple-element.29), channel_id=1, source_target_pairs={{0,1},{1,0},{2,3},{3,2},{4,5},{5,4},{6,7},{7,6},{8,9},{9,8},{10,11... | collective-permute-start | bytes 688136 | tf_op jit(solution)/shard_map/ppermute | solution.py:515
  20.4 0.0 collective-permute-start.2
  20.4 2.2 %collective-permute-start.8 = (f32[8,40,128]{2,1,0:T(8,128)S(1)}, f32[8,40,128]{2,1,0:T(8,128)S(1)}, u32[]{:S(2)}, u32[]{:S(2)}) collective-permute-start(f32[8,40,128]{2,1,0:T(8,128)S(1)} %get-tuple-element.43), channel_id=1, source_target_pairs={{0,28},{4,8},{8,4},{12,16},{16,12},{20,24},{24,20},{28,0},{1,29},{... | collective-permute-start | bytes 491528 | tf_op jit(solution)/shard_map/ppermute | solution.py:565
  22.7 0.5 %collective-permute-done.5.z1 = f32[8,24,128]{2,1,0:T(8,128)S(1)} collective-permute-done((f32[8,24,128]{2,1,0:T(8,128)S(1)}, f32[8,24,128]{2,1,0:T(8,128)S(1)}, u32[]{:S(2)}, u32[]{:S(2)}) %collective-permute-start.5) | collective-permute-done | bytes 98336 | tf_op jit(solution)/shard_map/ppermute | solution.py:515
  23.2 2.2 %collective-permute-start.7 = (f32[1,48,1024]{2,1,0:T(8,128)S(1)}, f32[1,48,1024]{2,1,0:T(8,128)S(1)}, u32[]{:S(2)}, u32[]{:S(2)}) collective-permute-start(f32[1,48,1024]{2,1,0:T(8,128)S(1)} %get-tuple-element.39), channel_id=1, source_target_pairs={{0,28},{4,8},{8,4},{12,16},{16,12},{20,24},{24,20},{28,0},{1,29},{... | collective-permute-start | bytes 589832 | tf_op jit(solution)/shard_map/ppermute | solution.py:565
  25.4 0.0 copy-done.2
  25.4 2.3 %collective-permute-done.1.z1 = f32[8,56,128]{2,1,0:T(8,128)S(1)} collective-permute-done((f32[8,56,128]{2,1,0:T(8,128)S(1)}, f32[8,56,128]{2,1,0:T(8,128)S(1)}, u32[]{:S(2)}, u32[]{:S(2)}) %collective-permute-start.1) | collective-permute-done | bytes 229408 | tf_op jit(solution)/shard_map/ppermute | solution.py:515
  27.7 2.0 %collective-permute-start.9 = (f32[8,8,128]{2,1,0:T(8,128)S(1)}, f32[8,8,128]{2,1,0:T(8,128)S(1)}, u32[]{:S(2)}, u32[]{:S(2)}) collective-permute-start(f32[8,8,128]{2,1,0:T(8,128)S(1)} %get-tuple-element.44), channel_id=1, source_target_pairs={{0,28},{4,8},{8,4},{12,16},{16,12},{20,24},{24,20},{28,0},{1,29},{... | collective-permute-start | bytes 98312 | tf_op jit(solution)/shard_map/ppermute | solution.py:565
  29.7 0.0 collective-permute-done.2.z2
  29.7 0.0 collective-permute-start.6
  29.7 0.0 copy-done.1
  29.7 0.1 pad_add_fusion.boxes
  29.7 0.2 table.1.sel
  30.0 0.1 broadcast_in_dim.2.level
  30.0 0.0 copy-done
  30.0 9.8 %early.1 = (f32[16,64,1024]{2,1,0:T(8,128)}, f32[6,8,72,128]{3,2,1,0:T(8,128)S(1)}, f32[2,8,80,128]{3,2,1,0:T(8,128)S(1)}, f32[3,64]{1,0:T(4,128)S(1)}) custom-call(f32[16,64,1024]{2,1,0:T(8,128)S(1)} %copy-done, f32[6,64,1024]{2,1,0:T(8,128)S(1)} %collective-permute-done.refs_1_.a, f32[8,56,128]{2,1,0:T(8,128)S(1)} %collective-permute-done.1.z1, ...), custom_call_target="tpu_custom_call" | custom-call | flops 41943040 | bytes 16777216 | tf_op jit(solution)/shard_map/early/pallas_call | solution.py:581
  39.8 0.0 collective-permute-done.6.z2
  39.9 0.0 collective-permute-done.3.b
  39.9 4.4 %shard_map.52 = (f32[16,64,1024]{2,1,0:T(8,128)}, f32[2,8,72,128]{3,2,1,0:T(8,128)S(1)}, f32[2,8,80,128]{3,2,1,0:T(8,128)S(1)}, f32[3,64]{1,0:T(4,128)S(1)}) custom-call(f32[6,8,72,128]{3,2,1,0:T(8,128)S(1)} %get-tuple-element.31.part, f32[4,48,1024]{2,1,0:T(8,128)S(1)} %collective-permute-done.3.b, ...), custom_call_target="tpu_custom_call", output_to_operand_aliasing={{0}: (10, {})} | custom-call | flops 2097152 | bytes 4194304 | tf_op jit(solution)/shard_map/pallas_call | solution.py:617
  44.3 0.0 collective-permute-done.7.b
  44.3 2.6 %shard_map.53 = (f32[8,80,128]{2,1,0:T(8,128)S(1)}, f32[8,80,128]{2,1,0:T(8,128)S(1)}, f32[8,64,128]{2,1,0:T(8,128)S(1)}, f32[1,64,1024]{2,1,0:T(8,128)S(1)}, f32[3,64]{1,0:T(4,128)S(1)}) custom-call(f32[2,8,72,128]{3,2,1,0:T(8,128)S(1)} %get-tuple-element.38.part, f32[1,48,1024]{2,1,0:T(8,128)S(1)} %collective-permute-done.7.b, ...), custom_call_target="tpu_custom_call" | custom-call | flops 524288 | bytes 4194304 | tf_op jit(solution)/shard_map/pallas_call | solution.py:617
  46.9 0.0 collective-permute-done.8.fresh.fresh1
  46.9 0.4 last1.1
  47.4 0.0 collective-permute-done.9.fresh2
  47.4 1.1 %last2.1 = (f32[16,64,1024]{2,1,0:T(8,128)}, f32[4,32]{1,0:T(4,128)}) custom-call(f32[8,80,128]{2,1,0:T(8,128)S(1)} %get-tuple-element.42.ready, f32[8,40,128]{2,1,0:T(8,128)S(1)} %collective-permute-done.8.fresh.fresh1, f32[8,8,128]{2,1,0:T(8,128)S(1)} %collective-permute-done.9.fresh2, ...), custom_call_target="tpu_custom_call", output_to_operand_aliasing={{0}: (11, {})} | custom-call | flops 262144 | bytes 2097152 | tf_op jit(solution)/shard_map/last2/pallas_call | solution.py:642
  (1 shorter events, 0.0 us)
Async XLA Ops:
  2.9 22.5 %copy-start.2 = (s32[64]{0:T(128)S(1)}, s32[64]{0:T(128)}, u32[]{:S(2)}) copy-start(s32[64]{0:T(128)} %param.4) | copy-start | bytes 772
  2.9 26.7 %copy-start.1 = (s32[3,32]{1,0:T(4,128)S(1)}, s32[3,32]{1,0:T(4,128)}, u32[]{:S(2)}) copy-start(s32[3,32]{1,0:T(4,128)} %param.5) | copy-start | bytes 1156
  2.9 27.1 %copy-start = (f32[16,64,1024]{2,1,0:T(8,128)S(1)}, f32[16,64,1024]{2,1,0:T(8,128)}, u32[]{:S(2)}) copy-start(f32[16,64,1024]{2,1,0:T(8,128)} %x.5) | copy-start | bytes 12582916
  3.0 16.8 %collective-permute-start = (f32[6,64,1024]{2,1,0:T(8,128)S(1)}, f32[6,64,1024]{2,1,0:T(8,128)S(1)}, u32[]{:S(2)}, u32[]{:S(2)}) collective-permute-start(f32[6,64,1024]{2,1,0:T(8,128)S(1)} %get-tuple-element.27), channel_id=1, source_target_pairs={{0,4},{4,0},{8,12},{12,8},{16,20},{20,16},{24,28},{28,24},{1,5},{5... | collective-permute-start | bytes 4718600 | tf_op jit(solution)/shard_map/ppermute | solution.py:564
  4.8 13.2 %collective-permute-start.4 = (f32[6,16,1024]{2,1,0:T(8,128)S(1)}, f32[6,16,1024]{2,1,0:T(8,128)S(1)}, u32[]{:S(2)}, u32[]{:S(2)}) collective-permute-start(f32[6,16,1024]{2,1,0:T(8,128)S(1)} %edge.1), channel_id=1, source_target_pairs={{0,28},{4,8},{8,4},{12,16},{16,12},{20,24},{24,20},{28,0},{1,29},{... | collective-permute-start | bytes 1179656 | tf_op jit(solution)/shard_map/ppermute | solution.py:549
  8.5 31.3 %collective-permute-start.3 = (f32[4,48,1024]{2,1,0:T(8,128)S(1)}, f32[4,48,1024]{2,1,0:T(8,128)S(1)}, u32[]{:S(2)}, u32[]{:S(2)}) collective-permute-start(f32[4,48,1024]{2,1,0:T(8,128)S(1)} %get-tuple-element.32), channel_id=1, source_target_pairs={{0,28},{4,8},{8,4},{12,16},{16,12},{20,24},{24,20},{28,0},{1,29},{... | collective-permute-start | bytes 2359304 | tf_op jit(solution)/shard_map/ppermute | solution.py:565
  18.1 5.1 %collective-permute-start.5 = (f32[8,24,128]{2,1,0:T(8,128)S(1)}, f32[8,24,128]{2,1,0:T(8,128)S(1)}, u32[]{:S(2)}, u32[]{:S(2)}) collective-permute-start(f32[8,24,128]{2,1,0:T(8,128)S(1)} %get-tuple-element.33), channel_id=1, source_target_pairs={{0,1},{1,0},{2,3},{3,2},{4,5},{5,4},{6,7},{7,6},{8,9},{9,8},{10,11... | collective-permute-start | bytes 294920 | tf_op jit(solution)/shard_map/ppermute | solution.py:515
  19.9 7.8 %collective-permute-start.1 = (f32[8,56,128]{2,1,0:T(8,128)S(1)}, f32[8,56,128]{2,1,0:T(8,128)S(1)}, u32[]{:S(2)}, u32[]{:S(2)}) collective-permute-start(f32[8,56,128]{2,1,0:T(8,128)S(1)} %get-tuple-element.29), channel_id=1, source_target_pairs={{0,1},{1,0},{2,3},{3,2},{4,5},{5,4},{6,7},{7,6},{8,9},{9,8},{10,11... | collective-permute-start | bytes 688136 | tf_op jit(solution)/shard_map/ppermute | solution.py:515
  20.4 9.2 %collective-permute-start.2 = (f32[8,56,128]{2,1,0:T(8,128)S(1)}, f32[8,56,128]{2,1,0:T(8,128)S(1)}, u32[]{:S(2)}, u32[]{:S(2)}) collective-permute-start(f32[8,56,128]{2,1,0:T(8,128)S(1)} %get-tuple-element.30), channel_id=1, source_target_pairs={{0,4},{1,2},{2,1},{3,7},{4,0},{5,6},{6,5},{7,3},{8,12},{9,10},{10,... | collective-permute-start | bytes 688136 | tf_op jit(solution)/shard_map/ppermute | solution.py:515
  20.4 26.5 %collective-permute-start.8 = (f32[8,40,128]{2,1,0:T(8,128)S(1)}, f32[8,40,128]{2,1,0:T(8,128)S(1)}, u32[]{:S(2)}, u32[]{:S(2)}) collective-permute-start(f32[8,40,128]{2,1,0:T(8,128)S(1)} %get-tuple-element.43), channel_id=1, source_target_pairs={{0,28},{4,8},{8,4},{12,16},{16,12},{20,24},{24,20},{28,0},{1,29},{... | collective-permute-start | bytes 491528 | tf_op jit(solution)/shard_map/ppermute | solution.py:565
  23.2 21.1 %collective-permute-start.7 = (f32[1,48,1024]{2,1,0:T(8,128)S(1)}, f32[1,48,1024]{2,1,0:T(8,128)S(1)}, u32[]{:S(2)}, u32[]{:S(2)}) collective-permute-start(f32[1,48,1024]{2,1,0:T(8,128)S(1)} %get-tuple-element.39), channel_id=1, source_target_pairs={{0,28},{4,8},{8,4},{12,16},{16,12},{20,24},{24,20},{28,0},{1,29},{... | collective-permute-start | bytes 589832 | tf_op jit(solution)/shard_map/ppermute | solution.py:565
  27.7 19.7 %collective-permute-start.9 = (f32[8,8,128]{2,1,0:T(8,128)S(1)}, f32[8,8,128]{2,1,0:T(8,128)S(1)}, u32[]{:S(2)}, u32[]{:S(2)}) collective-permute-start(f32[8,8,128]{2,1,0:T(8,128)S(1)} %get-tuple-element.44), channel_id=1, source_target_pairs={{0,28},{4,8},{8,4},{12,16},{16,12},{20,24},{24,20},{28,0},{1,29},{... | collective-permute-start | bytes 98312 | tf_op jit(solution)/shard_map/ppermute | solution.py:565
  29.7 10.2 %collective-permute-start.6 = (f32[8,24,128]{2,1,0:T(8,128)S(1)}, f32[8,24,128]{2,1,0:T(8,128)S(1)}, u32[]{:S(2)}, u32[]{:S(2)}) collective-permute-start(f32[8,24,128]{2,1,0:T(8,128)S(1)} %get-tuple-element.34), channel_id=1, source_target_pairs={{0,4},{1,2},{2,1},{3,7},{4,0},{5,6},{6,5},{7,3},{8,12},{9,10},{10,... | collective-permute-start | bytes 294920 | tf_op jit(solution)/shard_map/ppermute | solution.py:515
